TPU v7x, 32 devices: a whole 2x2x4 slice. The times are simulated.
32 devices in a mesh: groups: 1, rows: 16 (over z, y, core), cols: 2 (over x), sub: 1.
Axes of the slice: x: 2, y: 2, z: 4, core: 2. Of those that a mesh axis runs over, the one named last changes fastest.
Arguments:
- activations: bfloat16 [4096, 5376], P(('groups', 'rows'), ('cols', 'sub')), may hold values from -40 to 40
- positions: int32 [4096], P('groups'), may hold values from 0 to 6143, as said below
- query_weight: bfloat16 [5376, 4096], P('rows', ('cols', 'sub')), may hold values from -0.078125 to 0.078125
- key_weight: bfloat16 [5376, 2048], P('rows', ('cols', 'sub')), may hold values from -0.078125 to 0.078125
- value_weight: bfloat16 [5376, 2048], P('rows', ('cols', 'sub')), may hold values from -0.078125 to 0.078125
- output_weight: bfloat16 [4096, 5376], P(('cols', 'sub'), 'rows'), may hold values from -0.09375 to 0.09375
- input_gain: float32 [5376], replicated, may hold values from 0.1 to 1.9
- query_gain: float32 [128], replicated, may hold values from 0.1 to 1.9
- key_gain: float32 [128], replicated, may hold values from 0.1 to 1.9
Outputs:
- attended: bfloat16 [4096, 5376], P(('groups', 'rows'), ('cols', 'sub'))
Inputs may be any that keep to these rules, and one draw needn't show every extreme that they name: `positions`: position of each token in its document: it rises by one from token to token, or falls to 0 where a new document begins; the first document may begin at any position.
All inputs are finite; a program needn't handle non-finite values.
Results may differ from a plain program's by a relative error of at most 0.0065.
Values may be sent and summed in bfloat16 or wider, within the bound.
No kernel may reach another device: no remote copies, remote signals or barrier semaphores. Data moves between devices by JAX's collectives and lax.ppermute only.
A program may use at most 128 MiB of HBM per device.

v0:
```python
import math

import jax
import jax.numpy as jnp
from jax import lax
from jax.sharding import PartitionSpec as P

HD = 128
WINDOW = 1024
QUERY_SCALAR = 168


def passed_along(value, axis, by):
    peers = lax.axis_size(axis)
    pairs = [(i, i + by) for i in range(peers) if 0 <= i + by < peers]
    return lax.ppermute(value, axis, pairs)


def head_norm(tensor, gain_vector):
    return (
        tensor * lax.rsqrt(jnp.mean(tensor * tensor, axis=-1, keepdims=True) + 1e-06) * gain_vector
    )


def rotate(tensor, token_positions):
    half_width = tensor.shape[-1] // 2
    frequency = 10000.0 ** (-(jnp.arange(half_width, dtype=jnp.float32) * 2.0 / tensor.shape[-1]))
    angles = token_positions.astype(jnp.float32)[:, None] * frequency[None, :]
    cosine = jnp.cos(angles)[:, None, :]
    sine_part = jnp.sin(angles)[:, None, :]
    first_half = tensor[..., :half_width]
    second_half = tensor[..., half_width:]
    return jnp.concatenate(
        [
            first_half * cosine - second_half * sine_part,
            second_half * cosine + first_half * sine_part,
        ],
        axis=-1,
    )


def attend(queries, key_rows, value_rows, query_index, key_index, query_pos, key_pos):
    row_count = queries.shape[0]
    key_count = key_rows.shape[0]
    kv_heads = key_rows.shape[1] // HD
    group_size = queries.shape[1] // key_rows.shape[1]
    query_four = queries.reshape(row_count, kv_heads, group_size, HD)
    key_three = key_rows.reshape(key_count, kv_heads, HD)
    value_three = value_rows.reshape(key_count, kv_heads, HD)
    score_scale = 1.0 / math.sqrt(QUERY_SCALAR)
    scores = (
        jnp.einsum("qgrd,kgd->grqk", query_four, key_three, preferred_element_type=jnp.float32)
        * score_scale
    )
    distance = query_index[:, None] - key_index[None, :]
    visible = (
        (key_index[None, :] >= 0)
        & (distance >= 0)
        & (distance < WINDOW)
        & (query_pos[:, None] - key_pos[None, :] == distance)
    )
    weights = jnp.where(visible[None, None], jnp.exp(scores), 0.0)
    totals = jnp.sum(weights, axis=-1)
    rounded = weights.astype(jnp.bfloat16)
    mixed_heads = jnp.einsum(
        "grqk,kgd->qgrd", rounded, value_three, preferred_element_type=jnp.float32
    )
    mixed_heads = mixed_heads / jnp.transpose(totals, (2, 0, 1))[..., None]
    return mixed_heads.astype(jnp.bfloat16).reshape(row_count, kv_heads * group_size * HD)


def reach_back(key_rows, value_rows, reach_rows):
    pieces = []
    carried = (key_rows, value_rows)
    for distance in range(reach_rows):
        carried = passed_along((carried[0], carried[1]), "rows", 1)
        pieces.append(carried)
    ordered = pieces[::-1] + [(key_rows, value_rows)]
    all_keys = jnp.concatenate([member[0] for member in ordered], axis=0)
    all_values = jnp.concatenate([member[1] for member in ordered], axis=0)
    return (all_keys, all_values)


def body(
    activations,
    positions,
    query_weight,
    key_weight,
    value_weight,
    output_weight,
    input_gain,
    query_gain,
    key_gain,
):
    rows_here = activations.shape[0]
    row_panel = lax.all_gather(activations, ("cols", "sub"), axis=1, tiled=True)
    panel_wide = row_panel.astype(jnp.float32)
    inverse = lax.rsqrt(jnp.mean(panel_wide * panel_wide, axis=-1, keepdims=True) + 1e-06)
    normed = (panel_wide * inverse * input_gain).astype(jnp.bfloat16)
    row_index = lax.axis_index("rows")
    own_positions = lax.dynamic_slice_in_dim(positions, row_index * rows_here, rows_here, 0)
    reach_rows = min(-(-WINDOW // rows_here), lax.axis_size("rows") - 1)

    def add_rows(weight_piece):
        return jnp.dot(normed, weight_piece, preferred_element_type=jnp.float32)

    weight_piece = (
        lax.all_gather(query_weight, "rows", axis=0, tiled=True),
        lax.all_gather(key_weight, "rows", axis=0, tiled=True),
        lax.all_gather(value_weight, "rows", axis=0, tiled=True),
    )
    query_raw = add_rows(weight_piece[0])
    key_raw = add_rows(weight_piece[1])
    value_raw = add_rows(weight_piece[2])
    key_rows = rotate(head_norm(key_raw.reshape(rows_here, -1, HD), key_gain), own_positions)
    key_rows, value_rows = (
        key_rows.astype(jnp.bfloat16).reshape(rows_here, -1),
        value_raw.astype(jnp.bfloat16),
    )
    all_keys, all_values = reach_back(key_rows, value_rows, reach_rows)
    queries = rotate(head_norm(query_raw.reshape(rows_here, -1, HD), query_gain), own_positions)
    queries = queries.astype(jnp.bfloat16).reshape(rows_here, -1)
    key_count = all_keys.shape[0]
    query_index = row_index * rows_here + jnp.arange(rows_here, dtype=jnp.int32)
    key_index = (row_index - reach_rows) * rows_here + jnp.arange(key_count, dtype=jnp.int32)
    padded = jnp.concatenate([jnp.zeros((reach_rows * rows_here,), jnp.int32), positions], axis=0)
    key_positions = lax.dynamic_slice_in_dim(padded, row_index * rows_here, key_count, 0)
    context = attend(
        queries, all_keys, all_values, query_index, key_index, own_positions, key_positions
    )
    partial_terms = jnp.dot(
        context,
        lax.all_gather(output_weight, "rows", axis=1, tiled=True),
        preferred_element_type=jnp.float32,
    )
    summed = lax.psum_scatter(
        partial_terms.astype(jnp.bfloat16), ("cols", "sub"), scatter_dimension=1, tiled=True
    ).astype(jnp.float32)
    return (activations.astype(jnp.float32) + summed).astype(jnp.bfloat16)


def solution(mesh):
    placed = (
        P(("groups", "rows"), ("cols", "sub")),
        P("groups"),
        P("rows", ("cols", "sub")),
        P("rows", ("cols", "sub")),
        P("rows", ("cols", "sub")),
        P(("cols", "sub"), "rows"),
        P(),
        P(),
        P(),
    )
    return jax.shard_map(
        body,
        mesh=mesh,
        in_specs=placed,
        out_specs=P(("groups", "rows"), ("cols", "sub")),
        check_vma=False,
    )
```

profile of v0, /device:TPU:0, one launch (start us, length us, event | category | flops | bytes accessed | tf_op | source)
XLA Modules:
  0.0 572.9 jit_solution(11946632752547401691)
XLA Ops:
  6.5 0.7 all-gather.6.cloned.1.call-update
  7.3 0.7 all-gather.8.cloned.1.call-update
  8.1 0.7 all-gather.10.cloned.1.call-update
  8.8 0.5 all-gather.12.cloned.1.call-update
  9.4 0.5 all-gather.14.cloned.1.call-update
  10.1 0.5 multiply_cosine_fusion
  10.6 41.5 %all-gather.6.cloned.1.call-done = bf16[256,5376]{1,0:T(8,128)(2,1)} async-done(((bf16[256,2688]{1,0:T(8,128)(2,1)}), bf16[256,5376]{1,0:T(8,128)(2,1)}) %all-gather.6.cloned.1.call-update) | async-done | bytes 2752528 | tf_op jit(solution)/shard_map/all_gather | solution.py:96
  52.1 2.6 fusion.2
  54.7 90.5 %all-gather.8.cloned.1.call-done = bf16[5376,1024]{1,0:T(8,128)(2,1)} async-done(((bf16[336,1024]{1,0:T(8,128)(2,1)}), bf16[5376,1024]{1,0:T(8,128)(2,1)}) %all-gather.8.cloned.1.call-update) | async-done | bytes 11010064 | tf_op jit(solution)/shard_map/all_gather | solution.py:110
  145.2 8.0 %convolution_convert_fusion.1 = bf16[256,1024]{1,0:T(8,128)(2,1)} fusion(bf16[5376,1024]{1,0:T(8,128)(2,1)} %all-gather.8.cloned.1.call-done, bf16[256,5376]{1,0:T(8,128)(2,1)S(1)} %copy-done.1, f32[5376]{0:T(1024)S(1)} %copy-done.8, f32[256]{0:T(256)S(1)} %add_rsqrt_fusion.2), kind=kOutput, calls=%fused_computation.24 | convolution fusion | flops 2824339456 | bytes 14309376 | tf_op jit(solution)/shard_map/dot_general | solution.py:105
  153.2 2.2 collective-permute-start
  155.4 86.7 %all-gather.10.cloned.1.call-done = bf16[5376,1024]{1,0:T(8,128)(2,1)} async-done(((bf16[336,1024]{1,0:T(8,128)(2,1)}), bf16[5376,1024]{1,0:T(8,128)(2,1)}) %all-gather.10.cloned.1.call-update) | async-done | bytes 11010064 | tf_op jit(solution)/shard_map/all_gather | solution.py:109
  242.0 6.7 %fusion.18 = f32[256,1024]{1,0:T(8,128)S(1)} fusion(bf16[5376,1024]{1,0:T(8,128)(2,1)} %all-gather.10.cloned.1.call-done, bf16[256,5376]{1,0:T(8,128)(2,1)} %all-gather.6.cloned.1.call-done, f32[5376]{0:T(1024)S(1)} %copy-done.8, f32[256]{0:T(256)S(1)} %add_rsqrt_fusion.2), kind=kOutput, calls=%fused_computation.55 | convolution fusion | flops 2824077312 | bytes 14833664 | tf_op jit(solution)/shard_map/dot_general | solution.py:105
  249.7 0.4 multiply_subtract_fusion
  250.7 2.2 collective-permute-start.4
  252.9 2.3 collective-permute-start.1
  255.3 17.4 %collective-permute-start.5 = (bf16[256,1024]{0,1:T(8,128)(2,1)S(1)}, bf16[256,1024]{0,1:T(8,128)(2,1)S(1)}, u32[]{:S(2)}, u32[]{:S(2)}) collective-permute-start(bf16[256,1024]{0,1:T(8,128)(2,1)S(1)} %collective-permute-done.4), channel_id=1, source_target_pairs={{0,2},{2,4},{4,6},{6,8},{8,10},{10,12},{12,14},{14,16},{16,18},{18... | collective-permute-start | bytes 1572872 | tf_op jit(solution)/shard_map/ppermute | solution.py:16
  272.7 17.6 %collective-permute-start.2 = (bf16[256,1024]{1,0:T(8,128)(2,1)S(1)}, bf16[256,1024]{1,0:T(8,128)(2,1)}, u32[]{:S(2)}, u32[]{:S(2)}) collective-permute-start(bf16[256,1024]{1,0:T(8,128)(2,1)S(1)} %collective-permute-done.1), channel_id=1, source_target_pairs={{0,2},{2,4},{4,6},{6,8},{8,10},{10,12},{12,14},{14,16},{16,18},{18... | collective-permute-start | bytes 1572872 | tf_op jit(solution)/shard_map/ppermute | solution.py:16
  290.4 16.8 %collective-permute-start.6 = (bf16[256,1024]{0,1:T(8,128)(2,1)S(1)}, bf16[256,1024]{0,1:T(8,128)(2,1)}, u32[]{:S(2)}, u32[]{:S(2)}) collective-permute-start(bf16[256,1024]{0,1:T(8,128)(2,1)S(1)} %collective-permute-done.5), channel_id=1, source_target_pairs={{0,2},{2,4},{4,6},{6,8},{8,10},{10,12},{12,14},{14,16},{16,18},{18... | collective-permute-start | bytes 1572872 | tf_op jit(solution)/shard_map/ppermute | solution.py:16
  307.2 16.8 %collective-permute-start.3 = (bf16[256,1024]{1,0:T(8,128)(2,1)}, bf16[256,1024]{1,0:T(8,128)(2,1)}, u32[]{:S(2)}, u32[]{:S(2)}) collective-permute-start(bf16[256,1024]{1,0:T(8,128)(2,1)} %collective-permute-done.2), channel_id=1, source_target_pairs={{0,2},{2,4},{4,6},{6,8},{8,10},{10,12},{12,14},{14,16},{16,18},{18... | collective-permute-start | bytes 1572872 | tf_op jit(solution)/shard_map/ppermute | solution.py:16
  324.1 2.0 fusion.9
  326.7 1.3 copy.52
  328.0 14.2 %collective-permute-start.7 = (bf16[256,1024]{0,1:T(8,128)(2,1)}, bf16[256,1024]{0,1:T(8,128)(2,1)}, u32[]{:S(2)}, u32[]{:S(2)}) collective-permute-start(bf16[256,1024]{0,1:T(8,128)(2,1)} %collective-permute-done.6), channel_id=1, source_target_pairs={{0,2},{2,4},{4,6},{6,8},{8,10},{10,12},{12,14},{14,16},{16,18},{18... | collective-permute-start | bytes 1572872 | tf_op jit(solution)/shard_map/ppermute | solution.py:16
  342.2 1.9 constant_dynamic-update-slice_fusion.4
  344.1 1.9 constant_dynamic-update-slice_fusion.3
  346.0 1.9 constant_dynamic-update-slice_fusion.2
  347.9 0.8 constant_dynamic-update-slice_fusion.1
  348.7 1.9 constant_dynamic-update-slice_fusion
  350.6 4.4 copy.64
  355.0 1.3 copy.51
  356.3 0.9 constant_dynamic-update-slice_fusion.9
  357.2 0.9 constant_dynamic-update-slice_fusion.8
  358.1 0.9 constant_dynamic-update-slice_fusion.7
  359.0 0.9 constant_dynamic-update-slice_fusion.6
  359.9 1.1 constant_dynamic-update-slice_fusion.5
  361.0 29.8 %all-gather.12.cloned.1.call-done = bf16[5376,2048]{1,0:T(8,128)(2,1)} async-done(((bf16[336,2048]{1,0:T(8,128)(2,1)}), bf16[5376,2048]{1,0:T(8,128)(2,1)}) %all-gather.12.cloned.1.call-update) | async-done | bytes 22020112 | tf_op jit(solution)/shard_map/all_gather | solution.py:108
  390.8 11.1 %convolution_bitcast_fusion = f32[32,8,16,128]{3,1,2,0:T(8,128)S(1)} fusion(bf16[5376,2048]{1,0:T(8,128)(2,1)} %all-gather.12.cloned.1.call-done, bf16[256,5376]{1,0:T(8,128)(2,1)} %all-gather.6.cloned.1.call-done, f32[5376]{0:T(1024)S(1)} %copy-done.8, f32[256]{0:T(256)S(1)} %add_rsqrt_fusion.2), kind=kOutput, calls=%fused_computation.20 | convolution fusion | flops 5642649600 | bytes 26892288 | tf_op jit(solution)/shard_map/dot_general | solution.py:105
  402.4 0.6 multiply_reduce_fusion
  403.2 0.9 multiply_multiply_fusion
  404.0 0.8 subtract_convert_fusion
  405.8 7.6 %fusion.22 = (f32[8,2,256]{2,1,0:T(2,128)S(1)}, bf16[8,2,256,1280]{2,3,1,0:T(8,128)(2,1)S(1)}) fusion(bf16[256,8,2,64]{3,0,2,1:T(8,128)(2,1)S(1)} %bitcast.55, bf16[256,8,2,64]{3,0,2,1:T(8,128)(2,1)S(1)} %bitcast.56, bf16[1280,8,128]{2,0,1:T(8,128)(2,1)} %constant_dynamic-update-slice_fusion.5, pred[256,1280]{0,1:T(8,128)(4,1)S(1)} %copy-done.4), kind=kOutput, calls=%fused_computation.57 | convolution fusion | flops 1365241856 | bytes 14499840 | tf_op jit(solution)/shard_map/qgrd,kgd->grqk/dot_general | solution.py:52
  413.4 2.5 fusion.6
  415.9 94.0 %all-gather.14.cloned.1.call-done = bf16[2048,5376]{0,1:T(8,128)(2,1)} async-done(((bf16[2048,336]{0,1:T(8,128)(2,1)}), bf16[2048,5376]{0,1:T(8,128)(2,1)}) %all-gather.14.cloned.1.call-update) | async-done | bytes 22020112 | tf_op jit(solution)/shard_map/all_gather | solution.py:133
  510.0 10.8 %convolution_convert_fusion = bf16[256,5376]{1,0:T(8,128)(2,1)S(1)} fusion(bf16[256,2048]{0,1:T(8,128)(2,1)} %bitcast.60, bf16[2048,5376]{0,1:T(8,128)(2,1)} %all-gather.14.cloned.1.call-done), kind=kOutput, calls=%fused_computation.3 | convolution fusion | flops 5638520832 | bytes 25821184 | tf_op jit(solution)/shard_map/dot_general | solution.py:131
  520.8 2.8 copy.65
  523.6 39.2 %reduce-scatter.4.cloned.1.call-done = bf16[2688,256]{1,0:T(8,128)(2,1)} async-done(((bf16[5376,256]{1,0:T(8,128)(2,1)}), bf16[2688,256]{1,0:T(8,128)(2,1)}) %reduce-scatter.4.cloned.1.call-update) | async-done | bytes 1376272
  562.8 1.8 copy.66
  564.6 1.4 add_convert_fusion
  (53 shorter events, 4.0 us)
Async XLA Ops:
  6.5 3.5 copy-start.5
  6.5 45.6 %all-gather.6.cloned.1.call-start = ((), (), s32[]{:S(2)}) async-start(), calls=%async_computation.1 | async-start | bytes 4128768 | tf_op jit(solution)/shard_map/all_gather | solution.py:96
  7.3 137.9 %all-gather.8.cloned.1.call-start = ((), (), s32[]{:S(2)}) async-start(), calls=%async_computation.2 | async-start | bytes 11698176 | tf_op jit(solution)/shard_map/all_gather | solution.py:110
  8.0 234.0 %all-gather.10.cloned.1.call-start = ((), (), s32[]{:S(2)}) async-start(), calls=%async_computation.3 | async-start | bytes 11698176 | tf_op jit(solution)/shard_map/all_gather | solution.py:109
  8.7 136.5 %copy-start.8 = (f32[5376]{0:T(1024)S(1)}, f32[5376]{0:T(1024)}, u32[]{:S(2)}) copy-start(f32[5376]{0:T(1024)} %param.15) | copy-start | bytes 64516
  8.8 382.1 %all-gather.12.cloned.1.call-start = ((), (), s32[]{:S(2)}) async-start(), calls=%async_computation.4 | async-start | bytes 23396352 | tf_op jit(solution)/shard_map/all_gather | solution.py:108
  9.3 500.6 %all-gather.14.cloned.1.call-start = ((), (), s32[]{:S(2)}) async-start(), calls=%async_computation.5 | async-start | bytes 23396352 | tf_op jit(solution)/shard_map/all_gather | solution.py:133
  9.9 552.9 %reduce-scatter.4.cloned.1.call-start = ((), (), s32[]{:S(2)}) async-start(), calls=%async_computation.6 | async-start | bytes 4128768
  52.1 93.1 %copy-start.1 = (bf16[256,5376]{1,0:T(8,128)(2,1)S(1)}, bf16[256,5376]{1,0:T(8,128)(2,1)}, u32[]{:S(2)}) copy-start(bf16[256,5376]{1,0:T(8,128)(2,1)} %all-gather.6.cloned.1.call-done) | copy-start | bytes 8257540
  153.2 99.7 %collective-permute-start = (bf16[256,1024]{1,0:T(8,128)(2,1)}, bf16[256,1024]{1,0:T(8,128)(2,1)S(1)}, u32[]{:S(2)}, u32[]{:S(2)}) collective-permute-start(bf16[256,1024]{1,0:T(8,128)(2,1)} %convolution_convert_fusion.1), channel_id=1, source_target_pairs={{0,2},{2,4},{4,6},{6,8},{8,10},{10,12},{12,14},{14,16},{16,18},{18... | collective-permute-start | bytes 1572872 | tf_op jit(solution)/shard_map/ppermute | solution.py:16
  248.7 0.7 copy-start.6
  250.7 4.6 collective-permute-start.4
  252.9 19.8 %collective-permute-start.1 = (bf16[256,1024]{1,0:T(8,128)(2,1)S(1)}, bf16[256,1024]{1,0:T(8,128)(2,1)S(1)}, u32[]{:S(2)}, u32[]{:S(2)}) collective-permute-start(bf16[256,1024]{1,0:T(8,128)(2,1)S(1)} %collective-permute-done), channel_id=1, source_target_pairs={{0,2},{2,4},{4,6},{6,8},{8,10},{10,12},{12,14},{14,16},{16,18},{18... | collective-permute-start | bytes 1572872 | tf_op jit(solution)/shard_map/ppermute | solution.py:16
  255.3 35.1 %collective-permute-start.5 = (bf16[256,1024]{0,1:T(8,128)(2,1)S(1)}, bf16[256,1024]{0,1:T(8,128)(2,1)S(1)}, u32[]{:S(2)}, u32[]{:S(2)}) collective-permute-start(bf16[256,1024]{0,1:T(8,128)(2,1)S(1)} %collective-permute-done.4), channel_id=1, source_target_pairs={{0,2},{2,4},{4,6},{6,8},{8,10},{10,12},{12,14},{14,16},{16,18},{18... | collective-permute-start | bytes 1572872 | tf_op jit(solution)/shard_map/ppermute | solution.py:16
  272.7 53.4 %copy-start.3 = (bf16[256,1024]{1,0:T(8,128)(2,1)}, bf16[256,1024]{1,0:T(8,128)(2,1)S(1)}, u32[]{:S(2)}) copy-start(bf16[256,1024]{1,0:T(8,128)(2,1)S(1)} %collective-permute-done.1) | copy-start | bytes 1572868
  272.7 34.5 %collective-permute-start.2 = (bf16[256,1024]{1,0:T(8,128)(2,1)S(1)}, bf16[256,1024]{1,0:T(8,128)(2,1)}, u32[]{:S(2)}, u32[]{:S(2)}) collective-permute-start(bf16[256,1024]{1,0:T(8,128)(2,1)S(1)} %collective-permute-done.1), channel_id=1, source_target_pairs={{0,2},{2,4},{4,6},{6,8},{8,10},{10,12},{12,14},{14,16},{16,18},{18... | collective-permute-start | bytes 1572872 | tf_op jit(solution)/shard_map/ppermute | solution.py:16
  290.4 36.2 %collective-permute-start.6 = (bf16[256,1024]{0,1:T(8,128)(2,1)S(1)}, bf16[256,1024]{0,1:T(8,128)(2,1)}, u32[]{:S(2)}, u32[]{:S(2)}) collective-permute-start(bf16[256,1024]{0,1:T(8,128)(2,1)S(1)} %collective-permute-done.5), channel_id=1, source_target_pairs={{0,2},{2,4},{4,6},{6,8},{8,10},{10,12},{12,14},{14,16},{16,18},{18... | collective-permute-start | bytes 1572872 | tf_op jit(solution)/shard_map/ppermute | solution.py:16
  307.2 35.0 %collective-permute-start.3 = (bf16[256,1024]{1,0:T(8,128)(2,1)}, bf16[256,1024]{1,0:T(8,128)(2,1)}, u32[]{:S(2)}, u32[]{:S(2)}) collective-permute-start(bf16[256,1024]{1,0:T(8,128)(2,1)} %collective-permute-done.2), channel_id=1, source_target_pairs={{0,2},{2,4},{4,6},{6,8},{8,10},{10,12},{12,14},{14,16},{16,18},{18... | collective-permute-start | bytes 1572872 | tf_op jit(solution)/shard_map/ppermute | solution.py:16
  328.0 27.0 %collective-permute-start.7 = (bf16[256,1024]{0,1:T(8,128)(2,1)}, bf16[256,1024]{0,1:T(8,128)(2,1)}, u32[]{:S(2)}, u32[]{:S(2)}) collective-permute-start(bf16[256,1024]{0,1:T(8,128)(2,1)} %collective-permute-done.6), channel_id=1, source_target_pairs={{0,2},{2,4},{4,6},{6,8},{8,10},{10,12},{12,14},{14,16},{16,18},{18... | collective-permute-start | bytes 1572872 | tf_op jit(solution)/shard_map/ppermute | solution.py:16
  402.0 1.2 copy-start.7
  404.8 1.0 copy-start.4
  405.8 7.6 %copy-start.2 = (bf16[1280,1024]{0,1:T(8,128)(2,1)S(1)}, bf16[1280,1024]{0,1:T(8,128)(2,1)}, u32[]{:S(2)}) copy-start(bf16[1280,1024]{0,1:T(8,128)(2,1)} %copy.64) | copy-start | bytes 7864324
  523.6 41.1 %copy-start = (bf16[256,2688]{1,0:T(8,128)(2,1)S(1)}, bf16[256,2688]{1,0:T(8,128)(2,1)}, u32[]{:S(2)}) copy-start(bf16[256,2688]{1,0:T(8,128)(2,1)} %param.9) | copy-start | bytes 4128772
Sparse Core Ops, SparseCore 0:
  8.9 43.1 all-gather.5
  54.4 90.7 all-gather.7
  147.5 94.5 all-gather.9
  243.5 147.2 all-gather.11
  392.3 117.6 all-gather.13
  523.7 39.0 reduce-scatter.3
where the time goes:
time: 574 us; the launch traced here: 573 us
  waiting for transfers between devices  385 us (67%)
  starting transfers between devices  89.8 us (16%)
  matrix products  46.8 us (8%)
  local copies, waits for them, and re-layouts  26.1 us (5%)
  between operations  13.8 us (2%)
  other arithmetic  11.4 us (2%)
    all_gather x1, waiting for transfers between devices, body(): lax.all_gather(output_weight, 'rows', axis=1, tiled=True)  94 us
    all_gather x1, waiting for transfers between devices, body(): lax.all_gather(value_weight, 'rows', axis=0, tiled=True)  90.5 us
    ppermute x8, starting transfers between devices, passed_along(): return lax.ppermute(value, axis, pairs)  89.6 us
    all_gather x1, waiting for transfers between devices, body(): lax.all_gather(key_weight, 'rows', axis=0, tiled=True)  86.7 us
    unnamed x7, waiting for transfers between devices  42.4 us
    all_gather x1, waiting for transfers between devices, body(): row_panel = lax.all_gather(activations, ('cols', 'sub'), axis=1, tiled=True)  41.5 us
    all_gather x1, waiting for transfers between devices, body(): lax.all_gather(query_weight, 'rows', axis=0, tiled=True)  29.8 us
    dot_general x3, matrix products, add_rows(): return jnp.dot(normed, weight_piece, preferred_element_type=jnp.float32)  25.8 us
  transfers between devices with their start and end apart: 14, of which 6 were waited for; matrix products, arithmetic and copies ran while one was open for 12% of the time, Pallas kernels for 0%

commit v1 on v0

--- a/solution.py
+++ b/solution.py
@@ -1,13 +1,22 @@
+import functools
 import math
 
 import jax
 import jax.numpy as jnp
 from jax import lax
+from jax.experimental import pallas as pl
+from jax.experimental.pallas import tpu as pltpu
+from jax.sharding import Mesh
 from jax.sharding import PartitionSpec as P
+
 
 HD = 128
 WINDOW = 1024
 QUERY_SCALAR = 168
+VMEM_BYTES = 67_000_000
+ANY = pl.BlockSpec(memory_space=pl.ANY)
+VMEM = pl.BlockSpec(memory_space=pltpu.VMEM)
+SMEM = pl.BlockSpec(memory_space=pltpu.SMEM)
 
 
 def passed_along(value, axis, by):
@@ -72,7 +81,7 @@
 def reach_back(key_rows, value_rows, reach_rows):
     pieces = []
     carried = (key_rows, value_rows)
-    for distance in range(reach_rows):
+    for _ in range(reach_rows):
         carried = passed_along((carried[0], carried[1]), "rows", 1)
         pieces.append(carried)
     ordered = pieces[::-1] + [(key_rows, value_rows)]
@@ -81,7 +90,7 @@
     return (all_keys, all_values)
 
 
-def body(
+def gathered_body(
     activations,
     positions,
     query_weight,
@@ -104,14 +113,9 @@
     def add_rows(weight_piece):
         return jnp.dot(normed, weight_piece, preferred_element_type=jnp.float32)
 
-    weight_piece = (
-        lax.all_gather(query_weight, "rows", axis=0, tiled=True),
-        lax.all_gather(key_weight, "rows", axis=0, tiled=True),
-        lax.all_gather(value_weight, "rows", axis=0, tiled=True),
-    )
-    query_raw = add_rows(weight_piece[0])
-    key_raw = add_rows(weight_piece[1])
-    value_raw = add_rows(weight_piece[2])
+    query_raw = add_rows(lax.all_gather(query_weight, "rows", axis=0, tiled=True))
+    key_raw = add_rows(lax.all_gather(key_weight, "rows", axis=0, tiled=True))
+    value_raw = add_rows(lax.all_gather(value_weight, "rows", axis=0, tiled=True))
     key_rows = rotate(head_norm(key_raw.reshape(rows_here, -1, HD), key_gain), own_positions)
     key_rows, value_rows = (
         key_rows.astype(jnp.bfloat16).reshape(rows_here, -1),
@@ -139,22 +143,440 @@
     return (activations.astype(jnp.float32) + summed).astype(jnp.bfloat16)
 
 
+def swapped(value, place=0, col=0):
+    places, cols = lax.axis_size("place"), lax.axis_size("cols")
+    pairs = [
+        (r * cols + c, (r ^ place) * cols + (c ^ col)) for r in range(places) for c in range(cols)
+    ]
+    return lax.ppermute(value, ("place", "cols"), pairs)
+
+
+def run(kernel, out_shape, in_specs, out_specs, scratch, flops, bytes_moved):
+    return pl.pallas_call(
+        kernel,
+        out_shape=out_shape,
+        in_specs=in_specs,
+        out_specs=out_specs,
+        scratch_shapes=scratch,
+        compiler_params=pltpu.CompilerParams(vmem_limit_bytes=VMEM_BYTES),
+        cost_estimate=pl.CostEstimate(
+            flops=int(flops), bytes_accessed=int(bytes_moved), transcendentals=0
+        ),
+    )
+
+
+def cut_kernel(n, meta, wq, wk, wv, kv_out, *outs):
+    place = meta[0]
+    wide_q = wq.shape[1] // n
+    for p in range(n):
+        kv_out[:, p * 2 * HD : p * 2 * HD + HD] = wk[:, p * HD : (p + 1) * HD]
+        kv_out[:, p * 2 * HD + HD : (p + 1) * 2 * HD] = wv[:, p * HD : (p + 1) * HD]
+    for m in range(n):
+        at = lax.bitwise_xor(place, m)
+        cols = pl.ds(pl.multiple_of(at * HD, HD), HD)
+        outs[m][:, :HD] = wk[:, cols]
+        outs[m][:, HD : 2 * HD] = wv[:, cols]
+        outs[m][:, 2 * HD :] = wq[:, pl.ds(pl.multiple_of(at * wide_q, 128), wide_q)]
+
+
+def join_kernel(*refs):
+    out = refs[-1]
+    deep = refs[0].shape[0]
+    for m, piece in enumerate(refs[:-1]):
+        out[m * deep : (m + 1) * deep] = piece[:, 2 * HD :]
+
+
+def pair_kernel(first, second, out):
+    out[0] = first[...]
+    out[1] = second[...]
+
+
+def normed_rotated(raw, gain, cosine, sine):
+    scaled = raw * lax.rsqrt(jnp.mean(raw * raw, axis=-1, keepdims=True) + 1e-06) * gain
+    return scaled * cosine + pltpu.roll(scaled, HD // 2, 1) * sine
+
+
+def project_kernel(n, reach, heads, meta, cosine, sine, key_gain, query_gain, *refs):
+    blocks, near, far = refs[: 2 * n], refs[2 * n : 3 * n], refs[3 * n : 4 * n]
+    q_far = refs[4 * n]
+    kv_out, tail_out, q_out = refs[4 * n + 1 : 4 * n + 4]
+    block_mem, weight_mem, block_sem, weight_sem = refs[4 * n + 4 :]
+    place, half, col = meta[0], meta[1], meta[2]
+    other = lax.bitwise_xor(half, 1)
+    _, _, tokens, features = block_mem.shape
+    deep = near[0].shape[0]
+    copies = []
+    for m in range(n):
+        rows = pl.ds(pl.multiple_of(lax.bitwise_xor(place, m) * deep, 16), deep)
+        source = pl.ds(pl.multiple_of((other * n + m) * deep, 16), deep)
+        for k, (start, target) in enumerate(
+            [
+                (near[m], weight_mem.at[half, rows, :]),
+                (far[m], weight_mem.at[other, rows, pl.ds(0, 2 * HD)]),
+                (q_far.at[source, :], weight_mem.at[other, rows, pl.ds(2 * HD, heads * HD)]),
+            ]
+        ):
+            copies.append(pltpu.make_async_copy(start, target, weight_sem.at[3 * m + k]))
+    for copy in copies:
+        copy.start()
+    for m in range(n):
+        for side in range(2):
+            pltpu.make_async_copy(
+                blocks[m * 2 + side], block_mem.at[side, m], block_sem.at[m, side]
+            ).start()
+    for copy in copies:
+        copy.wait()
+
+    @pl.loop(0, n // 2)
+    def _(t):
+        for m in range(2):
+            for side in range(2):
+                pltpu.make_async_copy(
+                    blocks[side], block_mem.at[side, 2 * t + m], block_sem.at[2 * t + m, side]
+                ).wait()
+        mine = block_mem[0, pl.ds(2 * t, 2)].reshape(2 * tokens, features)
+        theirs = block_mem[1, pl.ds(2 * t, 2)].reshape(2 * tokens, features)
+        raw_two = jnp.dot(mine, weight_mem[col], preferred_element_type=jnp.float32) + jnp.dot(
+            theirs, weight_mem[lax.bitwise_xor(col, 1)], preferred_element_type=jnp.float32
+        )
+        for m in range(2):
+            slot = 2 * t + m
+            at = lax.bitwise_xor(place, slot)
+            raw = raw_two[m * tokens : (m + 1) * tokens]
+            cosine_here, sine_here = cosine[at], sine[at]
+            keys = normed_rotated(raw[:, :HD], key_gain[...], cosine_here, sine_here)
+            keys = keys.astype(jnp.bfloat16)
+            values = raw[:, HD : 2 * HD].astype(jnp.bfloat16)
+            kv_out[at, :, :HD] = keys
+            kv_out[at, :, HD:] = values
+            for h in range(heads):
+                query = raw[:, (2 + h) * HD : (3 + h) * HD]
+                query = normed_rotated(query, query_gain[...], cosine_here, sine_here)
+                q_out[at, pl.ds(h * tokens, tokens), :] = query.astype(jnp.bfloat16)
+
+            @pl.when(at >= n - reach)
+            def _():
+                tail_out[at - (n - reach), :, :HD] = keys
+                tail_out[at - (n - reach), :, HD:] = values
+
+
+def attend_kernel(low, count, reach, heads, meta, q_doc, k_doc, queries, kv_own, *refs):
+    kv_back = refs[0] if low < reach else None
+    keep_out, send_out = refs[-2:]
+    col = meta[2]
+    tokens = kv_own.shape[1]
+    part = tokens // 2
+    scale = 1.0 / math.sqrt(QUERY_SCALAR)
+    row_at = lax.broadcasted_iota(jnp.int32, (tokens, tokens), 0)
+    col_at = lax.broadcasted_iota(jnp.int32, (tokens, tokens), 1)
+
+    for g in range(count):
+        doc = q_doc[low + g]
+        query = queries[low + g]
+        totals = jnp.zeros((heads * tokens, 1), jnp.float32)
+        mixed = jnp.zeros((heads * tokens, HD), jnp.float32)
+        for step in range(reach + 1):
+            at = low + g + step
+            pair = kv_back[at] if at < reach else kv_own[at - reach]
+            visible = doc == k_doc[at]
+            if step == 0:
+                visible = visible & (row_at < col_at)
+            if step == reach:
+                visible = visible & (row_at >= col_at)
+            scores = lax.dot_general(
+                query, pair[:, :HD], (((1,), (1,)), ((), ())), preferred_element_type=jnp.float32
+            )
+            weights_here = jnp.where(
+                visible[None], jnp.exp(scores * scale).reshape(heads, tokens, tokens), 0.0
+            ).reshape(heads * tokens, tokens)
+            totals = totals + jnp.sum(weights_here, axis=-1, keepdims=True)
+            mixed = mixed + jnp.dot(
+                weights_here.astype(jnp.bfloat16), pair[:, HD:], preferred_element_type=jnp.float32
+            )
+        done = (mixed / totals).astype(jnp.bfloat16)
+        for h in range(heads):
+            top = done[h * tokens : h * tokens + part]
+            bottom = done[h * tokens + part : (h + 1) * tokens]
+            keep_out[g, :, h * HD : (h + 1) * HD] = jnp.where(col == 0, top, bottom)
+            send_out[g, :, h * HD : (h + 1) * HD] = jnp.where(col == 0, bottom, top)
+
+
+def output_kernel(n, spans, meta, *refs):
+    count = n * len(spans)
+    contexts, weights = refs[:count], refs[count : count + 6]
+    out, context_mem, weight_mem, context_sem, weight_sem = refs[count + 6 :]
+    place, half, col = meta[0], meta[1], meta[2]
+    deep = weights[0].shape[1]
+    wide = contexts[0].shape[3]
+    part = contexts[0].shape[2]
+    copies = []
+    for k, source in enumerate(weights):
+        owner = half if k < 2 else lax.bitwise_xor(half, 1)
+        rows = source.shape[0]
+        first = 0 if k < 4 else weights[2].shape[0]
+        side = pl.multiple_of(lax.bitwise_xor(col, k % 2) * deep, 128)
+        copies.append(
+            pltpu.make_async_copy(
+                source,
+                weight_mem.at[owner, pl.ds(first, rows), pl.ds(side, deep)],
+                weight_sem.at[k],
+            )
+        )
+    for s, (low, size) in enumerate(spans):
+        for m in range(n):
+            for side in range(2):
+                first = lax.bitwise_xor(col, side) * deep + lax.bitwise_xor(place, m) * wide
+                copies.append(
+                    pltpu.make_async_copy(
+                        contexts[s * n + m].at[side],
+                        context_mem.at[
+                            pl.ds(low, size), :, pl.ds(pl.multiple_of(first, 128), wide)
+                        ],
+                        context_sem.at[(s * n + m) * 2 + side],
+                    )
+                )
+    for copy in copies:
+        copy.start()
+    for copy in copies:
+        copy.wait()
+
+    @pl.loop(0, n // 4)
+    def _(t):
+        left = context_mem[pl.ds(4 * t, 4)].reshape(4 * part, 2 * deep)
+        for block in range(2):
+            result = lax.dot_general(
+                left,
+                weight_mem[block],
+                (((1,), (1,)), ((), ())),
+                preferred_element_type=jnp.float32,
+            ).astype(jnp.bfloat16)
+            for k in range(4):
+                out[(4 * t + k) * 2 + block] = result[k * part : (k + 1) * part]
+
+
+def close_kernel(n, activations, arrived, out):
+    part = arrived.shape[1]
+    for col in range(2):
+        rows = pl.ds(col * part, part)
+        whole = jnp.concatenate([arrived[2 * p + col] for p in range(n)], axis=1)
+        out[rows, :] = (
+            activations[rows, :].astype(jnp.float32) + whole.astype(jnp.float32)
+        ).astype(jnp.bfloat16)
+
+
+def split_body(
+    activations,
+    positions,
+    query_weight,
+    key_weight,
+    value_weight,
+    output_weight,
+    input_gain,
+    query_gain,
+    key_gain,
+):
+    tokens, features = activations.shape
+    n = key_weight.shape[1] // HD
+    heads = query_weight.shape[1] // key_weight.shape[1]
+    reach = WINDOW // tokens
+    part = tokens // 2
+    half, place, col = lax.axis_index("half"), lax.axis_index("place"), lax.axis_index("cols")
+    meta = jnp.stack([place, half, col]).astype(jnp.int32)
+    bf16, f32 = jnp.bfloat16, jnp.float32
+    shaped = jax.ShapeDtypeStruct
+
+    deep = query_weight.shape[0]
+    kv_cut, *cut = run(
+        functools.partial(cut_kernel, n),
+        [shaped((deep, n * 2 * HD), bf16)] + [shaped((deep, (2 + heads) * HD), bf16)] * n,
+        [SMEM, VMEM, VMEM, VMEM],
+        [VMEM] * (n + 1),
+        [],
+        0,
+        5 * query_weight.size * 2,
+    )(meta, query_weight, key_weight, value_weight)
+    kv_rows = lax.all_gather(kv_cut, "half", axis=0, tiled=True)
+
+    wide = activations.astype(f32)
+    squares = jnp.sum(wide * wide, axis=-1).reshape(2, part)
+    squares = (squares + swapped(squares, 0, 1)).reshape(tokens, 1)
+    inverse = lax.rsqrt(squares / (2 * features) + 1e-06)
+    gain = lax.dynamic_slice_in_dim(input_gain, col * features, features, 0)
+    normed = (wide * inverse * gain).astype(bf16)
+
+    z, y, c = n // 2, n // 4, 1
+    blocks = {(0, 0): normed}
+    blocks[y, 0] = swapped(normed, y, 0)
+    blocks[0, 1] = swapped(normed, 0, 1)
+    blocks[z, 0] = swapped(normed, z, 0)
+    blocks[y, 1] = swapped(blocks[y, 0], 0, 1)
+    blocks[z, 1] = swapped(blocks[z, 0], 0, 1)
+    blocks[z + y, 0] = swapped(blocks[z, 0], y, 0)
+    blocks[z + y, 1] = swapped(blocks[z + y, 0], 0, 1)
+    for m, side in list(blocks):
+        blocks[m + c, side] = swapped(blocks[m, side], c, 0)
+    block_list = [blocks[m, side] for m in range(n) for side in range(2)]
+
+    in_half = lax.dynamic_slice_in_dim(positions, half * n * tokens, n * tokens, 0)
+    frequency = 10000.0 ** (-(jnp.arange(HD // 2, dtype=f32) * 2.0 / HD))
+    angles = in_half.astype(f32)[:, None] * frequency[None, :]
+    cosine, sine = jnp.cos(angles), jnp.sin(angles)
+    cosine = jnp.concatenate([cosine, cosine], -1).reshape(n, tokens, HD)
+    sine = jnp.concatenate([-sine, sine], -1).reshape(n, tokens, HD)
+    index = jnp.arange(positions.shape[0], dtype=jnp.int32)
+    starts = jnp.concatenate(
+        [jnp.full((reach * tokens,), -(2**30), jnp.int32), index - positions], 0
+    )
+    docs = lax.dynamic_slice_in_dim(starts, half * n * tokens, (n + reach) * tokens, 0)
+    k_doc = docs.reshape(n + reach, 1, tokens)
+    q_doc = docs[reach * tokens :].reshape(n, tokens, 1)
+
+    near = [cut[0]] + [swapped(cut[m], m, 0) for m in range(1, n)]
+    q_own = run(
+        join_kernel,
+        shaped((n * deep, heads * HD), bf16),
+        [VMEM] * n,
+        VMEM,
+        [],
+        0,
+        6 * n * deep * heads * HD,
+    )(*near)
+    q_rows = lax.all_gather(q_own, "half", axis=0, tiled=True)
+    kv_rows, cosine, sine, q_doc = lax.optimization_barrier((kv_rows, cosine, sine, q_doc))
+    far = []
+    for m in range(n):
+        first = lax.bitwise_xor(place, m) * 2 * HD
+        piece = lax.dynamic_slice(kv_rows, ((1 - half) * deep, first), (deep, 2 * HD))
+        far.append(piece if m == 0 else swapped(piece, m, 0))
+
+    flops = 2 * n * tokens * 2 * features * (2 + heads) * HD
+    kv_own, kv_tail, queries = run(
+        functools.partial(project_kernel, n, reach, heads),
+        [
+            shaped((n, tokens, 2 * HD), bf16),
+            shaped((reach, tokens, 2 * HD), bf16),
+            shaped((n, heads * tokens, HD), bf16),
+        ],
+        [SMEM, VMEM, VMEM, VMEM, VMEM] + [ANY] * (4 * n + 1),
+        [VMEM, VMEM, VMEM],
+        [
+            pltpu.VMEM((2, n, tokens, features), bf16),
+            pltpu.VMEM((2, features, (2 + heads) * HD), bf16),
+            pltpu.SemaphoreType.DMA((n, 2)),
+            pltpu.SemaphoreType.DMA((3 * n,)),
+        ],
+        flops,
+        2 * n * tokens * features * 2,
+    )(
+        meta,
+        cosine,
+        sine,
+        key_gain.reshape(1, HD),
+        query_gain.reshape(1, HD),
+        *block_list,
+        *near,
+        *far,
+        q_rows,
+    )
+    kv_back = lax.ppermute(kv_tail, "half", [(0, 1)])
+
+    own_weight = output_weight.T
+    ahead = own_weight.shape[0] // 32 * 16
+    own_weight, _ = lax.optimization_barrier((own_weight, q_own))
+    out_weights = [own_weight, swapped(own_weight, 0, 1)]
+    for rows in [own_weight[:ahead], own_weight[ahead:]]:
+        both = lax.all_gather(rows, "half", axis=0)
+        piece = lax.dynamic_index_in_dim(both, 1 - half, 0, keepdims=False)
+        out_weights += [piece, swapped(piece, 0, 1)]
+
+    contexts = []
+    spans = [(reach, n - reach), (0, reach)]
+    for low, count in spans:
+        backs = [kv_back] if low < reach else []
+        shape = shaped((count, part, heads * HD), bf16)
+        keep, send = run(
+            functools.partial(attend_kernel, low, count, reach, heads),
+            [shape, shape],
+            [SMEM] + [VMEM] * (4 + len(backs)),
+            [VMEM, VMEM],
+            [],
+            8 * count * heads * tokens * (reach + 1) * tokens * HD,
+            4 * n * tokens * 2 * HD,
+        )(meta, q_doc, k_doc, queries, kv_own, *backs)
+        there = swapped(send, 0, 1)
+        pair = run(
+            pair_kernel,
+            shaped((2, count, part, heads * HD), bf16),
+            [VMEM, VMEM],
+            VMEM,
+            [],
+            0,
+            8 * count * part * heads * HD,
+        )(keep, there)
+        pairs = {0: pair}
+        pairs[z] = swapped(pair, z, 0)
+        pairs[y] = swapped(pair, y, 0)
+        pairs[z + y] = swapped(pairs[z], y, 0)
+        for m in list(pairs):
+            pairs[m + c] = swapped(pairs[m], c, 0)
+        contexts += [pairs[m] for m in range(n)]
+
+    out_cols = output_weight.shape[1]
+    deep_out = output_weight.shape[0]
+    result = run(
+        functools.partial(output_kernel, n, spans),
+        shaped((2 * n, part, out_cols), bf16),
+        [SMEM] + [ANY] * (2 * n + 6),
+        VMEM,
+        [
+            pltpu.VMEM((n, part, 2 * deep_out), bf16),
+            pltpu.VMEM((2, out_cols, 2 * deep_out), bf16),
+            pltpu.SemaphoreType.DMA((4 * n,)),
+            pltpu.SemaphoreType.DMA((6,)),
+        ],
+        2 * n * part * 2 * deep_out * 2 * out_cols,
+        16 * deep_out * out_cols,
+    )(meta, *contexts, *out_weights)
+
+    arrived = lax.all_to_all(result, ("place", "cols"), 0, 0, tiled=True)
+    return run(
+        functools.partial(close_kernel, n),
+        shaped((tokens, features), bf16),
+        [VMEM, VMEM],
+        VMEM,
+        [],
+        0,
+        6 * tokens * features,
+    )(activations, arrived)
+
+
 def solution(mesh):
+    sizes = mesh.shape
+    if sizes["cols"] == 2 and sizes["sub"] == 1 and sizes["rows"] == 16:
+        shape = (sizes["groups"], 2, sizes["rows"] // 2, sizes["cols"], sizes["sub"])
+        names = ("groups", "half", "place", "cols", "sub")
+        fine, rows = Mesh(mesh.devices.reshape(shape), names), ("half", "place")
+    else:
+        fine, rows = mesh, ("rows",)
+    columns = ("cols", "sub")
     placed = (
-        P(("groups", "rows"), ("cols", "sub")),
+        P(("groups", *rows), columns),
         P("groups"),
-        P("rows", ("cols", "sub")),
-        P("rows", ("cols", "sub")),
-        P("rows", ("cols", "sub")),
-        P(("cols", "sub"), "rows"),
+        P(rows, columns),
+        P(rows, columns),
+        P(rows, columns),
+        P(columns, rows),
         P(),
         P(),
         P(),
     )
-    return jax.shard_map(
-        body,
-        mesh=mesh,
-        in_specs=placed,
-        out_specs=P(("groups", "rows"), ("cols", "sub")),
-        check_vma=False,
-    )
+
+    def mapped(body):
+        return jax.shard_map(
+            body, mesh=fine, in_specs=placed, out_specs=placed[0], check_vma=False
+        )
+
+    if fine is mesh:
+        return mapped(gathered_body)
+
+    return mapped(split_body)

time: 574 us -> 462 us (0.80)
  waiting for transfers between devices: 385 us -> 260 us
  Pallas kernels: 0 us -> 70.5 us
  matrix products: 46.8 us -> 0 us
  blocking collectives: 0 us -> 24.4 us
  starting transfers between devices: 89.8 us -> 66.1 us
  local copies, waits for them, and re-layouts: 26.1 us -> 19.3 us
    all_gather x5 -> x4, waiting for transfers between devices: 343 us -> 0.02 us  [the longest x1 0.02 us: split_body(): kv_rows = lax.all_gather(kv_cut, 'half', axis=0, tiled=True)]
    ppermute x8 -> x50, waiting for transfers between devices: 0.02 us -> 259 us  [the longest x49 259 us: swapped(): return lax.ppermute(value, ('place', 'cols'), pairs)]
    pallas_call x0 -> x9, Pallas kernels: none -> 70.5 us  [the longest x1 27.6 us: split_body(): run(functools.partial(project_kernel, n, reach, heads), [shaped((n, token...]
    dot_general x6 -> x0, matrix products: 46.8 us -> none  [the longest x3 25.8 us: add_rows(): return jnp.dot(normed, weight_piece, preferred_element_type=jnp.float32)]
    unnamed x7 -> x4, waiting for transfers between devices: 42.4 us -> 0.07 us
    all_to_all x0 -> x1, blocking collectives: none -> 24.4 us  [split_body(): arrived = lax.all_to_all(result, ('place', 'cols'), 0, 0, tiled=True)]
    ppermute x8 -> x50, starting transfers between devices: 89.6 us -> 66 us  [the longest x49 60.3 us: swapped(): return lax.ppermute(value, ('place', 'cols'), pairs)]
    unnamed x30 -> x58, local copies, waits for them, and re-layouts: 15.7 us -> 3.38 us
  transfers between devices with their start and end apart: 14 -> 54, of which waited for: 6 -> 24; matrix products, arithmetic and copies ran while one was open for 12% -> 4% of each run, Pallas kernels for 0% -> 10%
where the time goes in v1:
time: 462 us; the launch traced here: 461 us
  waiting for transfers between devices  260 us (56%)
  Pallas kernels  70.5 us (15%)
  starting transfers between devices  66.1 us (14%)
  blocking collectives  24.4 us (5%)
  local copies, waits for them, and re-layouts  19.3 us (4%)
  between operations  13.6 us (3%)
  other arithmetic  8.09 us (2%)
    ppermute x49, waiting for transfers between devices, swapped(): return lax.ppermute(value, ('place', 'cols'), pairs)  259 us
    ppermute x49, starting transfers between devices, swapped(): return lax.ppermute(value, ('place', 'cols'), pairs)  60.3 us
    pallas_call x1, Pallas kernels, split_body(): run(functools.partial(project_kernel, n, reach, heads), [shaped((n, token...  27.6 us
    all_to_all x1, blocking collectives, split_body(): arrived = lax.all_to_all(result, ('place', 'cols'), 0, 0, tiled=True)  24.4 us
    pallas_call x1, Pallas kernels, split_body(): run(functools.partial(output_kernel, n, spans), shaped((2 * n, part, out_...  16.3 us
    pallas_call x2, Pallas kernels, split_body(): run(functools.partial(attend_kernel, low, count, reach, heads), [shape, s...  12.1 us
  transfers between devices with their start and end apart: 54, of which 24 were waited for; matrix products, arithmetic and copies ran while one was open for 4% of the time, Pallas kernels for 10%

profile of v1, /device:TPU:0, one launch (start us, length us, event | category | flops | bytes accessed | tf_op | source)
XLA Modules:
  0.0 461.5 jit_solution(9948602276046496785)
XLA Ops:
  7.1 4.5 shard_map.91
  13.3 3.0 collective-permute-start
  19.4 2.1 collective-permute-start.8
  25.1 7.5 %collective-permute-done.17.refs_2_.refs_18_ = bf16[336,512]{1,0:T(8,128)(2,1)} collective-permute-done((bf16[336,512]{1,0:T(8,128)(2,1)S(1)}, bf16[336,512]{1,0:T(8,128)(2,1)}, u32[]{:S(2)}, u32[]{:S(2)}) %collective-permute-start.17) | collective-permute-done | bytes 344096 | tf_op jit(solution)/shard_map/ppermute | solution.py:151
  34.1 4.9 %collective-permute-done.18.refs_3_.refs_19_ = bf16[336,512]{1,0:T(8,128)(2,1)} collective-permute-done((bf16[336,512]{1,0:T(8,128)(2,1)S(1)}, bf16[336,512]{1,0:T(8,128)(2,1)}, u32[]{:S(2)}, u32[]{:S(2)}) %collective-permute-start.18) | collective-permute-done | bytes 344096 | tf_op jit(solution)/shard_map/ppermute | solution.py:151
  40.6 49.1 %collective-permute-done.19.refs_4_.refs_20_ = bf16[336,512]{1,0:T(8,128)(2,1)} collective-permute-done((bf16[336,512]{1,0:T(8,128)(2,1)S(1)}, bf16[336,512]{1,0:T(8,128)(2,1)}, u32[]{:S(2)}, u32[]{:S(2)}) %collective-permute-start.19) | collective-permute-done | bytes 344096 | tf_op jit(solution)/shard_map/ppermute | solution.py:151
  89.7 2.0 collective-permute-start.4
  91.7 4.8 %collective-permute-done.20.refs_5_.refs_21_ = bf16[336,512]{1,0:T(8,128)(2,1)} collective-permute-done((bf16[336,512]{1,0:T(8,128)(2,1)S(1)}, bf16[336,512]{1,0:T(8,128)(2,1)}, u32[]{:S(2)}, u32[]{:S(2)}) %collective-permute-start.20) | collective-permute-done | bytes 344096 | tf_op jit(solution)/shard_map/ppermute | solution.py:151
  97.2 8.8 %collective-permute-done.21.refs_6_.refs_22_ = bf16[336,512]{1,0:T(8,128)(2,1)} collective-permute-done((bf16[336,512]{1,0:T(8,128)(2,1)S(1)}, bf16[336,512]{1,0:T(8,128)(2,1)}, u32[]{:S(2)}, u32[]{:S(2)}) %collective-permute-start.21) | collective-permute-done | bytes 344096 | tf_op jit(solution)/shard_map/ppermute | solution.py:151
  109.1 2.9 shard_map.92
  112.1 1.9 collective-permute-start.10
  114.0 23.9 %collective-permute-done.4.refs_4_ = bf16[256,2688]{1,0:T(8,128)(2,1)} collective-permute-done((bf16[256,2688]{1,0:T(8,128)(2,1)}, bf16[256,2688]{1,0:T(8,128)(2,1)}, u32[]{:S(2)}, u32[]{:S(2)}) %collective-permute-start.4) | collective-permute-done | bytes 1376288 | tf_op jit(solution)/shard_map/ppermute | solution.py:151
  137.9 1.9 collective-permute-start.9
  140.0 22.5 %collective-permute-done.12.refs_12_ = bf16[256,2688]{1,0:T(8,128)(2,1)} collective-permute-done((bf16[256,2688]{1,0:T(8,128)(2,1)}, bf16[256,2688]{1,0:T(8,128)(2,1)}, u32[]{:S(2)}, u32[]{:S(2)}) %collective-permute-start.12) | collective-permute-done | bytes 1376288 | tf_op jit(solution)/shard_map/ppermute | solution.py:151
  163.9 3.7 fusion.3
  167.7 1.9 pad_maximum_fusion
  171.6 29.1 %collective-permute-done.5.refs_5_ = bf16[256,2688]{1,0:T(8,128)(2,1)} collective-permute-done((bf16[256,2688]{1,0:T(8,128)(2,1)}, bf16[256,2688]{1,0:T(8,128)(2,1)}, u32[]{:S(2)}, u32[]{:S(2)}) %collective-permute-start.5) | collective-permute-done | bytes 1376288 | tf_op jit(solution)/shard_map/ppermute | solution.py:151
  200.7 21.6 %collective-permute-done.13.refs_13_ = bf16[256,2688]{1,0:T(8,128)(2,1)} collective-permute-done((bf16[256,2688]{1,0:T(8,128)(2,1)}, bf16[256,2688]{1,0:T(8,128)(2,1)}, u32[]{:S(2)}, u32[]{:S(2)}) %collective-permute-start.13) | collective-permute-done | bytes 1376288 | tf_op jit(solution)/shard_map/ppermute | solution.py:151
  222.4 2.0 slice.21
  224.5 2.2 fusion.4
  228.4 5.3 %collective-permute-done.29.refs_31_ = bf16[336,256]{1,0:T(8,128)(2,1)S(1)} collective-permute-done((bf16[336,256]{1,0:T(8,128)(2,1)S(1)}, bf16[336,256]{1,0:T(8,128)(2,1)S(1)}, u32[]{:S(2)}, u32[]{:S(2)}) %collective-permute-start.29) | collective-permute-done | bytes 172064 | tf_op jit(solution)/shard_map/ppermute | solution.py:151
  235.3 8.3 %collective-permute-done.28.refs_30_ = bf16[336,256]{1,0:T(8,128)(2,1)S(1)} collective-permute-done((bf16[336,256]{1,0:T(8,128)(2,1)S(1)}, bf16[336,256]{1,0:T(8,128)(2,1)S(1)}, u32[]{:S(2)}, u32[]{:S(2)}) %collective-permute-start.28) | collective-permute-done | bytes 172064 | tf_op jit(solution)/shard_map/ppermute | solution.py:151
  243.6 2.9 collective-permute-start.27
  246.5 7.8 %collective-permute-done.27.refs_29_ = bf16[336,256]{1,0:T(8,128)(2,1)S(1)} collective-permute-done((bf16[336,256]{1,0:T(8,128)(2,1)S(1)}, bf16[336,256]{1,0:T(8,128)(2,1)S(1)}, u32[]{:S(2)}, u32[]{:S(2)}) %collective-permute-start.27) | collective-permute-done | bytes 172064 | tf_op jit(solution)/shard_map/ppermute | solution.py:151
  254.3 2.5 collective-permute-start.26
  256.8 10.6 %collective-permute-done.26.refs_28_ = bf16[336,256]{1,0:T(8,128)(2,1)S(1)} collective-permute-done((bf16[336,256]{1,0:T(8,128)(2,1)S(1)}, bf16[336,256]{1,0:T(8,128)(2,1)S(1)}, u32[]{:S(2)}, u32[]{:S(2)}) %collective-permute-start.26) | collective-permute-done | bytes 172064 | tf_op jit(solution)/shard_map/ppermute | solution.py:151
  267.8 6.3 %collective-permute-done.25.refs_27_ = bf16[336,256]{1,0:T(8,128)(2,1)S(1)} collective-permute-done((bf16[336,256]{1,0:T(8,128)(2,1)S(1)}, bf16[336,256]{1,0:T(8,128)(2,1)S(1)}, u32[]{:S(2)}, u32[]{:S(2)}) %collective-permute-start.25) | collective-permute-done | bytes 172064 | tf_op jit(solution)/shard_map/ppermute | solution.py:151
  275.0 5.4 %collective-permute-done.24.refs_26_ = bf16[336,256]{1,0:T(8,128)(2,1)S(1)} collective-permute-done((bf16[336,256]{1,0:T(8,128)(2,1)S(1)}, bf16[336,256]{1,0:T(8,128)(2,1)S(1)}, u32[]{:S(2)}, u32[]{:S(2)}) %collective-permute-start.24) | collective-permute-done | bytes 172064 | tf_op jit(solution)/shard_map/ppermute | solution.py:151
  280.4 2.1 slice.22
  284.2 27.6 %shard_map.93 = (bf16[8,256,256]{2,1,0:T(8,128)(2,1)}, bf16[4,256,256]{2,1,0:T(8,128)(2,1)}, bf16[8,512,128]{2,1,0:T(8,128)(2,1)}) custom-call(s32[3]{0:T(128)} %pad_add_fusion.meta, f32[8,256,128]{2,1,0:T(8,128)} %get-tuple-element.28.cosine, f32[8,256,128]{2,1,0:T(8,128)} %get-tuple-element.29.sine, f32[1,128]{1,0:T(1,128)} %bitcast.22, ...), custom_call_target="tpu_custom_call" | custom-call | flops 11274289152 | bytes 22020096 | tf_op jit(solution)/shard_map/pallas_call | solution.py:453
  311.9 5.7 %collective-permute-start.38 = (bf16[4,256,256]{2,1,0:T(8,128)(2,1)}, bf16[4,256,256]{2,1,0:T(8,128)(2,1)}, u32[]{:S(2)}, u32[]{:S(2)}) collective-permute-start(bf16[4,256,256]{2,1,0:T(8,128)(2,1)} %get-tuple-element.43), channel_id=1, source_target_pairs={{0,16},{1,17},{2,18},{3,19},{4,20},{5,21},{6,22},{7,23},{8,24},{9,... | collective-permute-start | bytes 1572872 | tf_op jit(solution)/shard_map/ppermute | solution.py:481
  318.2 2.0 dynamic-slice_bitcast_fusion.1.refs_18_
  322.1 6.0 %shard_map.94 = (bf16[4,128,256]{2,1,0:T(8,128)(2,1)}, bf16[4,128,256]{2,1,0:T(8,128)(2,1)}) custom-call(s32[3]{0:T(128)} %pad_add_fusion.meta, s32[8,256,1]{2,1,0:T(8,128)} %copy.12.q_doc, s32[12,1,256]{2,1,0:T(1,128)} %bitcast.19, bf16[8,512,128]{2,1,0:T(8,128)(2,1)} %get-tuple-element.39.queries, bf16[8,256,256]{2,1,0:T(8,128)(2,1)} %get-tuple-element.40.kv_own), custom_call_target="tpu_custom_call" | custom-call | flops 2684354560 | bytes 2097152 | tf_op jit(solution)/shard_map/pallas_call | solution.py:497
  329.6 6.1 %shard_map.96 = (bf16[4,128,256]{2,1,0:T(8,128)(2,1)}, bf16[4,128,256]{2,1,0:T(8,128)(2,1)}) custom-call(s32[3]{0:T(128)} %pad_add_fusion.meta, s32[8,256,1]{2,1,0:T(8,128)} %copy.12.q_doc, s32[12,1,256]{2,1,0:T(1,128)} %bitcast.20, bf16[8,512,128]{2,1,0:T(8,128)(2,1)} %get-tuple-element.39.queries, bf16[8,256,256]{2,1,0:T(8,128)(2,1)} %get-tuple-element.40.kv_own, ...), custom_call_target="tpu_custom_call" | custom-call | flops 2684354560 | bytes 2097152 | tf_op jit(solution)/shard_map/pallas_call | solution.py:497
  336.2 2.0 dynamic-slice_bitcast_fusion.refs_20_
  339.7 4.0 collective-permute-done.30.second
  343.8 1.9 shard_map.95.refs_0_
  345.6 12.3 %collective-permute-start.34 = (bf16[2,4,128,256]{3,2,1,0:T(8,128)(2,1)}, bf16[2,4,128,256]{3,2,1,0:T(8,128)(2,1)}, u32[]{:S(2)}, u32[]{:S(2)}) collective-permute-start(bf16[2,4,128,256]{3,2,1,0:T(8,128)(2,1)} %shard_map.95.refs_0_), channel_id=1, source_target_pairs={{0,8},{1,9},{2,10},{3,11},{4,12},{5,13},{6,14},{7,15},{8,0},{9,1},... | collective-permute-start | bytes 1572872 | tf_op jit(solution)/shard_map/ppermute | solution.py:151
  361.5 3.6 collective-permute-start.43
  365.2 5.9 %collective-permute-done.34.refs_4_ = bf16[2,4,128,256]{3,2,1,0:T(8,128)(2,1)} collective-permute-done((bf16[2,4,128,256]{3,2,1,0:T(8,128)(2,1)}, bf16[2,4,128,256]{3,2,1,0:T(8,128)(2,1)}, u32[]{:S(2)}, u32[]{:S(2)}) %collective-permute-start.34) | collective-permute-done | bytes 524320 | tf_op jit(solution)/shard_map/ppermute | solution.py:151
  373.6 7.4 %collective-permute-done.43.refs_12_ = bf16[2,4,128,256]{3,2,1,0:T(8,128)(2,1)S(1)} collective-permute-done((bf16[2,4,128,256]{3,2,1,0:T(8,128)(2,1)}, bf16[2,4,128,256]{3,2,1,0:T(8,128)(2,1)S(1)}, u32[]{:S(2)}, u32[]{:S(2)}) %collective-permute-start.43) | collective-permute-done | bytes 524320 | tf_op jit(solution)/shard_map/ppermute | solution.py:151
  382.7 3.4 collective-permute-done.36.refs_6_
  386.8 10.6 %collective-permute-done.41.refs_10_ = bf16[2,4,128,256]{3,2,1,0:T(8,128)(2,1)S(1)} collective-permute-done((bf16[2,4,128,256]{3,2,1,0:T(8,128)(2,1)}, bf16[2,4,128,256]{3,2,1,0:T(8,128)(2,1)S(1)}, u32[]{:S(2)}, u32[]{:S(2)}) %collective-permute-start.41) | collective-permute-done | bytes 524320 | tf_op jit(solution)/shard_map/ppermute | solution.py:151
  397.3 7.9 %collective-permute-done.45.refs_14_ = bf16[2,4,128,256]{3,2,1,0:T(8,128)(2,1)S(1)} collective-permute-done((bf16[2,4,128,256]{3,2,1,0:T(8,128)(2,1)S(1)}, bf16[2,4,128,256]{3,2,1,0:T(8,128)(2,1)S(1)}, u32[]{:S(2)}, u32[]{:S(2)}) %collective-permute-start.45) | collective-permute-done | bytes 524320 | tf_op jit(solution)/shard_map/ppermute | solution.py:151
  407.4 16.3 %shard_map.98 = bf16[16,128,336]{2,1,0:T(8,128)(2,1)} custom-call(s32[3]{0:T(128)} %pad_add_fusion.meta, bf16[2,4,128,256]{3,2,1,0:T(8,128)(2,1)} %shard_map.95.refs_0_, bf16[2,4,128,256]{3,2,1,0:T(8,128)(2,1)} %collective-permute-done.31.refs_1_, bf16[2,4,128,256]{3,2,1,0:T(8,128)(2,1)} %collective-permute-done.32.refs_2_, ...), custom_call_target="tpu_custom_call" | custom-call | flops 5637144576 | bytes 11010048 | tf_op jit(solution)/shard_map/pallas_call | solution.py:526
  423.7 1.9 copy.14
  425.6 24.4 %all_to_all.5 = bf16[16,128,336]{1,2,0:T(8,128)(2,1)S(1)} all-to-all(bf16[16,128,336]{1,2,0:T(8,128)(2,1)S(1)} %copy.14), channel_id=1, replica_groups=mesh['groups'=1,'half'=2,'place'=8,'cols'=2,'sub'=1] {'place','cols'}, dimensions={0} | all-to-all | bytes 2752512 | tf_op jit(solution)/shard_map/all_to_all | solution.py:541
  451.6 3.4 shard_map.99
  (154 shorter events, 43.7 us)
Async XLA Ops:
  6.5 218.0 %all-gather.7.cloned.1.call-start = ((), (), s32[]{:S(2)}) async-start(), calls=%async_computation.1 | async-start | bytes 4128768 | tf_op jit(solution)/shard_map/all_gather | solution.py:398
  11.7 272.5 %all-gather.9.cloned.1.call-start = ((), (), s32[]{:S(2)}) async-start(), calls=%async_computation.2 | async-start | bytes 4128768 | tf_op jit(solution)/shard_map/all_gather | solution.py:444
  19.4 88.1 %collective-permute-start.8 = (bf16[256,2688]{1,0:T(8,128)(2,1)}, bf16[256,2688]{1,0:T(8,128)(2,1)}, u32[]{:S(2)}, u32[]{:S(2)}) collective-permute-start(bf16[256,2688]{1,0:T(8,128)(2,1)} %fusion.2.refs_0_), channel_id=1, source_target_pairs={{0,8},{1,9},{2,10},{3,11},{4,12},{5,13},{6,14},{7,15},{8,0},{9,1},... | collective-permute-start | bytes 4128776 | tf_op jit(solution)/shard_map/ppermute | solution.py:151
  21.5 11.1 %collective-permute-start.17 = (bf16[336,512]{1,0:T(8,128)(2,1)S(1)}, bf16[336,512]{1,0:T(8,128)(2,1)}, u32[]{:S(2)}, u32[]{:S(2)}) collective-permute-start(bf16[336,512]{1,0:T(8,128)(2,1)S(1)} %copy-done.20), channel_id=1, source_target_pairs={{0,4},{1,5},{2,6},{3,7},{4,0},{5,1},{6,2},{7,3},{8,12},{9,13},{10,... | collective-permute-start | bytes 1032200 | tf_op jit(solution)/shard_map/ppermute | solution.py:151
  23.1 15.8 %collective-permute-start.18 = (bf16[336,512]{1,0:T(8,128)(2,1)S(1)}, bf16[336,512]{1,0:T(8,128)(2,1)}, u32[]{:S(2)}, u32[]{:S(2)}) collective-permute-start(bf16[336,512]{1,0:T(8,128)(2,1)S(1)} %copy-done.19), channel_id=1, source_target_pairs={{0,6},{1,7},{2,4},{3,5},{4,2},{5,3},{6,0},{7,1},{8,14},{9,15},{10,... | collective-permute-start | bytes 1032200 | tf_op jit(solution)/shard_map/ppermute | solution.py:151
  23.4 66.3 %collective-permute-start.19 = (bf16[336,512]{1,0:T(8,128)(2,1)S(1)}, bf16[336,512]{1,0:T(8,128)(2,1)}, u32[]{:S(2)}, u32[]{:S(2)}) collective-permute-start(bf16[336,512]{1,0:T(8,128)(2,1)S(1)} %copy-done.18), channel_id=1, source_target_pairs={{0,8},{1,9},{2,10},{3,11},{4,12},{5,13},{6,14},{7,15},{8,0},{9,1},... | collective-permute-start | bytes 1032200 | tf_op jit(solution)/shard_map/ppermute | solution.py:151
  23.7 72.8 %collective-permute-start.20 = (bf16[336,512]{1,0:T(8,128)(2,1)S(1)}, bf16[336,512]{1,0:T(8,128)(2,1)}, u32[]{:S(2)}, u32[]{:S(2)}) collective-permute-start(bf16[336,512]{1,0:T(8,128)(2,1)S(1)} %copy-done.17), channel_id=1, source_target_pairs={{0,10},{1,11},{2,8},{3,9},{4,14},{5,15},{6,12},{7,13},{8,2},{9,3},... | collective-permute-start | bytes 1032200 | tf_op jit(solution)/shard_map/ppermute | solution.py:151
  32.7 73.3 %collective-permute-start.21 = (bf16[336,512]{1,0:T(8,128)(2,1)S(1)}, bf16[336,512]{1,0:T(8,128)(2,1)}, u32[]{:S(2)}, u32[]{:S(2)}) collective-permute-start(bf16[336,512]{1,0:T(8,128)(2,1)S(1)} %copy-done.16), channel_id=1, source_target_pairs={{0,12},{1,13},{2,14},{3,15},{4,8},{5,9},{6,10},{7,11},{8,4},{9,5},... | collective-permute-start | bytes 1032200 | tf_op jit(solution)/shard_map/ppermute | solution.py:151
  39.0 70.1 %collective-permute-start.22 = (bf16[336,512]{1,0:T(8,128)(2,1)S(1)}, bf16[336,512]{1,0:T(8,128)(2,1)}, u32[]{:S(2)}, u32[]{:S(2)}) collective-permute-start(bf16[336,512]{1,0:T(8,128)(2,1)S(1)} %copy-done.15), channel_id=1, source_target_pairs={{0,14},{1,15},{2,12},{3,13},{4,10},{5,11},{6,8},{7,9},{8,6},{9,7},... | collective-permute-start | bytes 1032200 | tf_op jit(solution)/shard_map/ppermute | solution.py:151
  89.7 48.1 %collective-permute-start.4 = (bf16[256,2688]{1,0:T(8,128)(2,1)}, bf16[256,2688]{1,0:T(8,128)(2,1)}, u32[]{:S(2)}, u32[]{:S(2)}) collective-permute-start(bf16[256,2688]{1,0:T(8,128)(2,1)} %fusion.2.refs_0_), channel_id=1, source_target_pairs={{0,4},{1,5},{2,6},{3,7},{4,0},{5,1},{6,2},{7,3},{8,12},{9,13},{10,... | collective-permute-start | bytes 4128776 | tf_op jit(solution)/shard_map/ppermute | solution.py:151
  96.6 43.2 %collective-permute-start.2 = (bf16[256,2688]{1,0:T(8,128)(2,1)}, bf16[256,2688]{1,0:T(8,128)(2,1)}, u32[]{:S(2)}, u32[]{:S(2)}) collective-permute-start(bf16[256,2688]{1,0:T(8,128)(2,1)} %fusion.2.refs_0_), channel_id=1, source_target_pairs={{0,2},{1,3},{2,0},{3,1},{4,6},{5,7},{6,4},{7,5},{8,10},{9,11},{10,... | collective-permute-start | bytes 4128776 | tf_op jit(solution)/shard_map/ppermute | solution.py:151
  106.0 33.7 %collective-permute-start.1 = (bf16[256,2688]{1,0:T(8,128)(2,1)}, bf16[256,2688]{1,0:T(8,128)(2,1)}, u32[]{:S(2)}, u32[]{:S(2)}) collective-permute-start(bf16[256,2688]{1,0:T(8,128)(2,1)} %fusion.2.refs_0_), channel_id=1, source_target_pairs={{0,1},{1,0},{2,3},{3,2},{4,5},{5,4},{6,7},{7,6},{8,9},{9,8},{10,11... | collective-permute-start | bytes 4128776 | tf_op jit(solution)/shard_map/ppermute | solution.py:151
  107.5 55.0 %collective-permute-start.12 = (bf16[256,2688]{1,0:T(8,128)(2,1)}, bf16[256,2688]{1,0:T(8,128)(2,1)}, u32[]{:S(2)}, u32[]{:S(2)}) collective-permute-start(bf16[256,2688]{1,0:T(8,128)(2,1)} %collective-permute-done.8.refs_8_), channel_id=1, source_target_pairs={{0,4},{1,5},{2,6},{3,7},{4,0},{5,1},{6,2},{7,3},{8,12},{9,13},{10,... | collective-permute-start | bytes 4128776 | tf_op jit(solution)/shard_map/ppermute | solution.py:151
  112.0 206.2 %all-gather.11.cloned.1.call-start = ((), (), s32[]{:S(2)}) async-start(), calls=%async_computation.3 | async-start | bytes 1966080 | tf_op jit(solution)/shard_map/all_gather | solution.py:488
  112.1 51.8 %collective-permute-start.10 = (bf16[256,2688]{1,0:T(8,128)(2,1)}, bf16[256,2688]{1,0:T(8,128)(2,1)}, u32[]{:S(2)}, u32[]{:S(2)}) collective-permute-start(bf16[256,2688]{1,0:T(8,128)(2,1)} %collective-permute-done.8.refs_8_), channel_id=1, source_target_pairs={{0,2},{1,3},{2,0},{3,1},{4,6},{5,7},{6,4},{7,5},{8,10},{9,11},{10,... | collective-permute-start | bytes 4128776 | tf_op jit(solution)/shard_map/ppermute | solution.py:151
  137.9 33.3 %collective-permute-start.9 = (bf16[256,2688]{1,0:T(8,128)(2,1)}, bf16[256,2688]{1,0:T(8,128)(2,1)S(1)}, u32[]{:S(2)}, u32[]{:S(2)}) collective-permute-start(bf16[256,2688]{1,0:T(8,128)(2,1)} %collective-permute-done.8.refs_8_), channel_id=1, source_target_pairs={{0,1},{1,0},{2,3},{3,2},{4,5},{5,4},{6,7},{7,6},{8,9},{9,8},{10,11... | collective-permute-start | bytes 4128776 | tf_op jit(solution)/shard_map/ppermute | solution.py:151
  139.7 31.4 %collective-permute-start.6 = (bf16[256,2688]{1,0:T(8,128)(2,1)}, bf16[256,2688]{1,0:T(8,128)(2,1)S(1)}, u32[]{:S(2)}, u32[]{:S(2)}) collective-permute-start(bf16[256,2688]{1,0:T(8,128)(2,1)} %collective-permute-done.4.refs_4_), channel_id=1, source_target_pairs={{0,2},{1,3},{2,0},{3,1},{4,6},{5,7},{6,4},{7,5},{8,10},{9,11},{10,... | collective-permute-start | bytes 4128776 | tf_op jit(solution)/shard_map/ppermute | solution.py:151
  139.8 61.0 %collective-permute-start.5 = (bf16[256,2688]{1,0:T(8,128)(2,1)}, bf16[256,2688]{1,0:T(8,128)(2,1)}, u32[]{:S(2)}, u32[]{:S(2)}) collective-permute-start(bf16[256,2688]{1,0:T(8,128)(2,1)} %collective-permute-done.4.refs_4_), channel_id=1, source_target_pairs={{0,1},{1,0},{2,3},{3,2},{4,5},{5,4},{6,7},{7,6},{8,9},{9,8},{10,11... | collective-permute-start | bytes 4128776 | tf_op jit(solution)/shard_map/ppermute | solution.py:151
  162.5 59.9 %collective-permute-start.13 = (bf16[256,2688]{1,0:T(8,128)(2,1)}, bf16[256,2688]{1,0:T(8,128)(2,1)}, u32[]{:S(2)}, u32[]{:S(2)}) collective-permute-start(bf16[256,2688]{1,0:T(8,128)(2,1)} %collective-permute-done.12.refs_12_), channel_id=1, source_target_pairs={{0,1},{1,0},{2,3},{3,2},{4,5},{5,4},{6,7},{7,6},{8,9},{9,8},{10,11... | collective-permute-start | bytes 4128776 | tf_op jit(solution)/shard_map/ppermute | solution.py:151
  163.9 62.9 %collective-permute-start.3 = (bf16[256,2688]{1,0:T(8,128)(2,1)}, bf16[256,2688]{1,0:T(8,128)(2,1)}, u32[]{:S(2)}, u32[]{:S(2)}) collective-permute-start(bf16[256,2688]{1,0:T(8,128)(2,1)} %collective-permute-done.1.refs_1_), channel_id=1, source_target_pairs={{0,2},{1,3},{2,0},{3,1},{4,6},{5,7},{6,4},{7,5},{8,10},{9,11},{10,... | collective-permute-start | bytes 4128776 | tf_op jit(solution)/shard_map/ppermute | solution.py:151
  171.1 113.0 %collective-permute-start.14 = (bf16[256,2688]{1,0:T(8,128)(2,1)}, bf16[256,2688]{1,0:T(8,128)(2,1)}, u32[]{:S(2)}, u32[]{:S(2)}) collective-permute-start(bf16[256,2688]{1,0:T(8,128)(2,1)} %collective-permute-done.12.refs_12_), channel_id=1, source_target_pairs={{0,2},{1,3},{2,0},{3,1},{4,6},{5,7},{6,4},{7,5},{8,10},{9,11},{10,... | collective-permute-start | bytes 4128776 | tf_op jit(solution)/shard_map/ppermute | solution.py:151
  171.1 113.0 %collective-permute-start.11 = (bf16[256,2688]{1,0:T(8,128)(2,1)S(1)}, bf16[256,2688]{1,0:T(8,128)(2,1)}, u32[]{:S(2)}, u32[]{:S(2)}) collective-permute-start(bf16[256,2688]{1,0:T(8,128)(2,1)S(1)} %collective-permute-done.9.refs_9_), channel_id=1, source_target_pairs={{0,2},{1,3},{2,0},{3,1},{4,6},{5,7},{6,4},{7,5},{8,10},{9,11},{10,... | collective-permute-start | bytes 4128776 | tf_op jit(solution)/shard_map/ppermute | solution.py:151
  200.7 83.4 %collective-permute-start.7 = (bf16[256,2688]{1,0:T(8,128)(2,1)}, bf16[256,2688]{1,0:T(8,128)(2,1)}, u32[]{:S(2)}, u32[]{:S(2)}) collective-permute-start(bf16[256,2688]{1,0:T(8,128)(2,1)} %collective-permute-done.5.refs_5_), channel_id=1, source_target_pairs={{0,2},{1,3},{2,0},{3,1},{4,6},{5,7},{6,4},{7,5},{8,10},{9,11},{10,... | collective-permute-start | bytes 4128776 | tf_op jit(solution)/shard_map/ppermute | solution.py:151
  222.4 61.8 %collective-permute-start.15 = (bf16[256,2688]{1,0:T(8,128)(2,1)}, bf16[256,2688]{1,0:T(8,128)(2,1)}, u32[]{:S(2)}, u32[]{:S(2)}) collective-permute-start(bf16[256,2688]{1,0:T(8,128)(2,1)} %collective-permute-done.13.refs_13_), channel_id=1, source_target_pairs={{0,2},{1,3},{2,0},{3,1},{4,6},{5,7},{6,4},{7,5},{8,10},{9,11},{10,... | collective-permute-start | bytes 4128776 | tf_op jit(solution)/shard_map/ppermute | solution.py:151
  224.5 111.7 %all-gather.13.cloned.1.call-start = ((), (), s32[]{:S(2)}) async-start(), calls=%async_computation.4 | async-start | bytes 2162688 | tf_op jit(solution)/shard_map/all_gather | solution.py:488
  226.8 7.0 %collective-permute-start.29 = (bf16[336,256]{1,0:T(8,128)(2,1)S(1)}, bf16[336,256]{1,0:T(8,128)(2,1)S(1)}, u32[]{:S(2)}, u32[]{:S(2)}) collective-permute-start(bf16[336,256]{1,0:T(8,128)(2,1)S(1)} %get-tuple-element.47), channel_id=1, source_target_pairs={{0,14},{1,15},{2,12},{3,13},{4,10},{5,11},{6,8},{7,9},{8,6},{9,7},... | collective-permute-start | bytes 516104 | tf_op jit(solution)/shard_map/ppermute | solution.py:151
  233.8 9.8 %collective-permute-start.28 = (bf16[336,256]{1,0:T(8,128)(2,1)S(1)}, bf16[336,256]{1,0:T(8,128)(2,1)S(1)}, u32[]{:S(2)}, u32[]{:S(2)}) collective-permute-start(bf16[336,256]{1,0:T(8,128)(2,1)S(1)} %get-tuple-element.48), channel_id=1, source_target_pairs={{0,12},{1,13},{2,14},{3,15},{4,8},{5,9},{6,10},{7,11},{8,4},{9,5},... | collective-permute-start | bytes 516104 | tf_op jit(solution)/shard_map/ppermute | solution.py:151
  243.6 10.7 %collective-permute-start.27 = (bf16[336,256]{1,0:T(8,128)(2,1)S(1)}, bf16[336,256]{1,0:T(8,128)(2,1)S(1)}, u32[]{:S(2)}, u32[]{:S(2)}) collective-permute-start(bf16[336,256]{1,0:T(8,128)(2,1)S(1)} %get-tuple-element.49), channel_id=1, source_target_pairs={{0,10},{1,11},{2,8},{3,9},{4,14},{5,15},{6,12},{7,13},{8,2},{9,3},... | collective-permute-start | bytes 516104 | tf_op jit(solution)/shard_map/ppermute | solution.py:151
  254.3 13.1 %collective-permute-start.26 = (bf16[336,256]{1,0:T(8,128)(2,1)S(1)}, bf16[336,256]{1,0:T(8,128)(2,1)S(1)}, u32[]{:S(2)}, u32[]{:S(2)}) collective-permute-start(bf16[336,256]{1,0:T(8,128)(2,1)S(1)} %get-tuple-element.50), channel_id=1, source_target_pairs={{0,8},{1,9},{2,10},{3,11},{4,12},{5,13},{6,14},{7,15},{8,0},{9,1},... | collective-permute-start | bytes 516104 | tf_op jit(solution)/shard_map/ppermute | solution.py:151
  282.6 78.9 %collective-permute-start.47 = (bf16[336,2048]{1,0:T(8,128)(2,1)}, bf16[336,2048]{1,0:T(8,128)(2,1)}, u32[]{:S(2)}, u32[]{:S(2)}) collective-permute-start(bf16[336,2048]{1,0:T(8,128)(2,1)} %bitcast.8.refs_16_), channel_id=1, source_target_pairs={{0,1},{1,0},{2,3},{3,2},{4,5},{5,4},{6,7},{7,6},{8,9},{9,8},{10,11... | collective-permute-start | bytes 4128776 | tf_op jit(solution)/shard_map/ppermute | solution.py:151
  311.9 17.7 %collective-permute-start.38 = (bf16[4,256,256]{2,1,0:T(8,128)(2,1)}, bf16[4,256,256]{2,1,0:T(8,128)(2,1)}, u32[]{:S(2)}, u32[]{:S(2)}) collective-permute-start(bf16[4,256,256]{2,1,0:T(8,128)(2,1)} %get-tuple-element.43), channel_id=1, source_target_pairs={{0,16},{1,17},{2,18},{3,19},{4,20},{5,21},{6,22},{7,23},{8,24},{9,... | collective-permute-start | bytes 1572872 | tf_op jit(solution)/shard_map/ppermute | solution.py:481
  320.2 41.3 %collective-permute-start.48 = (bf16[160,2048]{1,0:T(8,128)(2,1)}, bf16[160,2048]{1,0:T(8,128)(2,1)}, u32[]{:S(2)}, u32[]{:S(2)}) collective-permute-start(bf16[160,2048]{1,0:T(8,128)(2,1)} %dynamic-slice_bitcast_fusion.1.refs_18_), channel_id=1, source_target_pairs={{0,1},{1,0},{2,3},{3,2},{4,5},{5,4},{6,7},{7,6},{8,9},{9,8},{10,11... | collective-permute-start | bytes 1966088 | tf_op jit(solution)/shard_map/ppermute | solution.py:151
  328.1 15.7 %collective-permute-start.30 = (bf16[4,128,256]{2,1,0:T(8,128)(2,1)}, bf16[4,128,256]{2,1,0:T(8,128)(2,1)}, u32[]{:S(2)}, u32[]{:S(2)}) collective-permute-start(bf16[4,128,256]{2,1,0:T(8,128)(2,1)} %get-tuple-element.42), channel_id=1, source_target_pairs={{0,1},{1,0},{2,3},{3,2},{4,5},{5,4},{6,7},{7,6},{8,9},{9,8},{10,11... | collective-permute-start | bytes 786440 | tf_op jit(solution)/shard_map/ppermute | solution.py:151
  335.7 22.3 %collective-permute-start.39 = (bf16[4,128,256]{2,1,0:T(8,128)(2,1)}, bf16[4,128,256]{2,1,0:T(8,128)(2,1)}, u32[]{:S(2)}, u32[]{:S(2)}) collective-permute-start(bf16[4,128,256]{2,1,0:T(8,128)(2,1)} %get-tuple-element.45), channel_id=1, source_target_pairs={{0,1},{1,0},{2,3},{3,2},{4,5},{5,4},{6,7},{7,6},{8,9},{9,8},{10,11... | collective-permute-start | bytes 786440 | tf_op jit(solution)/shard_map/ppermute | solution.py:151
  338.2 34.5 %collective-permute-start.49 = (bf16[176,2048]{1,0:T(8,128)(2,1)}, bf16[176,2048]{1,0:T(8,128)(2,1)}, u32[]{:S(2)}, u32[]{:S(2)}) collective-permute-start(bf16[176,2048]{1,0:T(8,128)(2,1)} %dynamic-slice_bitcast_fusion.refs_20_), channel_id=1, source_target_pairs={{0,1},{1,0},{2,3},{3,2},{4,5},{5,4},{6,7},{7,6},{8,9},{9,8},{10,11... | collective-permute-start | bytes 2162696 | tf_op jit(solution)/shard_map/ppermute | solution.py:151
  345.6 25.4 %collective-permute-start.34 = (bf16[2,4,128,256]{3,2,1,0:T(8,128)(2,1)}, bf16[2,4,128,256]{3,2,1,0:T(8,128)(2,1)}, u32[]{:S(2)}, u32[]{:S(2)}) collective-permute-start(bf16[2,4,128,256]{3,2,1,0:T(8,128)(2,1)} %shard_map.95.refs_0_), channel_id=1, source_target_pairs={{0,8},{1,9},{2,10},{3,11},{4,12},{5,13},{6,14},{7,15},{8,0},{9,1},... | collective-permute-start | bytes 1572872 | tf_op jit(solution)/shard_map/ppermute | solution.py:151
  358.0 14.8 %collective-permute-start.32 = (bf16[2,4,128,256]{3,2,1,0:T(8,128)(2,1)}, bf16[2,4,128,256]{3,2,1,0:T(8,128)(2,1)}, u32[]{:S(2)}, u32[]{:S(2)}) collective-permute-start(bf16[2,4,128,256]{3,2,1,0:T(8,128)(2,1)} %shard_map.95.refs_0_), channel_id=1, source_target_pairs={{0,4},{1,5},{2,6},{3,7},{4,0},{5,1},{6,2},{7,3},{8,12},{9,13},{10,... | collective-permute-start | bytes 1572872 | tf_op jit(solution)/shard_map/ppermute | solution.py:151
  361.5 11.7 %collective-permute-start.31 = (bf16[2,4,128,256]{3,2,1,0:T(8,128)(2,1)}, bf16[2,4,128,256]{3,2,1,0:T(8,128)(2,1)}, u32[]{:S(2)}, u32[]{:S(2)}) collective-permute-start(bf16[2,4,128,256]{3,2,1,0:T(8,128)(2,1)} %shard_map.95.refs_0_), channel_id=1, source_target_pairs={{0,2},{1,3},{2,0},{3,1},{4,6},{5,7},{6,4},{7,5},{8,10},{9,11},{10,... | collective-permute-start | bytes 1572872 | tf_op jit(solution)/shard_map/ppermute | solution.py:151
  361.5 19.5 %collective-permute-start.43 = (bf16[2,4,128,256]{3,2,1,0:T(8,128)(2,1)}, bf16[2,4,128,256]{3,2,1,0:T(8,128)(2,1)S(1)}, u32[]{:S(2)}, u32[]{:S(2)}) collective-permute-start(bf16[2,4,128,256]{3,2,1,0:T(8,128)(2,1)} %shard_map.97.refs_8_), channel_id=1, source_target_pairs={{0,8},{1,9},{2,10},{3,11},{4,12},{5,13},{6,14},{7,15},{8,0},{9,1},... | collective-permute-start | bytes 1572872 | tf_op jit(solution)/shard_map/ppermute | solution.py:151
  371.1 15.0 %collective-permute-start.36 = (bf16[2,4,128,256]{3,2,1,0:T(8,128)(2,1)}, bf16[2,4,128,256]{3,2,1,0:T(8,128)(2,1)S(1)}, u32[]{:S(2)}, u32[]{:S(2)}) collective-permute-start(bf16[2,4,128,256]{3,2,1,0:T(8,128)(2,1)} %collective-permute-done.34.refs_4_), channel_id=1, source_target_pairs={{0,4},{1,5},{2,6},{3,7},{4,0},{5,1},{6,2},{7,3},{8,12},{9,13},{10,... | collective-permute-start | bytes 1572872 | tf_op jit(solution)/shard_map/ppermute | solution.py:151
  372.8 13.3 %collective-permute-start.35 = (bf16[2,4,128,256]{3,2,1,0:T(8,128)(2,1)}, bf16[2,4,128,256]{3,2,1,0:T(8,128)(2,1)S(1)}, u32[]{:S(2)}, u32[]{:S(2)}) collective-permute-start(bf16[2,4,128,256]{3,2,1,0:T(8,128)(2,1)} %collective-permute-done.34.refs_4_), channel_id=1, source_target_pairs={{0,2},{1,3},{2,0},{3,1},{4,6},{5,7},{6,4},{7,5},{8,10},{9,11},{10,... | collective-permute-start | bytes 1572872 | tf_op jit(solution)/shard_map/ppermute | solution.py:151
  372.8 13.9 %collective-permute-start.33 = (bf16[2,4,128,256]{3,2,1,0:T(8,128)(2,1)}, bf16[2,4,128,256]{3,2,1,0:T(8,128)(2,1)S(1)}, u32[]{:S(2)}, u32[]{:S(2)}) collective-permute-start(bf16[2,4,128,256]{3,2,1,0:T(8,128)(2,1)} %collective-permute-done.32.refs_2_), channel_id=1, source_target_pairs={{0,2},{1,3},{2,0},{3,1},{4,6},{5,7},{6,4},{7,5},{8,10},{9,11},{10,... | collective-permute-start | bytes 1572872 | tf_op jit(solution)/shard_map/ppermute | solution.py:151
  373.3 24.0 %collective-permute-start.41 = (bf16[2,4,128,256]{3,2,1,0:T(8,128)(2,1)}, bf16[2,4,128,256]{3,2,1,0:T(8,128)(2,1)S(1)}, u32[]{:S(2)}, u32[]{:S(2)}) collective-permute-start(bf16[2,4,128,256]{3,2,1,0:T(8,128)(2,1)} %shard_map.97.refs_8_), channel_id=1, source_target_pairs={{0,4},{1,5},{2,6},{3,7},{4,0},{5,1},{6,2},{7,3},{8,12},{9,13},{10,... | collective-permute-start | bytes 1572872 | tf_op jit(solution)/shard_map/ppermute | solution.py:151
  381.0 24.3 %collective-permute-start.45 = (bf16[2,4,128,256]{3,2,1,0:T(8,128)(2,1)S(1)}, bf16[2,4,128,256]{3,2,1,0:T(8,128)(2,1)S(1)}, u32[]{:S(2)}, u32[]{:S(2)}) collective-permute-start(bf16[2,4,128,256]{3,2,1,0:T(8,128)(2,1)S(1)} %collective-permute-done.43.refs_12_), channel_id=1, source_target_pairs={{0,4},{1,5},{2,6},{3,7},{4,0},{5,1},{6,2},{7,3},{8,12},{9,13},{10,... | collective-permute-start | bytes 1572872 | tf_op jit(solution)/shard_map/ppermute | solution.py:151
  386.1 19.2 %collective-permute-start.40 = (bf16[2,4,128,256]{3,2,1,0:T(8,128)(2,1)}, bf16[2,4,128,256]{3,2,1,0:T(8,128)(2,1)S(1)}, u32[]{:S(2)}, u32[]{:S(2)}) collective-permute-start(bf16[2,4,128,256]{3,2,1,0:T(8,128)(2,1)} %shard_map.97.refs_8_), channel_id=1, source_target_pairs={{0,2},{1,3},{2,0},{3,1},{4,6},{5,7},{6,4},{7,5},{8,10},{9,11},{10,... | collective-permute-start | bytes 1572872 | tf_op jit(solution)/shard_map/ppermute | solution.py:151
  386.1 19.2 %collective-permute-start.44 = (bf16[2,4,128,256]{3,2,1,0:T(8,128)(2,1)S(1)}, bf16[2,4,128,256]{3,2,1,0:T(8,128)(2,1)S(1)}, u32[]{:S(2)}, u32[]{:S(2)}) collective-permute-start(bf16[2,4,128,256]{3,2,1,0:T(8,128)(2,1)S(1)} %collective-permute-done.43.refs_12_), channel_id=1, source_target_pairs={{0,2},{1,3},{2,0},{3,1},{4,6},{5,7},{6,4},{7,5},{8,10},{9,11},{10,... | collective-permute-start | bytes 1572872 | tf_op jit(solution)/shard_map/ppermute | solution.py:151
  386.7 18.6 %collective-permute-start.37 = (bf16[2,4,128,256]{3,2,1,0:T(8,128)(2,1)S(1)}, bf16[2,4,128,256]{3,2,1,0:T(8,128)(2,1)S(1)}, u32[]{:S(2)}, u32[]{:S(2)}) collective-permute-start(bf16[2,4,128,256]{3,2,1,0:T(8,128)(2,1)S(1)} %collective-permute-done.36.refs_6_), channel_id=1, source_target_pairs={{0,2},{1,3},{2,0},{3,1},{4,6},{5,7},{6,4},{7,5},{8,10},{9,11},{10,... | collective-permute-start | bytes 1572872 | tf_op jit(solution)/shard_map/ppermute | solution.py:151
  397.3 8.0 %collective-permute-start.42 = (bf16[2,4,128,256]{3,2,1,0:T(8,128)(2,1)S(1)}, bf16[2,4,128,256]{3,2,1,0:T(8,128)(2,1)S(1)}, u32[]{:S(2)}, u32[]{:S(2)}) collective-permute-start(bf16[2,4,128,256]{3,2,1,0:T(8,128)(2,1)S(1)} %collective-permute-done.41.refs_10_), channel_id=1, source_target_pairs={{0,2},{1,3},{2,0},{3,1},{4,6},{5,7},{6,4},{7,5},{8,10},{9,11},{10,... | collective-permute-start | bytes 1572872 | tf_op jit(solution)/shard_map/ppermute | solution.py:151
  (35 other events, 481.3 us)
Sparse Core Ops, SparseCore 0:
  11.8 72.6 all-gather.6
  112.2 72.6 all-gather.8
  224.6 39.5 all-gather.10
  282.7 42.4 all-gather.12

commit v2 on v1

--- a/solution.py
+++ b/solution.py
@@ -165,7 +165,7 @@
     )
 
 
-def cut_kernel(n, meta, wq, wk, wv, kv_out, *outs):
+def cut_kernel(n, meta, wq, wk, wv, kv_out, *q_outs):
     place = meta[0]
     wide_q = wq.shape[1] // n
     for p in range(n):
@@ -173,17 +173,14 @@
         kv_out[:, p * 2 * HD + HD : (p + 1) * 2 * HD] = wv[:, p * HD : (p + 1) * HD]
     for m in range(n):
         at = lax.bitwise_xor(place, m)
-        cols = pl.ds(pl.multiple_of(at * HD, HD), HD)
-        outs[m][:, :HD] = wk[:, cols]
-        outs[m][:, HD : 2 * HD] = wv[:, cols]
-        outs[m][:, 2 * HD :] = wq[:, pl.ds(pl.multiple_of(at * wide_q, 128), wide_q)]
+        q_outs[m][...] = wq[:, pl.ds(pl.multiple_of(at * wide_q, 128), wide_q)]
 
 
 def join_kernel(*refs):
     out = refs[-1]
     deep = refs[0].shape[0]
     for m, piece in enumerate(refs[:-1]):
-        out[m * deep : (m + 1) * deep] = piece[:, 2 * HD :]
+        out[m * deep : (m + 1) * deep] = piece[...]
 
 
 def pair_kernel(first, second, out):
@@ -197,26 +194,31 @@
 
 
 def project_kernel(n, reach, heads, meta, cosine, sine, key_gain, query_gain, *refs):
-    blocks, near, far = refs[: 2 * n], refs[2 * n : 3 * n], refs[3 * n : 4 * n]
-    q_far = refs[4 * n]
-    kv_out, tail_out, q_out = refs[4 * n + 1 : 4 * n + 4]
-    block_mem, weight_mem, block_sem, weight_sem = refs[4 * n + 4 :]
-    place, half, col = meta[0], meta[1], meta[2]
-    other = lax.bitwise_xor(half, 1)
+    blocks, kv_parts = refs[: 2 * n], refs[2 * n : 3 * n]
+    q_rows = refs[3 * n]
+    kv_out, tail_out, q_out = refs[3 * n + 1 : 3 * n + 4]
+    block_mem, weight_mem, block_sem, weight_sem = refs[3 * n + 4 :]
+    place, col = meta[0], meta[2]
     _, _, tokens, features = block_mem.shape
-    deep = near[0].shape[0]
+    deep = kv_parts[0].shape[0] // 2
     copies = []
     for m in range(n):
         rows = pl.ds(pl.multiple_of(lax.bitwise_xor(place, m) * deep, 16), deep)
-        source = pl.ds(pl.multiple_of((other * n + m) * deep, 16), deep)
-        for k, (start, target) in enumerate(
-            [
-                (near[m], weight_mem.at[half, rows, :]),
-                (far[m], weight_mem.at[other, rows, pl.ds(0, 2 * HD)]),
-                (q_far.at[source, :], weight_mem.at[other, rows, pl.ds(2 * HD, heads * HD)]),
-            ]
-        ):
-            copies.append(pltpu.make_async_copy(start, target, weight_sem.at[3 * m + k]))
+        for half in range(2):
+            for k, (source, target) in enumerate(
+                [
+                    (
+                        kv_parts[m].at[pl.ds(half * deep, deep)],
+                        weight_mem.at[half, rows, pl.ds(0, 2 * HD)],
+                    ),
+                    (
+                        q_rows.at[pl.ds((half * n + m) * deep, deep)],
+                        weight_mem.at[half, rows, pl.ds(2 * HD, heads * HD)],
+                    ),
+                ]
+            ):
+                sem = weight_sem.at[4 * m + 2 * half + k]
+                copies.append(pltpu.make_async_copy(source, target, sem))
     for copy in copies:
         copy.start()
     for m in range(n):
@@ -388,12 +390,12 @@
     deep = query_weight.shape[0]
     kv_cut, *cut = run(
         functools.partial(cut_kernel, n),
-        [shaped((deep, n * 2 * HD), bf16)] + [shaped((deep, (2 + heads) * HD), bf16)] * n,
+        [shaped((deep, n * 2 * HD), bf16)] + [shaped((deep, heads * HD), bf16)] * n,
         [SMEM, VMEM, VMEM, VMEM],
         [VMEM] * (n + 1),
         [],
         0,
-        5 * query_weight.size * 2,
+        4 * query_weight.size * 2,
     )(meta, query_weight, key_weight, value_weight)
     kv_rows = lax.all_gather(kv_cut, "half", axis=0, tiled=True)
 
@@ -439,15 +441,15 @@
         VMEM,
         [],
         0,
-        6 * n * deep * heads * HD,
+        4 * n * deep * heads * HD,
     )(*near)
     q_rows = lax.all_gather(q_own, "half", axis=0, tiled=True)
     kv_rows, cosine, sine, q_doc = lax.optimization_barrier((kv_rows, cosine, sine, q_doc))
-    far = []
+    kv_parts = []
     for m in range(n):
         first = lax.bitwise_xor(place, m) * 2 * HD
-        piece = lax.dynamic_slice(kv_rows, ((1 - half) * deep, first), (deep, 2 * HD))
-        far.append(piece if m == 0 else swapped(piece, m, 0))
+        piece = lax.dynamic_slice_in_dim(kv_rows, first, 2 * HD, 1)
+        kv_parts.append(piece if m == 0 else swapped(piece, m, 0))
 
     flops = 2 * n * tokens * 2 * features * (2 + heads) * HD
     kv_own, kv_tail, queries = run(
@@ -457,13 +459,13 @@
             shaped((reach, tokens, 2 * HD), bf16),
             shaped((n, heads * tokens, HD), bf16),
         ],
-        [SMEM, VMEM, VMEM, VMEM, VMEM] + [ANY] * (4 * n + 1),
+        [SMEM, VMEM, VMEM, VMEM, VMEM] + [ANY] * (3 * n + 1),
         [VMEM, VMEM, VMEM],
         [
             pltpu.VMEM((2, n, tokens, features), bf16),
             pltpu.VMEM((2, features, (2 + heads) * HD), bf16),
             pltpu.SemaphoreType.DMA((n, 2)),
-            pltpu.SemaphoreType.DMA((3 * n,)),
+            pltpu.SemaphoreType.DMA((4 * n,)),
         ],
         flops,
         2 * n * tokens * features * 2,
@@ -474,8 +476,7 @@
         key_gain.reshape(1, HD),
         query_gain.reshape(1, HD),
         *block_list,
-        *near,
-        *far,
+        *kv_parts,
         q_rows,
     )
     kv_back = lax.ppermute(kv_tail, "half", [(0, 1)])

time: 462 us -> 428 us (0.926)
  waiting for transfers between devices: 260 us -> 225 us
  blocking collectives: 24.4 us -> 29.1 us
    ppermute x49, waiting for transfers between devices: 259 us -> 225 us  [swapped(): return lax.ppermute(value, ('place', 'cols'), pairs)]
    all_to_all x1, blocking collectives: 24.4 us -> 29.1 us  [split_body(): arrived = lax.all_to_all(result, ('place', 'cols'), 0, 0, tiled=True)]
  transfers between devices with their start and end apart: 54 -> 54, of which waited for: 24 -> 25; matrix products, arithmetic and copies ran while one was open for 4% -> 5% of each run, Pallas kernels for 10% -> 11%
where the time goes in v2:
time: 428 us; the launch traced here: 427 us
  waiting for transfers between devices  225 us (53%)
  Pallas kernels  69.5 us (16%)
  starting transfers between devices  62.5 us (15%)
  blocking collectives  29.1 us (7%)
  local copies, waits for them, and re-layouts  19.6 us (5%)
  between operations  13.5 us (3%)
  other arithmetic  8.16 us (2%)
    ppermute x49, waiting for transfers between devices, swapped(): return lax.ppermute(value, ('place', 'cols'), pairs)  225 us
    ppermute x49, starting transfers between devices, swapped(): return lax.ppermute(value, ('place', 'cols'), pairs)  56.5 us
    all_to_all x1, blocking collectives, split_body(): arrived = lax.all_to_all(result, ('place', 'cols'), 0, 0, tiled=True)  29.1 us
    pallas_call x1, Pallas kernels, split_body(): run(functools.partial(project_kernel, n, reach, heads), [shaped((n, token...  27.7 us
    pallas_call x1, Pallas kernels, split_body(): run(functools.partial(output_kernel, n, spans), shaped((2 * n, part, out_...  16.3 us
    pallas_call x2, Pallas kernels, split_body(): run(functools.partial(attend_kernel, low, count, reach, heads), [shape, s...  12.1 us
  transfers between devices with their start and end apart: 54, of which 25 were waited for; matrix products, arithmetic and copies ran while one was open for 5% of the time, Pallas kernels for 11%

profile of v2, /device:TPU:0, one launch (start us, length us, event | category | flops | bytes accessed | tf_op | source)
XLA Modules:
  0.0 427.0 jit_solution(4411551348086906957)
XLA Ops:
  7.2 3.7 shard_map.91
  12.6 3.0 collective-permute-start
  18.7 2.1 collective-permute-start.8
  24.4 3.8 collective-permute-done.24.refs_2_
  32.4 52.9 %collective-permute-done.26.refs_4_ = bf16[336,256]{1,0:T(8,128)(2,1)} collective-permute-done((bf16[336,256]{1,0:T(8,128)(2,1)S(1)}, bf16[336,256]{1,0:T(8,128)(2,1)}, u32[]{:S(2)}, u32[]{:S(2)}) %collective-permute-start.26) | collective-permute-done | bytes 172064 | tf_op jit(solution)/shard_map/ppermute | solution.py:151
  85.3 1.9 collective-permute-start.1
  88.7 3.1 collective-permute-done.28.refs_6_
  92.2 6.5 %collective-permute-done.29.refs_7_ = bf16[336,256]{1,0:T(8,128)(2,1)} collective-permute-done((bf16[336,256]{1,0:T(8,128)(2,1)S(1)}, bf16[336,256]{1,0:T(8,128)(2,1)}, u32[]{:S(2)}, u32[]{:S(2)}) %collective-permute-start.29) | collective-permute-done | bytes 172064 | tf_op jit(solution)/shard_map/ppermute | solution.py:151
  100.3 2.6 shard_map.92
  103.6 15.1 %collective-permute-done.1.refs_1_ = bf16[256,2688]{1,0:T(8,128)(2,1)} collective-permute-done((bf16[256,2688]{1,0:T(8,128)(2,1)}, bf16[256,2688]{1,0:T(8,128)(2,1)}, u32[]{:S(2)}, u32[]{:S(2)}) %collective-permute-start.1) | collective-permute-done | bytes 1376288 | tf_op jit(solution)/shard_map/ppermute | solution.py:151
  119.2 8.9 %collective-permute-done.12.refs_12_ = bf16[256,2688]{1,0:T(8,128)(2,1)} collective-permute-done((bf16[256,2688]{1,0:T(8,128)(2,1)}, bf16[256,2688]{1,0:T(8,128)(2,1)}, u32[]{:S(2)}, u32[]{:S(2)}) %collective-permute-start.12) | collective-permute-done | bytes 1376288 | tf_op jit(solution)/shard_map/ppermute | solution.py:151
  128.3 19.9 %collective-permute-done.9.refs_9_ = bf16[256,2688]{1,0:T(8,128)(2,1)} collective-permute-done((bf16[256,2688]{1,0:T(8,128)(2,1)}, bf16[256,2688]{1,0:T(8,128)(2,1)}, u32[]{:S(2)}, u32[]{:S(2)}) %collective-permute-start.9) | collective-permute-done | bytes 1376288 | tf_op jit(solution)/shard_map/ppermute | solution.py:151
  148.2 1.9 collective-permute-start.13
  150.2 3.7 fusion.3
  153.9 1.9 pad_maximum_fusion
  155.9 2.6 constant_dynamic-slice_fusion
  158.5 19.1 %collective-permute-done.5.refs_5_ = bf16[256,2688]{1,0:T(8,128)(2,1)S(1)} collective-permute-done((bf16[256,2688]{1,0:T(8,128)(2,1)}, bf16[256,2688]{1,0:T(8,128)(2,1)S(1)}, u32[]{:S(2)}, u32[]{:S(2)}) %collective-permute-start.5) | collective-permute-done | bytes 1376288 | tf_op jit(solution)/shard_map/ppermute | solution.py:151
  177.6 2.0 collective-permute-start.17
  181.6 7.0 %collective-permute-done.17.refs_18_ = bf16[672,256]{1,0:T(8,128)(2,1)S(1)} collective-permute-done((bf16[672,256]{1,0:T(8,128)(2,1)S(1)}, bf16[672,256]{1,0:T(8,128)(2,1)S(1)}, u32[]{:S(2)}, u32[]{:S(2)}) %collective-permute-start.17) | collective-permute-done | bytes 344096 | tf_op jit(solution)/shard_map/ppermute | solution.py:151
  188.6 6.8 %collective-permute-done.18.refs_19_ = bf16[672,256]{1,0:T(8,128)(2,1)S(1)} collective-permute-done((bf16[672,256]{1,0:T(8,128)(2,1)S(1)}, bf16[672,256]{1,0:T(8,128)(2,1)S(1)}, u32[]{:S(2)}, u32[]{:S(2)}) %collective-permute-start.18) | collective-permute-done | bytes 344096 | tf_op jit(solution)/shard_map/ppermute | solution.py:151
  195.9 4.1 collective-permute-done.13.refs_13_
  200.0 2.0 slice.21
  202.1 2.8 collective-permute-start.20
  204.8 8.4 %collective-permute-done.20.refs_21_ = bf16[672,256]{1,0:T(8,128)(2,1)S(1)} collective-permute-done((bf16[672,256]{1,0:T(8,128)(2,1)S(1)}, bf16[672,256]{1,0:T(8,128)(2,1)S(1)}, u32[]{:S(2)}, u32[]{:S(2)}) %collective-permute-start.20) | collective-permute-done | bytes 344096 | tf_op jit(solution)/shard_map/ppermute | solution.py:151
  215.1 15.7 %collective-permute-done.21.refs_22_ = bf16[672,256]{1,0:T(8,128)(2,1)S(1)} collective-permute-done((bf16[672,256]{1,0:T(8,128)(2,1)S(1)}, bf16[672,256]{1,0:T(8,128)(2,1)S(1)}, u32[]{:S(2)}, u32[]{:S(2)}) %collective-permute-start.21) | collective-permute-done | bytes 344096 | tf_op jit(solution)/shard_map/ppermute | solution.py:151
  230.8 2.9 collective-permute-start.22
  233.7 2.1 slice.22
  235.8 11.4 %collective-permute-done.22.refs_23_ = bf16[672,256]{1,0:T(8,128)(2,1)S(1)} collective-permute-done((bf16[672,256]{1,0:T(8,128)(2,1)S(1)}, bf16[672,256]{1,0:T(8,128)(2,1)S(1)}, u32[]{:S(2)}, u32[]{:S(2)}) %collective-permute-start.22) | collective-permute-done | bytes 344096 | tf_op jit(solution)/shard_map/ppermute | solution.py:151
  248.8 27.7 %shard_map.93 = (bf16[8,256,256]{2,1,0:T(8,128)(2,1)}, bf16[4,256,256]{2,1,0:T(8,128)(2,1)}, bf16[8,512,128]{2,1,0:T(8,128)(2,1)}) custom-call(s32[3]{0:T(128)} %pad_add_fusion.meta, f32[8,256,128]{2,1,0:T(8,128)} %get-tuple-element.28.cosine, f32[8,256,128]{2,1,0:T(8,128)} %get-tuple-element.29.sine, f32[1,128]{1,0:T(1,128)} %bitcast.22, ...), custom_call_target="tpu_custom_call" | custom-call | flops 11274289152 | bytes 22020096 | tf_op jit(solution)/shard_map/pallas_call | solution.py:455
  276.5 5.9 %collective-permute-start.38 = (bf16[4,256,256]{2,1,0:T(8,128)(2,1)}, bf16[4,256,256]{2,1,0:T(8,128)(2,1)}, u32[]{:S(2)}, u32[]{:S(2)}) collective-permute-start(bf16[4,256,256]{2,1,0:T(8,128)(2,1)} %get-tuple-element.43), channel_id=1, source_target_pairs={{0,16},{1,17},{2,18},{3,19},{4,20},{5,21},{6,22},{7,23},{8,24},{9,... | collective-permute-start | bytes 1572872 | tf_op jit(solution)/shard_map/ppermute | solution.py:482
  283.0 2.0 dynamic-slice_bitcast_fusion.1.refs_18_
  287.1 6.0 %shard_map.94 = (bf16[4,128,256]{2,1,0:T(8,128)(2,1)}, bf16[4,128,256]{2,1,0:T(8,128)(2,1)}) custom-call(s32[3]{0:T(128)} %pad_add_fusion.meta, s32[8,256,1]{2,1,0:T(8,128)} %copy.12.q_doc, s32[12,1,256]{2,1,0:T(1,128)} %bitcast.19, bf16[8,512,128]{2,1,0:T(8,128)(2,1)} %get-tuple-element.39.queries, bf16[8,256,256]{2,1,0:T(8,128)(2,1)} %get-tuple-element.40.kv_own), custom_call_target="tpu_custom_call" | custom-call | flops 2684354560 | bytes 2097152 | tf_op jit(solution)/shard_map/pallas_call | solution.py:498
  294.4 6.1 %shard_map.96 = (bf16[4,128,256]{2,1,0:T(8,128)(2,1)}, bf16[4,128,256]{2,1,0:T(8,128)(2,1)}) custom-call(s32[3]{0:T(128)} %pad_add_fusion.meta, s32[8,256,1]{2,1,0:T(8,128)} %copy.12.q_doc, s32[12,1,256]{2,1,0:T(1,128)} %bitcast.20, bf16[8,512,128]{2,1,0:T(8,128)(2,1)} %get-tuple-element.39.queries, bf16[8,256,256]{2,1,0:T(8,128)(2,1)} %get-tuple-element.40.kv_own, ...), custom_call_target="tpu_custom_call" | custom-call | flops 2684354560 | bytes 2097152 | tf_op jit(solution)/shard_map/pallas_call | solution.py:498
  301.2 2.0 dynamic-slice_bitcast_fusion.refs_20_
  304.5 4.0 collective-permute-done.30.second
  310.4 8.8 %collective-permute-start.34 = (bf16[2,4,128,256]{3,2,1,0:T(8,128)(2,1)}, bf16[2,4,128,256]{3,2,1,0:T(8,128)(2,1)}, u32[]{:S(2)}, u32[]{:S(2)}) collective-permute-start(bf16[2,4,128,256]{3,2,1,0:T(8,128)(2,1)} %shard_map.95.refs_0_), channel_id=1, source_target_pairs={{0,8},{1,9},{2,10},{3,11},{4,12},{5,13},{6,14},{7,15},{8,0},{9,1},... | collective-permute-start | bytes 1572872 | tf_op jit(solution)/shard_map/ppermute | solution.py:151
  320.8 1.9 shard_map.97.refs_8_
  322.7 3.6 collective-permute-start.43
  326.4 1.9 collective-permute-done.49.refs_21_
  329.3 2.9 collective-permute-done.34.refs_4_
  332.2 2.0 collective-permute-done.32.refs_2_
  336.0 6.3 %collective-permute-done.43.refs_12_ = bf16[2,4,128,256]{3,2,1,0:T(8,128)(2,1)S(1)} collective-permute-done((bf16[2,4,128,256]{3,2,1,0:T(8,128)(2,1)}, bf16[2,4,128,256]{3,2,1,0:T(8,128)(2,1)S(1)}, u32[]{:S(2)}, u32[]{:S(2)}) %collective-permute-start.43) | collective-permute-done | bytes 524320 | tf_op jit(solution)/shard_map/ppermute | solution.py:151
  346.0 10.7 %collective-permute-done.36.refs_6_ = bf16[2,4,128,256]{3,2,1,0:T(8,128)(2,1)S(1)} collective-permute-done((bf16[2,4,128,256]{3,2,1,0:T(8,128)(2,1)}, bf16[2,4,128,256]{3,2,1,0:T(8,128)(2,1)S(1)}, u32[]{:S(2)}, u32[]{:S(2)}) %collective-permute-start.36) | collective-permute-done | bytes 524320 | tf_op jit(solution)/shard_map/ppermute | solution.py:151
  357.1 9.0 %collective-permute-done.45.refs_14_ = bf16[2,4,128,256]{3,2,1,0:T(8,128)(2,1)S(1)} collective-permute-done((bf16[2,4,128,256]{3,2,1,0:T(8,128)(2,1)S(1)}, bf16[2,4,128,256]{3,2,1,0:T(8,128)(2,1)S(1)}, u32[]{:S(2)}, u32[]{:S(2)}) %collective-permute-start.45) | collective-permute-done | bytes 524320 | tf_op jit(solution)/shard_map/ppermute | solution.py:151
  368.3 16.3 %shard_map.98 = bf16[16,128,336]{2,1,0:T(8,128)(2,1)} custom-call(s32[3]{0:T(128)} %pad_add_fusion.meta, bf16[2,4,128,256]{3,2,1,0:T(8,128)(2,1)} %shard_map.95.refs_0_, bf16[2,4,128,256]{3,2,1,0:T(8,128)(2,1)} %collective-permute-done.31.refs_1_, bf16[2,4,128,256]{3,2,1,0:T(8,128)(2,1)} %collective-permute-done.32.refs_2_, ...), custom_call_target="tpu_custom_call" | custom-call | flops 5637144576 | bytes 11010048 | tf_op jit(solution)/shard_map/pallas_call | solution.py:527
  384.6 1.9 copy.14
  386.5 29.1 %all_to_all.5 = bf16[16,128,336]{1,2,0:T(8,128)(2,1)S(1)} all-to-all(bf16[16,128,336]{1,2,0:T(8,128)(2,1)S(1)} %copy.14), channel_id=1, replica_groups=mesh['groups'=1,'half'=2,'place'=8,'cols'=2,'sub'=1] {'place','cols'}, dimensions={0} | all-to-all | bytes 2752512 | tf_op jit(solution)/shard_map/all_to_all | solution.py:542
  417.1 3.4 shard_map.99
  (150 shorter events, 43.9 us)
Async XLA Ops:
  6.5 149.3 %all-gather.7.cloned.1.call-start = ((), (), s32[]{:S(2)}) async-start(), calls=%async_computation.1 | async-start | bytes 4128768 | tf_op jit(solution)/shard_map/all_gather | solution.py:400
  10.9 237.8 %all-gather.9.cloned.1.call-start = ((), (), s32[]{:S(2)}) async-start(), calls=%async_computation.2 | async-start | bytes 4128768 | tf_op jit(solution)/shard_map/all_gather | solution.py:446
  18.7 73.1 %collective-permute-start.8 = (bf16[256,2688]{1,0:T(8,128)(2,1)}, bf16[256,2688]{1,0:T(8,128)(2,1)}, u32[]{:S(2)}, u32[]{:S(2)}) collective-permute-start(bf16[256,2688]{1,0:T(8,128)(2,1)} %fusion.2.refs_0_), channel_id=1, source_target_pairs={{0,8},{1,9},{2,10},{3,11},{4,12},{5,13},{6,14},{7,15},{8,0},{9,1},... | collective-permute-start | bytes 4128776 | tf_op jit(solution)/shard_map/ppermute | solution.py:151
  22.4 8.4 %collective-permute-start.25 = (bf16[336,256]{1,0:T(8,128)(2,1)S(1)}, bf16[336,256]{1,0:T(8,128)(2,1)}, u32[]{:S(2)}, u32[]{:S(2)}) collective-permute-start(bf16[336,256]{1,0:T(8,128)(2,1)S(1)} %copy-done.24), channel_id=1, source_target_pairs={{0,6},{1,7},{2,4},{3,5},{4,2},{5,3},{6,0},{7,1},{8,14},{9,15},{10,... | collective-permute-start | bytes 516104 | tf_op jit(solution)/shard_map/ppermute | solution.py:151
  22.7 62.7 %collective-permute-start.26 = (bf16[336,256]{1,0:T(8,128)(2,1)S(1)}, bf16[336,256]{1,0:T(8,128)(2,1)}, u32[]{:S(2)}, u32[]{:S(2)}) collective-permute-start(bf16[336,256]{1,0:T(8,128)(2,1)S(1)} %copy-done.23), channel_id=1, source_target_pairs={{0,8},{1,9},{2,10},{3,11},{4,12},{5,13},{6,14},{7,15},{8,0},{9,1},... | collective-permute-start | bytes 516104 | tf_op jit(solution)/shard_map/ppermute | solution.py:151
  23.0 65.0 %collective-permute-start.27 = (bf16[336,256]{1,0:T(8,128)(2,1)S(1)}, bf16[336,256]{1,0:T(8,128)(2,1)}, u32[]{:S(2)}, u32[]{:S(2)}) collective-permute-start(bf16[336,256]{1,0:T(8,128)(2,1)S(1)} %copy-done.22), channel_id=1, source_target_pairs={{0,10},{1,11},{2,8},{3,9},{4,14},{5,15},{6,12},{7,13},{8,2},{9,3},... | collective-permute-start | bytes 516104 | tf_op jit(solution)/shard_map/ppermute | solution.py:151
  28.2 63.6 %collective-permute-start.28 = (bf16[336,256]{1,0:T(8,128)(2,1)S(1)}, bf16[336,256]{1,0:T(8,128)(2,1)}, u32[]{:S(2)}, u32[]{:S(2)}) collective-permute-start(bf16[336,256]{1,0:T(8,128)(2,1)S(1)} %copy-done.21), channel_id=1, source_target_pairs={{0,12},{1,13},{2,14},{3,15},{4,8},{5,9},{6,10},{7,11},{8,4},{9,5},... | collective-permute-start | bytes 516104 | tf_op jit(solution)/shard_map/ppermute | solution.py:151
  30.9 72.1 %collective-permute-start.4 = (bf16[256,2688]{1,0:T(8,128)(2,1)}, bf16[256,2688]{1,0:T(8,128)(2,1)}, u32[]{:S(2)}, u32[]{:S(2)}) collective-permute-start(bf16[256,2688]{1,0:T(8,128)(2,1)} %fusion.2.refs_0_), channel_id=1, source_target_pairs={{0,4},{1,5},{2,6},{3,7},{4,0},{5,1},{6,2},{7,3},{8,12},{9,13},{10,... | collective-permute-start | bytes 4128776 | tf_op jit(solution)/shard_map/ppermute | solution.py:151
  85.3 33.4 %collective-permute-start.1 = (bf16[256,2688]{1,0:T(8,128)(2,1)}, bf16[256,2688]{1,0:T(8,128)(2,1)}, u32[]{:S(2)}, u32[]{:S(2)}) collective-permute-start(bf16[256,2688]{1,0:T(8,128)(2,1)} %fusion.2.refs_0_), channel_id=1, source_target_pairs={{0,1},{1,0},{2,3},{3,2},{4,5},{5,4},{6,7},{7,6},{8,9},{9,8},{10,11... | collective-permute-start | bytes 4128776 | tf_op jit(solution)/shard_map/ppermute | solution.py:151
  88.0 30.7 %collective-permute-start.2 = (bf16[256,2688]{1,0:T(8,128)(2,1)}, bf16[256,2688]{1,0:T(8,128)(2,1)}, u32[]{:S(2)}, u32[]{:S(2)}) collective-permute-start(bf16[256,2688]{1,0:T(8,128)(2,1)} %fusion.2.refs_0_), channel_id=1, source_target_pairs={{0,2},{1,3},{2,0},{3,1},{4,6},{5,7},{6,4},{7,5},{8,10},{9,11},{10,... | collective-permute-start | bytes 4128776 | tf_op jit(solution)/shard_map/ppermute | solution.py:151
  91.8 36.3 %collective-permute-start.12 = (bf16[256,2688]{1,0:T(8,128)(2,1)}, bf16[256,2688]{1,0:T(8,128)(2,1)}, u32[]{:S(2)}, u32[]{:S(2)}) collective-permute-start(bf16[256,2688]{1,0:T(8,128)(2,1)} %collective-permute-done.8.refs_8_), channel_id=1, source_target_pairs={{0,4},{1,5},{2,6},{3,7},{4,0},{5,1},{6,2},{7,3},{8,12},{9,13},{10,... | collective-permute-start | bytes 4128776 | tf_op jit(solution)/shard_map/ppermute | solution.py:151
  98.8 49.4 %collective-permute-start.9 = (bf16[256,2688]{1,0:T(8,128)(2,1)}, bf16[256,2688]{1,0:T(8,128)(2,1)}, u32[]{:S(2)}, u32[]{:S(2)}) collective-permute-start(bf16[256,2688]{1,0:T(8,128)(2,1)} %collective-permute-done.8.refs_8_), channel_id=1, source_target_pairs={{0,1},{1,0},{2,3},{3,2},{4,5},{5,4},{6,7},{7,6},{8,9},{9,8},{10,11... | collective-permute-start | bytes 4128776 | tf_op jit(solution)/shard_map/ppermute | solution.py:151
  102.9 180.1 %all-gather.11.cloned.1.call-start = ((), (), s32[]{:S(2)}) async-start(), calls=%async_computation.3 | async-start | bytes 1966080 | tf_op jit(solution)/shard_map/all_gather | solution.py:489
  103.0 74.6 %collective-permute-start.5 = (bf16[256,2688]{1,0:T(8,128)(2,1)}, bf16[256,2688]{1,0:T(8,128)(2,1)S(1)}, u32[]{:S(2)}, u32[]{:S(2)}) collective-permute-start(bf16[256,2688]{1,0:T(8,128)(2,1)} %collective-permute-done.4.refs_4_), channel_id=1, source_target_pairs={{0,1},{1,0},{2,3},{3,2},{4,5},{5,4},{6,7},{7,6},{8,9},{9,8},{10,11... | collective-permute-start | bytes 4128776 | tf_op jit(solution)/shard_map/ppermute | solution.py:151
  118.7 58.9 %collective-permute-start.10 = (bf16[256,2688]{1,0:T(8,128)(2,1)}, bf16[256,2688]{1,0:T(8,128)(2,1)}, u32[]{:S(2)}, u32[]{:S(2)}) collective-permute-start(bf16[256,2688]{1,0:T(8,128)(2,1)} %collective-permute-done.8.refs_8_), channel_id=1, source_target_pairs={{0,2},{1,3},{2,0},{3,1},{4,6},{5,7},{6,4},{7,5},{8,10},{9,11},{10,... | collective-permute-start | bytes 4128776 | tf_op jit(solution)/shard_map/ppermute | solution.py:151
  118.7 60.9 %collective-permute-start.6 = (bf16[256,2688]{1,0:T(8,128)(2,1)}, bf16[256,2688]{1,0:T(8,128)(2,1)}, u32[]{:S(2)}, u32[]{:S(2)}) collective-permute-start(bf16[256,2688]{1,0:T(8,128)(2,1)} %collective-permute-done.4.refs_4_), channel_id=1, source_target_pairs={{0,2},{1,3},{2,0},{3,1},{4,6},{5,7},{6,4},{7,5},{8,10},{9,11},{10,... | collective-permute-start | bytes 4128776 | tf_op jit(solution)/shard_map/ppermute | solution.py:151
  128.1 51.6 %collective-permute-start.3 = (bf16[256,2688]{1,0:T(8,128)(2,1)}, bf16[256,2688]{1,0:T(8,128)(2,1)}, u32[]{:S(2)}, u32[]{:S(2)}) collective-permute-start(bf16[256,2688]{1,0:T(8,128)(2,1)} %collective-permute-done.1.refs_1_), channel_id=1, source_target_pairs={{0,2},{1,3},{2,0},{3,1},{4,6},{5,7},{6,4},{7,5},{8,10},{9,11},{10,... | collective-permute-start | bytes 4128776 | tf_op jit(solution)/shard_map/ppermute | solution.py:151
  148.2 51.8 %collective-permute-start.13 = (bf16[256,2688]{1,0:T(8,128)(2,1)}, bf16[256,2688]{1,0:T(8,128)(2,1)}, u32[]{:S(2)}, u32[]{:S(2)}) collective-permute-start(bf16[256,2688]{1,0:T(8,128)(2,1)} %collective-permute-done.12.refs_12_), channel_id=1, source_target_pairs={{0,1},{1,0},{2,3},{3,2},{4,5},{5,4},{6,7},{7,6},{8,9},{9,8},{10,11... | collective-permute-start | bytes 4128776 | tf_op jit(solution)/shard_map/ppermute | solution.py:151
  177.6 11.0 %collective-permute-start.17 = (bf16[672,256]{1,0:T(8,128)(2,1)S(1)}, bf16[672,256]{1,0:T(8,128)(2,1)S(1)}, u32[]{:S(2)}, u32[]{:S(2)}) collective-permute-start(bf16[672,256]{1,0:T(8,128)(2,1)S(1)} %get-tuple-element.52), channel_id=1, source_target_pairs={{0,4},{1,5},{2,6},{3,7},{4,0},{5,1},{6,2},{7,3},{8,12},{9,13},{10,... | collective-permute-start | bytes 1032200 | tf_op jit(solution)/shard_map/ppermute | solution.py:151
  179.6 15.7 %collective-permute-start.18 = (bf16[672,256]{1,0:T(8,128)(2,1)S(1)}, bf16[672,256]{1,0:T(8,128)(2,1)S(1)}, u32[]{:S(2)}, u32[]{:S(2)}) collective-permute-start(bf16[672,256]{1,0:T(8,128)(2,1)S(1)} %get-tuple-element.51), channel_id=1, source_target_pairs={{0,6},{1,7},{2,4},{3,5},{4,2},{5,3},{6,0},{7,1},{8,14},{9,15},{10,... | collective-permute-start | bytes 1032200 | tf_op jit(solution)/shard_map/ppermute | solution.py:151
  179.8 22.3 %collective-permute-start.19 = (bf16[672,256]{1,0:T(8,128)(2,1)S(1)}, bf16[672,256]{1,0:T(8,128)(2,1)}, u32[]{:S(2)}, u32[]{:S(2)}) collective-permute-start(bf16[672,256]{1,0:T(8,128)(2,1)S(1)} %get-tuple-element.50), channel_id=1, source_target_pairs={{0,8},{1,9},{2,10},{3,11},{4,12},{5,13},{6,14},{7,15},{8,0},{9,1},... | collective-permute-start | bytes 1032200 | tf_op jit(solution)/shard_map/ppermute | solution.py:151
  181.5 67.3 %collective-permute-start.14 = (bf16[256,2688]{1,0:T(8,128)(2,1)}, bf16[256,2688]{1,0:T(8,128)(2,1)}, u32[]{:S(2)}, u32[]{:S(2)}) collective-permute-start(bf16[256,2688]{1,0:T(8,128)(2,1)} %collective-permute-done.12.refs_12_), channel_id=1, source_target_pairs={{0,2},{1,3},{2,0},{3,1},{4,6},{5,7},{6,4},{7,5},{8,10},{9,11},{10,... | collective-permute-start | bytes 4128776 | tf_op jit(solution)/shard_map/ppermute | solution.py:151
  188.6 60.1 %collective-permute-start.11 = (bf16[256,2688]{1,0:T(8,128)(2,1)}, bf16[256,2688]{1,0:T(8,128)(2,1)}, u32[]{:S(2)}, u32[]{:S(2)}) collective-permute-start(bf16[256,2688]{1,0:T(8,128)(2,1)} %collective-permute-done.9.refs_9_), channel_id=1, source_target_pairs={{0,2},{1,3},{2,0},{3,1},{4,6},{5,7},{6,4},{7,5},{8,10},{9,11},{10,... | collective-permute-start | bytes 4128776 | tf_op jit(solution)/shard_map/ppermute | solution.py:151
  195.4 53.4 %collective-permute-start.7 = (bf16[256,2688]{1,0:T(8,128)(2,1)S(1)}, bf16[256,2688]{1,0:T(8,128)(2,1)}, u32[]{:S(2)}, u32[]{:S(2)}) collective-permute-start(bf16[256,2688]{1,0:T(8,128)(2,1)S(1)} %collective-permute-done.5.refs_5_), channel_id=1, source_target_pairs={{0,2},{1,3},{2,0},{3,1},{4,6},{5,7},{6,4},{7,5},{8,10},{9,11},{10,... | collective-permute-start | bytes 4128776 | tf_op jit(solution)/shard_map/ppermute | solution.py:151
  200.0 48.8 %collective-permute-start.15 = (bf16[256,2688]{1,0:T(8,128)(2,1)}, bf16[256,2688]{1,0:T(8,128)(2,1)}, u32[]{:S(2)}, u32[]{:S(2)}) collective-permute-start(bf16[256,2688]{1,0:T(8,128)(2,1)} %collective-permute-done.13.refs_13_), channel_id=1, source_target_pairs={{0,2},{1,3},{2,0},{3,1},{4,6},{5,7},{6,4},{7,5},{8,10},{9,11},{10,... | collective-permute-start | bytes 4128776 | tf_op jit(solution)/shard_map/ppermute | solution.py:151
  202.0 99.2 %all-gather.13.cloned.1.call-start = ((), (), s32[]{:S(2)}) async-start(), calls=%async_computation.4 | async-start | bytes 2162688 | tf_op jit(solution)/shard_map/all_gather | solution.py:489
  202.1 11.2 %collective-permute-start.20 = (bf16[672,256]{1,0:T(8,128)(2,1)S(1)}, bf16[672,256]{1,0:T(8,128)(2,1)S(1)}, u32[]{:S(2)}, u32[]{:S(2)}) collective-permute-start(bf16[672,256]{1,0:T(8,128)(2,1)S(1)} %get-tuple-element.49), channel_id=1, source_target_pairs={{0,10},{1,11},{2,8},{3,9},{4,14},{5,15},{6,12},{7,13},{8,2},{9,3},... | collective-permute-start | bytes 1032200 | tf_op jit(solution)/shard_map/ppermute | solution.py:151
  213.3 17.6 %collective-permute-start.21 = (bf16[672,256]{1,0:T(8,128)(2,1)S(1)}, bf16[672,256]{1,0:T(8,128)(2,1)S(1)}, u32[]{:S(2)}, u32[]{:S(2)}) collective-permute-start(bf16[672,256]{1,0:T(8,128)(2,1)S(1)} %get-tuple-element.48), channel_id=1, source_target_pairs={{0,12},{1,13},{2,14},{3,15},{4,8},{5,9},{6,10},{7,11},{8,4},{9,5},... | collective-permute-start | bytes 1032200 | tf_op jit(solution)/shard_map/ppermute | solution.py:151
  230.8 16.4 %collective-permute-start.22 = (bf16[672,256]{1,0:T(8,128)(2,1)S(1)}, bf16[672,256]{1,0:T(8,128)(2,1)S(1)}, u32[]{:S(2)}, u32[]{:S(2)}) collective-permute-start(bf16[672,256]{1,0:T(8,128)(2,1)S(1)} %get-tuple-element.47), channel_id=1, source_target_pairs={{0,14},{1,15},{2,12},{3,13},{4,10},{5,11},{6,8},{7,9},{8,6},{9,7},... | collective-permute-start | bytes 1032200 | tf_op jit(solution)/shard_map/ppermute | solution.py:151
  247.2 75.5 %collective-permute-start.47 = (bf16[336,2048]{1,0:T(8,128)(2,1)}, bf16[336,2048]{1,0:T(8,128)(2,1)}, u32[]{:S(2)}, u32[]{:S(2)}) collective-permute-start(bf16[336,2048]{1,0:T(8,128)(2,1)} %bitcast.8.refs_16_), channel_id=1, source_target_pairs={{0,1},{1,0},{2,3},{3,2},{4,5},{5,4},{6,7},{7,6},{8,9},{9,8},{10,11... | collective-permute-start | bytes 4128776 | tf_op jit(solution)/shard_map/ppermute | solution.py:151
  276.5 17.9 %collective-permute-start.38 = (bf16[4,256,256]{2,1,0:T(8,128)(2,1)}, bf16[4,256,256]{2,1,0:T(8,128)(2,1)}, u32[]{:S(2)}, u32[]{:S(2)}) collective-permute-start(bf16[4,256,256]{2,1,0:T(8,128)(2,1)} %get-tuple-element.43), channel_id=1, source_target_pairs={{0,16},{1,17},{2,18},{3,19},{4,20},{5,21},{6,22},{7,23},{8,24},{9,... | collective-permute-start | bytes 1572872 | tf_op jit(solution)/shard_map/ppermute | solution.py:482
  285.0 37.7 %collective-permute-start.48 = (bf16[160,2048]{1,0:T(8,128)(2,1)}, bf16[160,2048]{1,0:T(8,128)(2,1)}, u32[]{:S(2)}, u32[]{:S(2)}) collective-permute-start(bf16[160,2048]{1,0:T(8,128)(2,1)} %dynamic-slice_bitcast_fusion.1.refs_18_), channel_id=1, source_target_pairs={{0,1},{1,0},{2,3},{3,2},{4,5},{5,4},{6,7},{7,6},{8,9},{9,8},{10,11... | collective-permute-start | bytes 1966088 | tf_op jit(solution)/shard_map/ppermute | solution.py:151
  293.0 15.5 %collective-permute-start.30 = (bf16[4,128,256]{2,1,0:T(8,128)(2,1)}, bf16[4,128,256]{2,1,0:T(8,128)(2,1)}, u32[]{:S(2)}, u32[]{:S(2)}) collective-permute-start(bf16[4,128,256]{2,1,0:T(8,128)(2,1)} %get-tuple-element.42), channel_id=1, source_target_pairs={{0,1},{1,0},{2,3},{3,2},{4,5},{5,4},{6,7},{7,6},{8,9},{9,8},{10,11... | collective-permute-start | bytes 786440 | tf_op jit(solution)/shard_map/ppermute | solution.py:151
  300.5 18.7 %collective-permute-start.39 = (bf16[4,128,256]{2,1,0:T(8,128)(2,1)}, bf16[4,128,256]{2,1,0:T(8,128)(2,1)}, u32[]{:S(2)}, u32[]{:S(2)}) collective-permute-start(bf16[4,128,256]{2,1,0:T(8,128)(2,1)} %get-tuple-element.45), channel_id=1, source_target_pairs={{0,1},{1,0},{2,3},{3,2},{4,5},{5,4},{6,7},{7,6},{8,9},{9,8},{10,11... | collective-permute-start | bytes 786440 | tf_op jit(solution)/shard_map/ppermute | solution.py:151
  303.2 25.0 %collective-permute-start.49 = (bf16[176,2048]{1,0:T(8,128)(2,1)}, bf16[176,2048]{1,0:T(8,128)(2,1)}, u32[]{:S(2)}, u32[]{:S(2)}) collective-permute-start(bf16[176,2048]{1,0:T(8,128)(2,1)} %dynamic-slice_bitcast_fusion.refs_20_), channel_id=1, source_target_pairs={{0,1},{1,0},{2,3},{3,2},{4,5},{5,4},{6,7},{7,6},{8,9},{9,8},{10,11... | collective-permute-start | bytes 2162696 | tf_op jit(solution)/shard_map/ppermute | solution.py:151
  310.4 21.8 %collective-permute-start.34 = (bf16[2,4,128,256]{3,2,1,0:T(8,128)(2,1)}, bf16[2,4,128,256]{3,2,1,0:T(8,128)(2,1)}, u32[]{:S(2)}, u32[]{:S(2)}) collective-permute-start(bf16[2,4,128,256]{3,2,1,0:T(8,128)(2,1)} %shard_map.95.refs_0_), channel_id=1, source_target_pairs={{0,8},{1,9},{2,10},{3,11},{4,12},{5,13},{6,14},{7,15},{8,0},{9,1},... | collective-permute-start | bytes 1572872 | tf_op jit(solution)/shard_map/ppermute | solution.py:151
  319.2 15.1 %collective-permute-start.32 = (bf16[2,4,128,256]{3,2,1,0:T(8,128)(2,1)}, bf16[2,4,128,256]{3,2,1,0:T(8,128)(2,1)}, u32[]{:S(2)}, u32[]{:S(2)}) collective-permute-start(bf16[2,4,128,256]{3,2,1,0:T(8,128)(2,1)} %shard_map.95.refs_0_), channel_id=1, source_target_pairs={{0,4},{1,5},{2,6},{3,7},{4,0},{5,1},{6,2},{7,3},{8,12},{9,13},{10,... | collective-permute-start | bytes 1572872 | tf_op jit(solution)/shard_map/ppermute | solution.py:151
  322.7 13.2 %collective-permute-start.31 = (bf16[2,4,128,256]{3,2,1,0:T(8,128)(2,1)}, bf16[2,4,128,256]{3,2,1,0:T(8,128)(2,1)}, u32[]{:S(2)}, u32[]{:S(2)}) collective-permute-start(bf16[2,4,128,256]{3,2,1,0:T(8,128)(2,1)} %shard_map.95.refs_0_), channel_id=1, source_target_pairs={{0,2},{1,3},{2,0},{3,1},{4,6},{5,7},{6,4},{7,5},{8,10},{9,11},{10,... | collective-permute-start | bytes 1572872 | tf_op jit(solution)/shard_map/ppermute | solution.py:151
  322.7 19.5 %collective-permute-start.43 = (bf16[2,4,128,256]{3,2,1,0:T(8,128)(2,1)}, bf16[2,4,128,256]{3,2,1,0:T(8,128)(2,1)S(1)}, u32[]{:S(2)}, u32[]{:S(2)}) collective-permute-start(bf16[2,4,128,256]{3,2,1,0:T(8,128)(2,1)} %shard_map.97.refs_8_), channel_id=1, source_target_pairs={{0,8},{1,9},{2,10},{3,11},{4,12},{5,13},{6,14},{7,15},{8,0},{9,1},... | collective-permute-start | bytes 1572872 | tf_op jit(solution)/shard_map/ppermute | solution.py:151
  328.3 17.1 %collective-permute-start.41 = (bf16[2,4,128,256]{3,2,1,0:T(8,128)(2,1)}, bf16[2,4,128,256]{3,2,1,0:T(8,128)(2,1)S(1)}, u32[]{:S(2)}, u32[]{:S(2)}) collective-permute-start(bf16[2,4,128,256]{3,2,1,0:T(8,128)(2,1)} %shard_map.97.refs_8_), channel_id=1, source_target_pairs={{0,4},{1,5},{2,6},{3,7},{4,0},{5,1},{6,2},{7,3},{8,12},{9,13},{10,... | collective-permute-start | bytes 1572872 | tf_op jit(solution)/shard_map/ppermute | solution.py:151
  332.2 13.2 %collective-permute-start.40 = (bf16[2,4,128,256]{3,2,1,0:T(8,128)(2,1)}, bf16[2,4,128,256]{3,2,1,0:T(8,128)(2,1)S(1)}, u32[]{:S(2)}, u32[]{:S(2)}) collective-permute-start(bf16[2,4,128,256]{3,2,1,0:T(8,128)(2,1)} %shard_map.97.refs_8_), channel_id=1, source_target_pairs={{0,2},{1,3},{2,0},{3,1},{4,6},{5,7},{6,4},{7,5},{8,10},{9,11},{10,... | collective-permute-start | bytes 1572872 | tf_op jit(solution)/shard_map/ppermute | solution.py:151
  334.3 22.4 %collective-permute-start.36 = (bf16[2,4,128,256]{3,2,1,0:T(8,128)(2,1)}, bf16[2,4,128,256]{3,2,1,0:T(8,128)(2,1)S(1)}, u32[]{:S(2)}, u32[]{:S(2)}) collective-permute-start(bf16[2,4,128,256]{3,2,1,0:T(8,128)(2,1)} %collective-permute-done.34.refs_4_), channel_id=1, source_target_pairs={{0,4},{1,5},{2,6},{3,7},{4,0},{5,1},{6,2},{7,3},{8,12},{9,13},{10,... | collective-permute-start | bytes 1572872 | tf_op jit(solution)/shard_map/ppermute | solution.py:151
  335.9 20.7 %collective-permute-start.33 = (bf16[2,4,128,256]{3,2,1,0:T(8,128)(2,1)}, bf16[2,4,128,256]{3,2,1,0:T(8,128)(2,1)S(1)}, u32[]{:S(2)}, u32[]{:S(2)}) collective-permute-start(bf16[2,4,128,256]{3,2,1,0:T(8,128)(2,1)} %collective-permute-done.32.refs_2_), channel_id=1, source_target_pairs={{0,2},{1,3},{2,0},{3,1},{4,6},{5,7},{6,4},{7,5},{8,10},{9,11},{10,... | collective-permute-start | bytes 1572872 | tf_op jit(solution)/shard_map/ppermute | solution.py:151
  342.2 23.9 %collective-permute-start.45 = (bf16[2,4,128,256]{3,2,1,0:T(8,128)(2,1)S(1)}, bf16[2,4,128,256]{3,2,1,0:T(8,128)(2,1)S(1)}, u32[]{:S(2)}, u32[]{:S(2)}) collective-permute-start(bf16[2,4,128,256]{3,2,1,0:T(8,128)(2,1)S(1)} %collective-permute-done.43.refs_12_), channel_id=1, source_target_pairs={{0,4},{1,5},{2,6},{3,7},{4,0},{5,1},{6,2},{7,3},{8,12},{9,13},{10,... | collective-permute-start | bytes 1572872 | tf_op jit(solution)/shard_map/ppermute | solution.py:151
  345.4 20.8 %collective-permute-start.35 = (bf16[2,4,128,256]{3,2,1,0:T(8,128)(2,1)}, bf16[2,4,128,256]{3,2,1,0:T(8,128)(2,1)S(1)}, u32[]{:S(2)}, u32[]{:S(2)}) collective-permute-start(bf16[2,4,128,256]{3,2,1,0:T(8,128)(2,1)} %collective-permute-done.34.refs_4_), channel_id=1, source_target_pairs={{0,2},{1,3},{2,0},{3,1},{4,6},{5,7},{6,4},{7,5},{8,10},{9,11},{10,... | collective-permute-start | bytes 1572872 | tf_op jit(solution)/shard_map/ppermute | solution.py:151
  345.4 20.8 %collective-permute-start.44 = (bf16[2,4,128,256]{3,2,1,0:T(8,128)(2,1)S(1)}, bf16[2,4,128,256]{3,2,1,0:T(8,128)(2,1)S(1)}, u32[]{:S(2)}, u32[]{:S(2)}) collective-permute-start(bf16[2,4,128,256]{3,2,1,0:T(8,128)(2,1)S(1)} %collective-permute-done.43.refs_12_), channel_id=1, source_target_pairs={{0,2},{1,3},{2,0},{3,1},{4,6},{5,7},{6,4},{7,5},{8,10},{9,11},{10,... | collective-permute-start | bytes 1572872 | tf_op jit(solution)/shard_map/ppermute | solution.py:151
  356.6 9.6 %collective-permute-start.42 = (bf16[2,4,128,256]{3,2,1,0:T(8,128)(2,1)S(1)}, bf16[2,4,128,256]{3,2,1,0:T(8,128)(2,1)S(1)}, u32[]{:S(2)}, u32[]{:S(2)}) collective-permute-start(bf16[2,4,128,256]{3,2,1,0:T(8,128)(2,1)S(1)} %collective-permute-done.41.refs_10_), channel_id=1, source_target_pairs={{0,2},{1,3},{2,0},{3,1},{4,6},{5,7},{6,4},{7,5},{8,10},{9,11},{10,... | collective-permute-start | bytes 1572872 | tf_op jit(solution)/shard_map/ppermute | solution.py:151
  356.6 9.6 %collective-permute-start.37 = (bf16[2,4,128,256]{3,2,1,0:T(8,128)(2,1)S(1)}, bf16[2,4,128,256]{3,2,1,0:T(8,128)(2,1)S(1)}, u32[]{:S(2)}, u32[]{:S(2)}) collective-permute-start(bf16[2,4,128,256]{3,2,1,0:T(8,128)(2,1)S(1)} %collective-permute-done.36.refs_6_), channel_id=1, source_target_pairs={{0,2},{1,3},{2,0},{3,1},{4,6},{5,7},{6,4},{7,5},{8,10},{9,11},{10,... | collective-permute-start | bytes 1572872 | tf_op jit(solution)/shard_map/ppermute | solution.py:151
  (33 other events, 367.0 us)
Sparse Core Ops, SparseCore 0:
  11.1 72.6 all-gather.6
  103.0 70.0 all-gather.8
  202.1 41.8 all-gather.10
  245.4 40.9 all-gather.12

commit v3 on v2

--- a/solution.py
+++ b/solution.py
@@ -197,7 +197,7 @@
     blocks, kv_parts = refs[: 2 * n], refs[2 * n : 3 * n]
     q_rows = refs[3 * n]
     kv_out, tail_out, q_out = refs[3 * n + 1 : 3 * n + 4]
-    block_mem, weight_mem, block_sem, weight_sem = refs[3 * n + 4 :]
+    block_mem, kv_mem, q_mem, block_sem, weight_sem = refs[3 * n + 4 :]
     place, col = meta[0], meta[2]
     _, _, tokens, features = block_mem.shape
     deep = kv_parts[0].shape[0] // 2
@@ -207,14 +207,8 @@
         for half in range(2):
             for k, (source, target) in enumerate(
                 [
-                    (
-                        kv_parts[m].at[pl.ds(half * deep, deep)],
-                        weight_mem.at[half, rows, pl.ds(0, 2 * HD)],
-                    ),
-                    (
-                        q_rows.at[pl.ds((half * n + m) * deep, deep)],
-                        weight_mem.at[half, rows, pl.ds(2 * HD, heads * HD)],
-                    ),
+                    (kv_parts[m].at[pl.ds(half * deep, deep)], kv_mem.at[half, rows, :]),
+                    (q_rows.at[pl.ds((half * n + m) * deep, deep)], q_mem.at[half, rows, :]),
                 ]
             ):
                 sem = weight_sem.at[4 * m + 2 * half + k]
@@ -238,13 +232,15 @@
                 ).wait()
         mine = block_mem[0, pl.ds(2 * t, 2)].reshape(2 * tokens, features)
         theirs = block_mem[1, pl.ds(2 * t, 2)].reshape(2 * tokens, features)
-        raw_two = jnp.dot(mine, weight_mem[col], preferred_element_type=jnp.float32) + jnp.dot(
-            theirs, weight_mem[lax.bitwise_xor(col, 1)], preferred_element_type=jnp.float32
-        )
+        kv_two, q_two = [
+            jnp.dot(mine, mem[col], preferred_element_type=jnp.float32)
+            + jnp.dot(theirs, mem[lax.bitwise_xor(col, 1)], preferred_element_type=jnp.float32)
+            for mem in (kv_mem, q_mem)
+        ]
         for m in range(2):
             slot = 2 * t + m
             at = lax.bitwise_xor(place, slot)
-            raw = raw_two[m * tokens : (m + 1) * tokens]
+            raw = kv_two[m * tokens : (m + 1) * tokens]
             cosine_here, sine_here = cosine[at], sine[at]
             keys = normed_rotated(raw[:, :HD], key_gain[...], cosine_here, sine_here)
             keys = keys.astype(jnp.bfloat16)
@@ -252,7 +248,7 @@
             kv_out[at, :, :HD] = keys
             kv_out[at, :, HD:] = values
             for h in range(heads):
-                query = raw[:, (2 + h) * HD : (3 + h) * HD]
+                query = q_two[m * tokens : (m + 1) * tokens, h * HD : (h + 1) * HD]
                 query = normed_rotated(query, query_gain[...], cosine_here, sine_here)
                 q_out[at, pl.ds(h * tokens, tokens), :] = query.astype(jnp.bfloat16)
 
@@ -303,24 +299,24 @@
             send_out[g, :, h * HD : (h + 1) * HD] = jnp.where(col == 0, bottom, top)
 
 
-def output_kernel(n, spans, meta, *refs):
+def output_kernel(n, spans, far, meta, *refs):
     count = n * len(spans)
-    contexts, weights = refs[:count], refs[count : count + 6]
-    out, context_mem, weight_mem, context_sem, weight_sem = refs[count + 6 :]
+    contexts, weights = refs[:count], refs[count:-5]
+    if far:
+        weights, before = weights[:-1], weights[-1]
+    out, context_mem, weight_mem, context_sem, weight_sem = refs[-5:]
     place, half, col = meta[0], meta[1], meta[2]
     deep = weights[0].shape[1]
     wide = contexts[0].shape[3]
     part = contexts[0].shape[2]
     copies = []
     for k, source in enumerate(weights):
-        owner = half if k < 2 else lax.bitwise_xor(half, 1)
-        rows = source.shape[0]
-        first = 0 if k < 4 else weights[2].shape[0]
+        first = sum(weights[j].shape[0] for j in range(k % 2, k, 2))
         side = pl.multiple_of(lax.bitwise_xor(col, k % 2) * deep, 128)
         copies.append(
             pltpu.make_async_copy(
                 source,
-                weight_mem.at[owner, pl.ds(first, rows), pl.ds(side, deep)],
+                weight_mem.at[pl.ds(first, source.shape[0]), pl.ds(side, deep)],
                 weight_sem.at[k],
             )
         )
@@ -345,15 +341,16 @@
     @pl.loop(0, n // 4)
     def _(t):
         left = context_mem[pl.ds(4 * t, 4)].reshape(4 * part, 2 * deep)
-        for block in range(2):
-            result = lax.dot_general(
-                left,
-                weight_mem[block],
-                (((1,), (1,)), ((), ())),
-                preferred_element_type=jnp.float32,
-            ).astype(jnp.bfloat16)
-            for k in range(4):
-                out[(4 * t + k) * 2 + block] = result[k * part : (k + 1) * part]
+        result = lax.dot_general(
+            left, weight_mem[...], (((1,), (1,)), ((), ())), preferred_element_type=jnp.float32
+        ).astype(jnp.bfloat16)
+        for k in range(4):
+            slab = result[k * part : (k + 1) * part]
+            if far:
+                out[2 * (4 * t + k) + lax.bitwise_xor(half, 1)] = slab
+                out[2 * (4 * t + k) + half] = before[4 * t + k]
+            else:
+                out[4 * t + k] = slab
 
 
 def close_kernel(n, activations, arrived, out):
@@ -463,7 +460,8 @@
         [VMEM, VMEM, VMEM],
         [
             pltpu.VMEM((2, n, tokens, features), bf16),
-            pltpu.VMEM((2, features, (2 + heads) * HD), bf16),
+            pltpu.VMEM((2, features, 2 * HD), bf16),
+            pltpu.VMEM((2, features, heads * HD), bf16),
             pltpu.SemaphoreType.DMA((n, 2)),
             pltpu.SemaphoreType.DMA((4 * n,)),
         ],
@@ -481,14 +479,14 @@
     )
     kv_back = lax.ppermute(kv_tail, "half", [(0, 1)])
 
-    own_weight = output_weight.T
-    ahead = own_weight.shape[0] // 32 * 16
-    own_weight, _ = lax.optimization_barrier((own_weight, q_own))
-    out_weights = [own_weight, swapped(own_weight, 0, 1)]
+    own_weight, _ = lax.optimization_barrier((output_weight.T, q_own))
+    ahead = own_weight.shape[0] * 4 // 7 // 16 * 16
+    near_weights = [own_weight, swapped(own_weight, 0, 1)]
+    far_weights = []
     for rows in [own_weight[:ahead], own_weight[ahead:]]:
         both = lax.all_gather(rows, "half", axis=0)
         piece = lax.dynamic_index_in_dim(both, 1 - half, 0, keepdims=False)
-        out_weights += [piece, swapped(piece, 0, 1)]
+        far_weights += [piece, swapped(piece, 0, 1)]
 
     contexts = []
     spans = [(reach, n - reach), (0, reach)]
@@ -524,22 +522,26 @@
 
     out_cols = output_weight.shape[1]
     deep_out = output_weight.shape[0]
-    result = run(
-        functools.partial(output_kernel, n, spans),
-        shaped((2 * n, part, out_cols), bf16),
-        [SMEM] + [ANY] * (2 * n + 6),
-        VMEM,
-        [
-            pltpu.VMEM((n, part, 2 * deep_out), bf16),
-            pltpu.VMEM((2, out_cols, 2 * deep_out), bf16),
-            pltpu.SemaphoreType.DMA((4 * n,)),
-            pltpu.SemaphoreType.DMA((6,)),
-        ],
-        2 * n * part * 2 * deep_out * 2 * out_cols,
-        16 * deep_out * out_cols,
-    )(meta, *contexts, *out_weights)
-
-    arrived = lax.all_to_all(result, ("place", "cols"), 0, 0, tiled=True)
+    result = []
+    for weights, shape in ((near_weights, (n,)), (far_weights, (2 * n,))):
+        result = [
+            run(
+                functools.partial(output_kernel, n, spans, len(result)),
+                shaped((*shape, part, out_cols), bf16),
+                [SMEM] + [ANY] * (2 * n + len(weights)) + [VMEM] * len(result),
+                VMEM,
+                [
+                    pltpu.VMEM((n, part, 2 * deep_out), bf16),
+                    pltpu.VMEM((out_cols, 2 * deep_out), bf16),
+                    pltpu.SemaphoreType.DMA((4 * n,)),
+                    pltpu.SemaphoreType.DMA((len(weights),)),
+                ],
+                2 * n * part * 2 * deep_out * out_cols,
+                8 * deep_out * out_cols,
+            )(meta, *contexts, *weights, *result)
+        ]
+
+    arrived = lax.all_to_all(result[0], ("place", "cols"), 0, 0, tiled=True)
     return run(
         functools.partial(close_kernel, n),
         shaped((tokens, features), bf16),

time: 428 us -> 413 us (0.965)
  starting transfers between devices: 62.5 us -> 46.8 us
  Pallas kernels: 69.5 us -> 75.2 us
  blocking collectives: 29.1 us -> 23.4 us
    ppermute x49, starting transfers between devices: 56.5 us -> 43.4 us  [swapped(): return lax.ppermute(value, ('place', 'cols'), pairs)]
    pallas_call x1 -> x2, Pallas kernels: 16.3 us -> 22.5 us  [split_body(): run(functools.partial(output_kernel, n, spans, len(result)), shaped((*sha...]
    all_to_all x1, blocking collectives: 29.1 us -> 23.4 us  [split_body(): arrived = lax.all_to_all(result[0], ('place', 'cols'), 0, 0, tiled=True)]
  transfers between devices with their start and end apart: 54 -> 54, of which waited for: 25 -> 22; matrix products, arithmetic and copies ran while one was open for 5% -> 5% of each run, Pallas kernels for 11% -> 15%
where the time goes in v3:
time: 413 us; the launch traced here: 412 us
  waiting for transfers between devices  225 us (54%)
  Pallas kernels  75.2 us (18%)
  starting transfers between devices  46.8 us (11%)
  blocking collectives  23.4 us (6%)
  local copies, waits for them, and re-layouts  20 us (5%)
  between operations  13.6 us (3%)
  other arithmetic  8.34 us (2%)
    ppermute x49, waiting for transfers between devices, swapped(): return lax.ppermute(value, ('place', 'cols'), pairs)  225 us
    ppermute x49, starting transfers between devices, swapped(): return lax.ppermute(value, ('place', 'cols'), pairs)  43.4 us
    pallas_call x1, Pallas kernels, split_body(): run(functools.partial(project_kernel, n, reach, heads), [shaped((n, token...  27.1 us
    all_to_all x1, blocking collectives, split_body(): arrived = lax.all_to_all(result[0], ('place', 'cols'), 0, 0, tiled=True)  23.4 us
    pallas_call x2, Pallas kernels, split_body(): run(functools.partial(output_kernel, n, spans, len(result)), shaped((*sha...  22.5 us
    pallas_call x2, Pallas kernels, split_body(): run(functools.partial(attend_kernel, low, count, reach, heads), [shape, s...  12.1 us
  transfers between devices with their start and end apart: 54, of which 22 were waited for; matrix products, arithmetic and copies ran while one was open for 5% of the time, Pallas kernels for 15%

profile of v3, /device:TPU:0, one launch (start us, length us, event | category | flops | bytes accessed | tf_op | source)
XLA Modules:
  0.0 412.1 jit_solution(3802492935704814949)
XLA Ops:
  6.5 1.7 fusion
  8.2 3.0 collective-permute-start
  11.9 3.8 shard_map.91
  22.7 3.7 collective-permute-done.24.refs_2_
  30.6 51.4 %collective-permute-done.26.refs_4_ = bf16[336,256]{1,0:T(8,128)(2,1)S(1)} collective-permute-done((bf16[336,256]{1,0:T(8,128)(2,1)S(1)}, bf16[336,256]{1,0:T(8,128)(2,1)S(1)}, u32[]{:S(2)}, u32[]{:S(2)}) %collective-permute-start.26) | collective-permute-done | bytes 172064 | tf_op jit(solution)/shard_map/ppermute | solution.py:151
  81.9 4.6 %collective-permute-done.27.refs_5_ = bf16[336,256]{1,0:T(8,128)(2,1)S(1)} collective-permute-done((bf16[336,256]{1,0:T(8,128)(2,1)S(1)}, bf16[336,256]{1,0:T(8,128)(2,1)S(1)}, u32[]{:S(2)}, u32[]{:S(2)}) %collective-permute-start.27) | collective-permute-done | bytes 172064 | tf_op jit(solution)/shard_map/ppermute | solution.py:151
  87.5 3.1 collective-permute-done.28.refs_6_
  92.0 5.5 %collective-permute-done.29.refs_7_ = bf16[336,256]{1,0:T(8,128)(2,1)S(1)} collective-permute-done((bf16[336,256]{1,0:T(8,128)(2,1)S(1)}, bf16[336,256]{1,0:T(8,128)(2,1)S(1)}, u32[]{:S(2)}, u32[]{:S(2)}) %collective-permute-start.29) | collective-permute-done | bytes 172064 | tf_op jit(solution)/shard_map/ppermute | solution.py:151
  99.5 15.5 %collective-permute-done.1.refs_1_ = bf16[256,2688]{1,0:T(8,128)(2,1)S(1)} collective-permute-done((bf16[256,2688]{1,0:T(8,128)(2,1)S(1)}, bf16[256,2688]{1,0:T(8,128)(2,1)S(1)}, u32[]{:S(2)}, u32[]{:S(2)}) %collective-permute-start.1) | collective-permute-done | bytes 1376288 | tf_op jit(solution)/shard_map/ppermute | solution.py:151
  117.2 2.7 shard_map.92
  120.0 7.0 %collective-permute-done.12.refs_12_ = bf16[256,2688]{1,0:T(8,128)(2,1)} collective-permute-done((bf16[256,2688]{1,0:T(8,128)(2,1)}, bf16[256,2688]{1,0:T(8,128)(2,1)}, u32[]{:S(2)}, u32[]{:S(2)}) %collective-permute-start.12) | collective-permute-done | bytes 1376288 | tf_op jit(solution)/shard_map/ppermute | solution.py:151
  127.1 17.5 %collective-permute-done.9.refs_9_ = bf16[256,2688]{1,0:T(8,128)(2,1)} collective-permute-done((bf16[256,2688]{1,0:T(8,128)(2,1)}, bf16[256,2688]{1,0:T(8,128)(2,1)}, u32[]{:S(2)}, u32[]{:S(2)}) %collective-permute-start.9) | collective-permute-done | bytes 1376288 | tf_op jit(solution)/shard_map/ppermute | solution.py:151
  144.7 3.7 fusion.3
  148.4 1.9 pad_maximum_fusion
  150.3 2.6 constant_dynamic-slice_fusion
  152.9 21.1 %collective-permute-done.5.refs_5_ = bf16[256,2688]{1,0:T(8,128)(2,1)} collective-permute-done((bf16[256,2688]{1,0:T(8,128)(2,1)}, bf16[256,2688]{1,0:T(8,128)(2,1)}, u32[]{:S(2)}, u32[]{:S(2)}) %collective-permute-start.5) | collective-permute-done | bytes 1376288 | tf_op jit(solution)/shard_map/ppermute | solution.py:151
  175.9 2.5 collective-permute-start.19
  178.4 6.6 %collective-permute-done.17.refs_18_ = bf16[672,256]{1,0:T(8,128)(2,1)S(1)} collective-permute-done((bf16[672,256]{1,0:T(8,128)(2,1)S(1)}, bf16[672,256]{1,0:T(8,128)(2,1)S(1)}, u32[]{:S(2)}, u32[]{:S(2)}) %collective-permute-start.17) | collective-permute-done | bytes 344096 | tf_op jit(solution)/shard_map/ppermute | solution.py:151
  185.0 6.4 %collective-permute-done.18.refs_19_ = bf16[672,256]{1,0:T(8,128)(2,1)S(1)} collective-permute-done((bf16[672,256]{1,0:T(8,128)(2,1)S(1)}, bf16[672,256]{1,0:T(8,128)(2,1)S(1)}, u32[]{:S(2)}, u32[]{:S(2)}) %collective-permute-start.18) | collective-permute-done | bytes 344096 | tf_op jit(solution)/shard_map/ppermute | solution.py:151
  192.1 4.9 %collective-permute-done.13.refs_13_ = bf16[256,2688]{1,0:T(8,128)(2,1)} collective-permute-done((bf16[256,2688]{1,0:T(8,128)(2,1)}, bf16[256,2688]{1,0:T(8,128)(2,1)}, u32[]{:S(2)}, u32[]{:S(2)}) %collective-permute-start.13) | collective-permute-done | bytes 1376288 | tf_op jit(solution)/shard_map/ppermute | solution.py:151
  197.0 2.6 collective-permute-done.19.refs_20_
  199.7 10.0 %collective-permute-done.20.refs_21_ = bf16[672,256]{1,0:T(8,128)(2,1)S(1)} collective-permute-done((bf16[672,256]{1,0:T(8,128)(2,1)S(1)}, bf16[672,256]{1,0:T(8,128)(2,1)S(1)}, u32[]{:S(2)}, u32[]{:S(2)}) %collective-permute-start.20) | collective-permute-done | bytes 344096 | tf_op jit(solution)/shard_map/ppermute | solution.py:151
  210.4 10.3 %collective-permute-done.21.refs_22_ = bf16[672,256]{1,0:T(8,128)(2,1)S(1)} collective-permute-done((bf16[672,256]{1,0:T(8,128)(2,1)S(1)}, bf16[672,256]{1,0:T(8,128)(2,1)S(1)}, u32[]{:S(2)}, u32[]{:S(2)}) %collective-permute-start.21) | collective-permute-done | bytes 344096 | tf_op jit(solution)/shard_map/ppermute | solution.py:151
  220.7 2.2 slice.21
  223.0 8.4 %collective-permute-done.22.refs_23_ = bf16[672,256]{1,0:T(8,128)(2,1)S(1)} collective-permute-done((bf16[672,256]{1,0:T(8,128)(2,1)S(1)}, bf16[672,256]{1,0:T(8,128)(2,1)S(1)}, u32[]{:S(2)}, u32[]{:S(2)}) %collective-permute-start.22) | collective-permute-done | bytes 344096 | tf_op jit(solution)/shard_map/ppermute | solution.py:151
  232.9 27.1 %shard_map.93 = (bf16[8,256,256]{2,1,0:T(8,128)(2,1)}, bf16[4,256,256]{2,1,0:T(8,128)(2,1)}, bf16[8,512,128]{2,1,0:T(8,128)(2,1)}) custom-call(s32[3]{0:T(128)} %pad_add_fusion.meta, f32[8,256,128]{2,1,0:T(8,128)} %get-tuple-element.28.cosine, f32[8,256,128]{2,1,0:T(8,128)} %get-tuple-element.29.sine, f32[1,128]{1,0:T(1,128)} %bitcast.22, ...), custom_call_target="tpu_custom_call" | custom-call | flops 11274289152 | bytes 22020096 | tf_op jit(solution)/shard_map/pallas_call | solution.py:452
  260.0 3.3 collective-permute-start.38
  265.3 6.0 %shard_map.94 = (bf16[4,128,256]{2,1,0:T(8,128)(2,1)}, bf16[4,128,256]{2,1,0:T(8,128)(2,1)}) custom-call(s32[3]{0:T(128)} %pad_add_fusion.meta, s32[8,256,1]{2,1,0:T(8,128)} %copy.12.q_doc, s32[12,1,256]{2,1,0:T(1,128)} %bitcast.19, bf16[8,512,128]{2,1,0:T(8,128)(2,1)} %get-tuple-element.39.queries, bf16[8,256,256]{2,1,0:T(8,128)(2,1)} %get-tuple-element.40.kv_own), custom_call_target="tpu_custom_call" | custom-call | flops 2684354560 | bytes 2097152 | tf_op jit(solution)/shard_map/pallas_call | solution.py:496
  272.6 6.9 %collective-permute-done.30.second = bf16[4,128,256]{2,1,0:T(8,128)(2,1)} collective-permute-done((bf16[4,128,256]{2,1,0:T(8,128)(2,1)}, bf16[4,128,256]{2,1,0:T(8,128)(2,1)}, u32[]{:S(2)}, u32[]{:S(2)}) %collective-permute-start.30) | collective-permute-done | bytes 262176 | tf_op jit(solution)/shard_map/ppermute | solution.py:151
  279.6 1.9 shard_map.95.refs_0_
  282.8 6.1 %shard_map.96 = (bf16[4,128,256]{2,1,0:T(8,128)(2,1)}, bf16[4,128,256]{2,1,0:T(8,128)(2,1)}) custom-call(s32[3]{0:T(128)} %pad_add_fusion.meta, s32[8,256,1]{2,1,0:T(8,128)} %copy.12.q_doc, s32[12,1,256]{2,1,0:T(1,128)} %bitcast.20, bf16[8,512,128]{2,1,0:T(8,128)(2,1)} %get-tuple-element.39.queries, bf16[8,256,256]{2,1,0:T(8,128)(2,1)} %get-tuple-element.40.kv_own, ...), custom_call_target="tpu_custom_call" | custom-call | flops 2684354560 | bytes 2097152 | tf_op jit(solution)/shard_map/pallas_call | solution.py:496
  290.1 1.9 slice.22
  292.1 1.7 collective-permute-start.32
  293.8 2.2 collective-permute-done.39.second
  296.0 1.9 shard_map.97.refs_8_
  297.9 6.8 %collective-permute-start.43 = (bf16[2,4,128,256]{3,2,1,0:T(8,128)(2,1)}, bf16[2,4,128,256]{3,2,1,0:T(8,128)(2,1)S(1)}, u32[]{:S(2)}, u32[]{:S(2)}) collective-permute-start(bf16[2,4,128,256]{3,2,1,0:T(8,128)(2,1)} %shard_map.97.refs_8_), channel_id=1, source_target_pairs={{0,8},{1,9},{2,10},{3,11},{4,12},{5,13},{6,14},{7,15},{8,0},{9,1},... | collective-permute-start | bytes 1572872 | tf_op jit(solution)/shard_map/ppermute | solution.py:151
  304.7 1.7 collective-permute-start.41
  307.0 20.1 %collective-permute-done.43.refs_12_ = bf16[2,4,128,256]{3,2,1,0:T(8,128)(2,1)S(1)} collective-permute-done((bf16[2,4,128,256]{3,2,1,0:T(8,128)(2,1)}, bf16[2,4,128,256]{3,2,1,0:T(8,128)(2,1)S(1)}, u32[]{:S(2)}, u32[]{:S(2)}) %collective-permute-start.43) | collective-permute-done | bytes 524320 | tf_op jit(solution)/shard_map/ppermute | solution.py:151
  327.1 1.7 collective-permute-start.45
  329.0 2.1 dynamic-slice_bitcast_fusion.refs_16_
  333.1 8.4 %collective-permute-done.45.refs_14_ = bf16[2,4,128,256]{3,2,1,0:T(8,128)(2,1)S(1)} collective-permute-done((bf16[2,4,128,256]{3,2,1,0:T(8,128)(2,1)S(1)}, bf16[2,4,128,256]{3,2,1,0:T(8,128)(2,1)S(1)}, u32[]{:S(2)}, u32[]{:S(2)}) %collective-permute-start.45) | collective-permute-done | bytes 524320 | tf_op jit(solution)/shard_map/ppermute | solution.py:151
  341.5 2.1 dynamic-slice_bitcast_fusion.1.refs_18_
  345.3 11.0 %shard_map.98.refs_20_ = bf16[8,128,336]{2,1,0:T(8,128)(2,1)} custom-call(s32[3]{0:T(128)} %pad_add_fusion.meta, bf16[2,4,128,256]{3,2,1,0:T(8,128)(2,1)} %shard_map.95.refs_0_, bf16[2,4,128,256]{3,2,1,0:T(8,128)(2,1)} %collective-permute-done.31.refs_1_, bf16[2,4,128,256]{3,2,1,0:T(8,128)(2,1)} %collective-permute-done.32.refs_2_, ...), custom_call_target="tpu_custom_call" | custom-call | flops 2818572288 | bytes 5505024 | tf_op jit(solution)/shard_map/pallas_call | solution.py:528
  356.3 7.5 %collective-permute-done.48.refs_19_ = bf16[144,2048]{1,0:T(8,128)(2,1)} collective-permute-done((bf16[144,2048]{1,0:T(8,128)(2,1)}, bf16[144,2048]{1,0:T(8,128)(2,1)}, u32[]{:S(2)}, u32[]{:S(2)}) %collective-permute-start.48) | collective-permute-done | bytes 589856 | tf_op jit(solution)/shard_map/ppermute | solution.py:151
  363.9 11.5 %shard_map.99 = bf16[16,128,336]{2,1,0:T(8,128)(2,1)} custom-call(s32[3]{0:T(128)} %pad_add_fusion.meta, bf16[2,4,128,256]{3,2,1,0:T(8,128)(2,1)} %shard_map.95.refs_0_, bf16[2,4,128,256]{3,2,1,0:T(8,128)(2,1)} %collective-permute-done.31.refs_1_, bf16[2,4,128,256]{3,2,1,0:T(8,128)(2,1)} %collective-permute-done.32.refs_2_, ...), custom_call_target="tpu_custom_call" | custom-call | flops 2818572288 | bytes 5505024 | tf_op jit(solution)/shard_map/pallas_call | solution.py:528
  375.3 1.9 copy.14
  377.2 23.4 %all_to_all.5 = bf16[16,128,336]{1,2,0:T(8,128)(2,1)S(1)} all-to-all(bf16[16,128,336]{1,2,0:T(8,128)(2,1)S(1)} %copy.14), channel_id=1, replica_groups=mesh['groups'=1,'half'=2,'place'=8,'cols'=2,'sub'=1] {'place','cols'}, dimensions={0} | all-to-all | bytes 2752512 | tf_op jit(solution)/shard_map/all_to_all | solution.py:544
  402.2 3.4 shard_map.100
  (167 shorter events, 35.4 us)
Async XLA Ops:
  6.5 143.8 %all-gather.7.cloned.1.call-start = ((), (), s32[]{:S(2)}) async-start(), calls=%async_computation.1 | async-start | bytes 4128768 | tf_op jit(solution)/shard_map/all_gather | solution.py:397
  8.2 7.6 %collective-permute-start = (f32[2,128]{1,0:T(2,128)S(1)}, f32[2,128]{1,0:T(2,128)S(1)}, u32[]{:S(2)}, u32[]{:S(2)}) collective-permute-start(f32[2,128]{1,0:T(2,128)S(1)} %bitcast.21), channel_id=1, source_target_pairs={{0,1},{1,0},{2,3},{3,2},{4,5},{5,4},{6,7},{7,6},{8,9},{9,8},{10,11... | collective-permute-start | bytes 3080 | tf_op jit(solution)/shard_map/ppermute | solution.py:151
  15.7 217.2 %all-gather.9.cloned.1.call-start = ((), (), s32[]{:S(2)}) async-start(), calls=%async_computation.2 | async-start | bytes 4128768 | tf_op jit(solution)/shard_map/all_gather | solution.py:443
  17.4 73.2 %collective-permute-start.8 = (bf16[256,2688]{1,0:T(8,128)(2,1)S(1)}, bf16[256,2688]{1,0:T(8,128)(2,1)}, u32[]{:S(2)}, u32[]{:S(2)}) collective-permute-start(bf16[256,2688]{1,0:T(8,128)(2,1)S(1)} %fusion.2.refs_0_), channel_id=1, source_target_pairs={{0,8},{1,9},{2,10},{3,11},{4,12},{5,13},{6,14},{7,15},{8,0},{9,1},... | collective-permute-start | bytes 4128776 | tf_op jit(solution)/shard_map/ppermute | solution.py:151
  19.1 7.3 %collective-permute-start.24 = (bf16[336,256]{1,0:T(8,128)(2,1)S(1)}, bf16[336,256]{1,0:T(8,128)(2,1)S(1)}, u32[]{:S(2)}, u32[]{:S(2)}) collective-permute-start(bf16[336,256]{1,0:T(8,128)(2,1)S(1)} %copy-done.33), channel_id=1, source_target_pairs={{0,4},{1,5},{2,6},{3,7},{4,0},{5,1},{6,2},{7,3},{8,12},{9,13},{10,... | collective-permute-start | bytes 516104 | tf_op jit(solution)/shard_map/ppermute | solution.py:151
  20.7 8.3 %collective-permute-start.25 = (bf16[336,256]{1,0:T(8,128)(2,1)S(1)}, bf16[336,256]{1,0:T(8,128)(2,1)S(1)}, u32[]{:S(2)}, u32[]{:S(2)}) collective-permute-start(bf16[336,256]{1,0:T(8,128)(2,1)S(1)} %copy-done.32), channel_id=1, source_target_pairs={{0,6},{1,7},{2,4},{3,5},{4,2},{5,3},{6,0},{7,1},{8,14},{9,15},{10,... | collective-permute-start | bytes 516104 | tf_op jit(solution)/shard_map/ppermute | solution.py:151
  20.9 61.0 %collective-permute-start.26 = (bf16[336,256]{1,0:T(8,128)(2,1)S(1)}, bf16[336,256]{1,0:T(8,128)(2,1)S(1)}, u32[]{:S(2)}, u32[]{:S(2)}) collective-permute-start(bf16[336,256]{1,0:T(8,128)(2,1)S(1)} %copy-done.31), channel_id=1, source_target_pairs={{0,8},{1,9},{2,10},{3,11},{4,12},{5,13},{6,14},{7,15},{8,0},{9,1},... | collective-permute-start | bytes 516104 | tf_op jit(solution)/shard_map/ppermute | solution.py:151
  21.4 65.1 %collective-permute-start.27 = (bf16[336,256]{1,0:T(8,128)(2,1)S(1)}, bf16[336,256]{1,0:T(8,128)(2,1)S(1)}, u32[]{:S(2)}, u32[]{:S(2)}) collective-permute-start(bf16[336,256]{1,0:T(8,128)(2,1)S(1)} %copy-done.30), channel_id=1, source_target_pairs={{0,10},{1,11},{2,8},{3,9},{4,14},{5,15},{6,12},{7,13},{8,2},{9,3},... | collective-permute-start | bytes 516104 | tf_op jit(solution)/shard_map/ppermute | solution.py:151
  26.4 64.2 %collective-permute-start.28 = (bf16[336,256]{1,0:T(8,128)(2,1)S(1)}, bf16[336,256]{1,0:T(8,128)(2,1)S(1)}, u32[]{:S(2)}, u32[]{:S(2)}) collective-permute-start(bf16[336,256]{1,0:T(8,128)(2,1)S(1)} %copy-done.29), channel_id=1, source_target_pairs={{0,12},{1,13},{2,14},{3,15},{4,8},{5,9},{6,10},{7,11},{8,4},{9,5},... | collective-permute-start | bytes 516104 | tf_op jit(solution)/shard_map/ppermute | solution.py:151
  29.0 69.0 %collective-permute-start.4 = (bf16[256,2688]{1,0:T(8,128)(2,1)S(1)}, bf16[256,2688]{1,0:T(8,128)(2,1)}, u32[]{:S(2)}, u32[]{:S(2)}) collective-permute-start(bf16[256,2688]{1,0:T(8,128)(2,1)S(1)} %fusion.2.refs_0_), channel_id=1, source_target_pairs={{0,4},{1,5},{2,6},{3,7},{4,0},{5,1},{6,2},{7,3},{8,12},{9,13},{10,... | collective-permute-start | bytes 4128776 | tf_op jit(solution)/shard_map/ppermute | solution.py:151
  81.9 33.1 %collective-permute-start.1 = (bf16[256,2688]{1,0:T(8,128)(2,1)S(1)}, bf16[256,2688]{1,0:T(8,128)(2,1)S(1)}, u32[]{:S(2)}, u32[]{:S(2)}) collective-permute-start(bf16[256,2688]{1,0:T(8,128)(2,1)S(1)} %fusion.2.refs_0_), channel_id=1, source_target_pairs={{0,1},{1,0},{2,3},{3,2},{4,5},{5,4},{6,7},{7,6},{8,9},{9,8},{10,11... | collective-permute-start | bytes 4128776 | tf_op jit(solution)/shard_map/ppermute | solution.py:151
  86.5 28.5 %collective-permute-start.2 = (bf16[256,2688]{1,0:T(8,128)(2,1)S(1)}, bf16[256,2688]{1,0:T(8,128)(2,1)S(1)}, u32[]{:S(2)}, u32[]{:S(2)}) collective-permute-start(bf16[256,2688]{1,0:T(8,128)(2,1)S(1)} %fusion.2.refs_0_), channel_id=1, source_target_pairs={{0,2},{1,3},{2,0},{3,1},{4,6},{5,7},{6,4},{7,5},{8,10},{9,11},{10,... | collective-permute-start | bytes 4128776 | tf_op jit(solution)/shard_map/ppermute | solution.py:151
  90.7 36.3 %collective-permute-start.12 = (bf16[256,2688]{1,0:T(8,128)(2,1)}, bf16[256,2688]{1,0:T(8,128)(2,1)}, u32[]{:S(2)}, u32[]{:S(2)}) collective-permute-start(bf16[256,2688]{1,0:T(8,128)(2,1)} %collective-permute-done.8.refs_8_), channel_id=1, source_target_pairs={{0,4},{1,5},{2,6},{3,7},{4,0},{5,1},{6,2},{7,3},{8,12},{9,13},{10,... | collective-permute-start | bytes 4128776 | tf_op jit(solution)/shard_map/ppermute | solution.py:151
  97.5 47.1 %collective-permute-start.9 = (bf16[256,2688]{1,0:T(8,128)(2,1)}, bf16[256,2688]{1,0:T(8,128)(2,1)}, u32[]{:S(2)}, u32[]{:S(2)}) collective-permute-start(bf16[256,2688]{1,0:T(8,128)(2,1)} %collective-permute-done.8.refs_8_), channel_id=1, source_target_pairs={{0,1},{1,0},{2,3},{3,2},{4,5},{5,4},{6,7},{7,6},{8,9},{9,8},{10,11... | collective-permute-start | bytes 4128776 | tf_op jit(solution)/shard_map/ppermute | solution.py:151
  98.0 76.0 %collective-permute-start.5 = (bf16[256,2688]{1,0:T(8,128)(2,1)}, bf16[256,2688]{1,0:T(8,128)(2,1)}, u32[]{:S(2)}, u32[]{:S(2)}) collective-permute-start(bf16[256,2688]{1,0:T(8,128)(2,1)} %collective-permute-done.4.refs_4_), channel_id=1, source_target_pairs={{0,1},{1,0},{2,3},{3,2},{4,5},{5,4},{6,7},{7,6},{8,9},{9,8},{10,11... | collective-permute-start | bytes 4128776 | tf_op jit(solution)/shard_map/ppermute | solution.py:151
  115.0 59.1 %collective-permute-start.10 = (bf16[256,2688]{1,0:T(8,128)(2,1)}, bf16[256,2688]{1,0:T(8,128)(2,1)}, u32[]{:S(2)}, u32[]{:S(2)}) collective-permute-start(bf16[256,2688]{1,0:T(8,128)(2,1)} %collective-permute-done.8.refs_8_), channel_id=1, source_target_pairs={{0,2},{1,3},{2,0},{3,1},{4,6},{5,7},{6,4},{7,5},{8,10},{9,11},{10,... | collective-permute-start | bytes 4128776 | tf_op jit(solution)/shard_map/ppermute | solution.py:151
  117.2 58.2 %collective-permute-start.6 = (bf16[256,2688]{1,0:T(8,128)(2,1)}, bf16[256,2688]{1,0:T(8,128)(2,1)}, u32[]{:S(2)}, u32[]{:S(2)}) collective-permute-start(bf16[256,2688]{1,0:T(8,128)(2,1)} %collective-permute-done.4.refs_4_), channel_id=1, source_target_pairs={{0,2},{1,3},{2,0},{3,1},{4,6},{5,7},{6,4},{7,5},{8,10},{9,11},{10,... | collective-permute-start | bytes 4128776 | tf_op jit(solution)/shard_map/ppermute | solution.py:151
  119.9 209.1 %all-gather.11.cloned.1.call-start = ((), (), s32[]{:S(2)}) async-start(), calls=%async_computation.3 | async-start | bytes 2359296 | tf_op jit(solution)/shard_map/all_gather | solution.py:487
  126.9 49.0 %collective-permute-start.3 = (bf16[256,2688]{1,0:T(8,128)(2,1)S(1)}, bf16[256,2688]{1,0:T(8,128)(2,1)S(1)}, u32[]{:S(2)}, u32[]{:S(2)}) collective-permute-start(bf16[256,2688]{1,0:T(8,128)(2,1)S(1)} %copy-done.18), channel_id=1, source_target_pairs={{0,2},{1,3},{2,0},{3,1},{4,6},{5,7},{6,4},{7,5},{8,10},{9,11},{10,... | collective-permute-start | bytes 4128776 | tf_op jit(solution)/shard_map/ppermute | solution.py:151
  144.6 52.4 %collective-permute-start.13 = (bf16[256,2688]{1,0:T(8,128)(2,1)}, bf16[256,2688]{1,0:T(8,128)(2,1)}, u32[]{:S(2)}, u32[]{:S(2)}) collective-permute-start(bf16[256,2688]{1,0:T(8,128)(2,1)} %collective-permute-done.12.refs_12_), channel_id=1, source_target_pairs={{0,1},{1,0},{2,3},{3,2},{4,5},{5,4},{6,7},{7,6},{8,9},{9,8},{10,11... | collective-permute-start | bytes 4128776 | tf_op jit(solution)/shard_map/ppermute | solution.py:151
  174.1 10.9 %collective-permute-start.17 = (bf16[672,256]{1,0:T(8,128)(2,1)S(1)}, bf16[672,256]{1,0:T(8,128)(2,1)S(1)}, u32[]{:S(2)}, u32[]{:S(2)}) collective-permute-start(bf16[672,256]{1,0:T(8,128)(2,1)S(1)} %get-tuple-element.52), channel_id=1, source_target_pairs={{0,4},{1,5},{2,6},{3,7},{4,0},{5,1},{6,2},{7,3},{8,12},{9,13},{10,... | collective-permute-start | bytes 1032200 | tf_op jit(solution)/shard_map/ppermute | solution.py:151
  175.4 16.0 %collective-permute-start.18 = (bf16[672,256]{1,0:T(8,128)(2,1)S(1)}, bf16[672,256]{1,0:T(8,128)(2,1)S(1)}, u32[]{:S(2)}, u32[]{:S(2)}) collective-permute-start(bf16[672,256]{1,0:T(8,128)(2,1)S(1)} %get-tuple-element.51), channel_id=1, source_target_pairs={{0,6},{1,7},{2,4},{3,5},{4,2},{5,3},{6,0},{7,1},{8,14},{9,15},{10,... | collective-permute-start | bytes 1032200 | tf_op jit(solution)/shard_map/ppermute | solution.py:151
  175.9 23.6 %collective-permute-start.19 = (bf16[672,256]{1,0:T(8,128)(2,1)S(1)}, bf16[672,256]{1,0:T(8,128)(2,1)S(1)}, u32[]{:S(2)}, u32[]{:S(2)}) collective-permute-start(bf16[672,256]{1,0:T(8,128)(2,1)S(1)} %get-tuple-element.50), channel_id=1, source_target_pairs={{0,8},{1,9},{2,10},{3,11},{4,12},{5,13},{6,14},{7,15},{8,0},{9,1},... | collective-permute-start | bytes 1032200 | tf_op jit(solution)/shard_map/ppermute | solution.py:151
  178.4 54.4 %collective-permute-start.14 = (bf16[256,2688]{1,0:T(8,128)(2,1)}, bf16[256,2688]{1,0:T(8,128)(2,1)}, u32[]{:S(2)}, u32[]{:S(2)}) collective-permute-start(bf16[256,2688]{1,0:T(8,128)(2,1)} %collective-permute-done.12.refs_12_), channel_id=1, source_target_pairs={{0,2},{1,3},{2,0},{3,1},{4,6},{5,7},{6,4},{7,5},{8,10},{9,11},{10,... | collective-permute-start | bytes 4128776 | tf_op jit(solution)/shard_map/ppermute | solution.py:151
  185.0 47.9 %collective-permute-start.11 = (bf16[256,2688]{1,0:T(8,128)(2,1)}, bf16[256,2688]{1,0:T(8,128)(2,1)}, u32[]{:S(2)}, u32[]{:S(2)}) collective-permute-start(bf16[256,2688]{1,0:T(8,128)(2,1)} %collective-permute-done.9.refs_9_), channel_id=1, source_target_pairs={{0,2},{1,3},{2,0},{3,1},{4,6},{5,7},{6,4},{7,5},{8,10},{9,11},{10,... | collective-permute-start | bytes 4128776 | tf_op jit(solution)/shard_map/ppermute | solution.py:151
  191.5 41.4 %collective-permute-start.7 = (bf16[256,2688]{1,0:T(8,128)(2,1)}, bf16[256,2688]{1,0:T(8,128)(2,1)}, u32[]{:S(2)}, u32[]{:S(2)}) collective-permute-start(bf16[256,2688]{1,0:T(8,128)(2,1)} %collective-permute-done.5.refs_5_), channel_id=1, source_target_pairs={{0,2},{1,3},{2,0},{3,1},{4,6},{5,7},{6,4},{7,5},{8,10},{9,11},{10,... | collective-permute-start | bytes 4128776 | tf_op jit(solution)/shard_map/ppermute | solution.py:151
  197.0 35.9 %collective-permute-start.15 = (bf16[256,2688]{1,0:T(8,128)(2,1)}, bf16[256,2688]{1,0:T(8,128)(2,1)}, u32[]{:S(2)}, u32[]{:S(2)}) collective-permute-start(bf16[256,2688]{1,0:T(8,128)(2,1)} %collective-permute-done.13.refs_13_), channel_id=1, source_target_pairs={{0,2},{1,3},{2,0},{3,1},{4,6},{5,7},{6,4},{7,5},{8,10},{9,11},{10,... | collective-permute-start | bytes 4128776 | tf_op jit(solution)/shard_map/ppermute | solution.py:151
  199.6 10.1 %collective-permute-start.20 = (bf16[672,256]{1,0:T(8,128)(2,1)S(1)}, bf16[672,256]{1,0:T(8,128)(2,1)S(1)}, u32[]{:S(2)}, u32[]{:S(2)}) collective-permute-start(bf16[672,256]{1,0:T(8,128)(2,1)S(1)} %get-tuple-element.49), channel_id=1, source_target_pairs={{0,10},{1,11},{2,8},{3,9},{4,14},{5,15},{6,12},{7,13},{8,2},{9,3},... | collective-permute-start | bytes 1032200 | tf_op jit(solution)/shard_map/ppermute | solution.py:151
  209.7 11.0 %collective-permute-start.21 = (bf16[672,256]{1,0:T(8,128)(2,1)S(1)}, bf16[672,256]{1,0:T(8,128)(2,1)S(1)}, u32[]{:S(2)}, u32[]{:S(2)}) collective-permute-start(bf16[672,256]{1,0:T(8,128)(2,1)S(1)} %get-tuple-element.48), channel_id=1, source_target_pairs={{0,12},{1,13},{2,14},{3,15},{4,8},{5,9},{6,10},{7,11},{8,4},{9,5},... | collective-permute-start | bytes 1032200 | tf_op jit(solution)/shard_map/ppermute | solution.py:151
  220.7 10.7 %collective-permute-start.22 = (bf16[672,256]{1,0:T(8,128)(2,1)S(1)}, bf16[672,256]{1,0:T(8,128)(2,1)S(1)}, u32[]{:S(2)}, u32[]{:S(2)}) collective-permute-start(bf16[672,256]{1,0:T(8,128)(2,1)S(1)} %get-tuple-element.47), channel_id=1, source_target_pairs={{0,14},{1,15},{2,12},{3,13},{4,10},{5,11},{6,8},{7,9},{8,6},{9,7},... | collective-permute-start | bytes 1032200 | tf_op jit(solution)/shard_map/ppermute | solution.py:151
  223.0 118.5 %all-gather.13.cloned.1.call-start = ((), (), s32[]{:S(2)}) async-start(), calls=%async_computation.4 | async-start | bytes 1769472 | tf_op jit(solution)/shard_map/all_gather | solution.py:487
  231.4 73.3 %collective-permute-start.49 = (bf16[336,2048]{1,0:T(8,128)(2,1)}, bf16[336,2048]{1,0:T(8,128)(2,1)}, u32[]{:S(2)}, u32[]{:S(2)}) collective-permute-start(bf16[336,2048]{1,0:T(8,128)(2,1)} %bitcast.8.refs_16_), channel_id=1, source_target_pairs={{0,1},{1,0},{2,3},{3,2},{4,5},{5,4},{6,7},{7,6},{8,9},{9,8},{10,11... | collective-permute-start | bytes 4128776 | tf_op jit(solution)/shard_map/ppermute | solution.py:151
  260.0 22.8 %collective-permute-start.38 = (bf16[4,256,256]{2,1,0:T(8,128)(2,1)}, bf16[4,256,256]{2,1,0:T(8,128)(2,1)}, u32[]{:S(2)}, u32[]{:S(2)}) collective-permute-start(bf16[4,256,256]{2,1,0:T(8,128)(2,1)} %get-tuple-element.43), channel_id=1, source_target_pairs={{0,16},{1,17},{2,18},{3,19},{4,20},{5,21},{6,22},{7,23},{8,24},{9,... | collective-permute-start | bytes 1572872 | tf_op jit(solution)/shard_map/ppermute | solution.py:480
  271.3 8.3 %collective-permute-start.30 = (bf16[4,128,256]{2,1,0:T(8,128)(2,1)}, bf16[4,128,256]{2,1,0:T(8,128)(2,1)}, u32[]{:S(2)}, u32[]{:S(2)}) collective-permute-start(bf16[4,128,256]{2,1,0:T(8,128)(2,1)} %get-tuple-element.42), channel_id=1, source_target_pairs={{0,1},{1,0},{2,3},{3,2},{4,5},{5,4},{6,7},{7,6},{8,9},{9,8},{10,11... | collective-permute-start | bytes 786440 | tf_op jit(solution)/shard_map/ppermute | solution.py:151
  281.4 24.9 %collective-permute-start.34 = (bf16[2,4,128,256]{3,2,1,0:T(8,128)(2,1)}, bf16[2,4,128,256]{3,2,1,0:T(8,128)(2,1)}, u32[]{:S(2)}, u32[]{:S(2)}) collective-permute-start(bf16[2,4,128,256]{3,2,1,0:T(8,128)(2,1)} %shard_map.95.refs_0_), channel_id=1, source_target_pairs={{0,8},{1,9},{2,10},{3,11},{4,12},{5,13},{6,14},{7,15},{8,0},{9,1},... | collective-permute-start | bytes 1572872 | tf_op jit(solution)/shard_map/ppermute | solution.py:151
  292.1 14.3 %collective-permute-start.32 = (bf16[2,4,128,256]{3,2,1,0:T(8,128)(2,1)}, bf16[2,4,128,256]{3,2,1,0:T(8,128)(2,1)}, u32[]{:S(2)}, u32[]{:S(2)}) collective-permute-start(bf16[2,4,128,256]{3,2,1,0:T(8,128)(2,1)} %shard_map.95.refs_0_), channel_id=1, source_target_pairs={{0,4},{1,5},{2,6},{3,7},{4,0},{5,1},{6,2},{7,3},{8,12},{9,13},{10,... | collective-permute-start | bytes 1572872 | tf_op jit(solution)/shard_map/ppermute | solution.py:151
  293.8 13.0 %collective-permute-start.31 = (bf16[2,4,128,256]{3,2,1,0:T(8,128)(2,1)}, bf16[2,4,128,256]{3,2,1,0:T(8,128)(2,1)}, u32[]{:S(2)}, u32[]{:S(2)}) collective-permute-start(bf16[2,4,128,256]{3,2,1,0:T(8,128)(2,1)} %shard_map.95.refs_0_), channel_id=1, source_target_pairs={{0,2},{1,3},{2,0},{3,1},{4,6},{5,7},{6,4},{7,5},{8,10},{9,11},{10,... | collective-permute-start | bytes 1572872 | tf_op jit(solution)/shard_map/ppermute | solution.py:151
  297.9 29.3 %collective-permute-start.43 = (bf16[2,4,128,256]{3,2,1,0:T(8,128)(2,1)}, bf16[2,4,128,256]{3,2,1,0:T(8,128)(2,1)S(1)}, u32[]{:S(2)}, u32[]{:S(2)}) collective-permute-start(bf16[2,4,128,256]{3,2,1,0:T(8,128)(2,1)} %shard_map.97.refs_8_), channel_id=1, source_target_pairs={{0,8},{1,9},{2,10},{3,11},{4,12},{5,13},{6,14},{7,15},{8,0},{9,1},... | collective-permute-start | bytes 1572872 | tf_op jit(solution)/shard_map/ppermute | solution.py:151
  304.7 22.4 %collective-permute-start.41 = (bf16[2,4,128,256]{3,2,1,0:T(8,128)(2,1)}, bf16[2,4,128,256]{3,2,1,0:T(8,128)(2,1)S(1)}, u32[]{:S(2)}, u32[]{:S(2)}) collective-permute-start(bf16[2,4,128,256]{3,2,1,0:T(8,128)(2,1)} %shard_map.97.refs_8_), channel_id=1, source_target_pairs={{0,4},{1,5},{2,6},{3,7},{4,0},{5,1},{6,2},{7,3},{8,12},{9,13},{10,... | collective-permute-start | bytes 1572872 | tf_op jit(solution)/shard_map/ppermute | solution.py:151
  306.4 22.5 %collective-permute-start.40 = (bf16[2,4,128,256]{3,2,1,0:T(8,128)(2,1)}, bf16[2,4,128,256]{3,2,1,0:T(8,128)(2,1)}, u32[]{:S(2)}, u32[]{:S(2)}) collective-permute-start(bf16[2,4,128,256]{3,2,1,0:T(8,128)(2,1)} %shard_map.97.refs_8_), channel_id=1, source_target_pairs={{0,2},{1,3},{2,0},{3,1},{4,6},{5,7},{6,4},{7,5},{8,10},{9,11},{10,... | collective-permute-start | bytes 1572872 | tf_op jit(solution)/shard_map/ppermute | solution.py:151
  306.4 24.7 %collective-permute-start.36 = (bf16[2,4,128,256]{3,2,1,0:T(8,128)(2,1)}, bf16[2,4,128,256]{3,2,1,0:T(8,128)(2,1)S(1)}, u32[]{:S(2)}, u32[]{:S(2)}) collective-permute-start(bf16[2,4,128,256]{3,2,1,0:T(8,128)(2,1)} %collective-permute-done.34.refs_4_), channel_id=1, source_target_pairs={{0,4},{1,5},{2,6},{3,7},{4,0},{5,1},{6,2},{7,3},{8,12},{9,13},{10,... | collective-permute-start | bytes 1572872 | tf_op jit(solution)/shard_map/ppermute | solution.py:151
  306.8 25.8 %collective-permute-start.33 = (bf16[2,4,128,256]{3,2,1,0:T(8,128)(2,1)}, bf16[2,4,128,256]{3,2,1,0:T(8,128)(2,1)S(1)}, u32[]{:S(2)}, u32[]{:S(2)}) collective-permute-start(bf16[2,4,128,256]{3,2,1,0:T(8,128)(2,1)} %collective-permute-done.32.refs_2_), channel_id=1, source_target_pairs={{0,2},{1,3},{2,0},{3,1},{4,6},{5,7},{6,4},{7,5},{8,10},{9,11},{10,... | collective-permute-start | bytes 1572872 | tf_op jit(solution)/shard_map/ppermute | solution.py:151
  327.1 14.3 %collective-permute-start.45 = (bf16[2,4,128,256]{3,2,1,0:T(8,128)(2,1)S(1)}, bf16[2,4,128,256]{3,2,1,0:T(8,128)(2,1)S(1)}, u32[]{:S(2)}, u32[]{:S(2)}) collective-permute-start(bf16[2,4,128,256]{3,2,1,0:T(8,128)(2,1)S(1)} %collective-permute-done.43.refs_12_), channel_id=1, source_target_pairs={{0,4},{1,5},{2,6},{3,7},{4,0},{5,1},{6,2},{7,3},{8,12},{9,13},{10,... | collective-permute-start | bytes 1572872 | tf_op jit(solution)/shard_map/ppermute | solution.py:151
  328.8 14.8 %collective-permute-start.42 = (bf16[2,4,128,256]{3,2,1,0:T(8,128)(2,1)S(1)}, bf16[2,4,128,256]{3,2,1,0:T(8,128)(2,1)}, u32[]{:S(2)}, u32[]{:S(2)}) collective-permute-start(bf16[2,4,128,256]{3,2,1,0:T(8,128)(2,1)S(1)} %collective-permute-done.41.refs_10_), channel_id=1, source_target_pairs={{0,2},{1,3},{2,0},{3,1},{4,6},{5,7},{6,4},{7,5},{8,10},{9,11},{10,... | collective-permute-start | bytes 1572872 | tf_op jit(solution)/shard_map/ppermute | solution.py:151
  331.1 32.8 %collective-permute-start.47 = (bf16[192,2048]{1,0:T(8,128)(2,1)}, bf16[192,2048]{1,0:T(8,128)(2,1)}, u32[]{:S(2)}, u32[]{:S(2)}) collective-permute-start(bf16[192,2048]{1,0:T(8,128)(2,1)} %dynamic-slice_bitcast_fusion.refs_16_), channel_id=1, source_target_pairs={{0,1},{1,0},{2,3},{3,2},{4,5},{5,4},{6,7},{7,6},{8,9},{9,8},{10,11... | collective-permute-start | bytes 2359304 | tf_op jit(solution)/shard_map/ppermute | solution.py:151
  332.6 12.7 %collective-permute-start.44 = (bf16[2,4,128,256]{3,2,1,0:T(8,128)(2,1)S(1)}, bf16[2,4,128,256]{3,2,1,0:T(8,128)(2,1)}, u32[]{:S(2)}, u32[]{:S(2)}) collective-permute-start(bf16[2,4,128,256]{3,2,1,0:T(8,128)(2,1)S(1)} %collective-permute-done.43.refs_12_), channel_id=1, source_target_pairs={{0,2},{1,3},{2,0},{3,1},{4,6},{5,7},{6,4},{7,5},{8,10},{9,11},{10,... | collective-permute-start | bytes 1572872 | tf_op jit(solution)/shard_map/ppermute | solution.py:151
  332.7 12.6 %collective-permute-start.37 = (bf16[2,4,128,256]{3,2,1,0:T(8,128)(2,1)S(1)}, bf16[2,4,128,256]{3,2,1,0:T(8,128)(2,1)}, u32[]{:S(2)}, u32[]{:S(2)}) collective-permute-start(bf16[2,4,128,256]{3,2,1,0:T(8,128)(2,1)S(1)} %collective-permute-done.36.refs_6_), channel_id=1, source_target_pairs={{0,2},{1,3},{2,0},{3,1},{4,6},{5,7},{6,4},{7,5},{8,10},{9,11},{10,... | collective-permute-start | bytes 1572872 | tf_op jit(solution)/shard_map/ppermute | solution.py:151
  343.6 20.2 %collective-permute-start.48 = (bf16[144,2048]{1,0:T(8,128)(2,1)}, bf16[144,2048]{1,0:T(8,128)(2,1)}, u32[]{:S(2)}, u32[]{:S(2)}) collective-permute-start(bf16[144,2048]{1,0:T(8,128)(2,1)} %dynamic-slice_bitcast_fusion.1.refs_18_), channel_id=1, source_target_pairs={{0,1},{1,0},{2,3},{3,2},{4,5},{5,4},{6,7},{7,6},{8,9},{9,8},{10,11... | collective-permute-start | bytes 1769480 | tf_op jit(solution)/shard_map/ppermute | solution.py:151
  (41 other events, 1006.0 us)
Sparse Core Ops, SparseCore 0:
  15.8 70.2 all-gather.6
  120.0 72.4 all-gather.8
  223.1 44.1 all-gather.10
  292.2 41.6 all-gather.12

commit v4 on v3

--- a/solution.py
+++ b/solution.py
@@ -199,7 +199,7 @@
     kv_out, tail_out, q_out = refs[3 * n + 1 : 3 * n + 4]
     block_mem, kv_mem, q_mem, block_sem, weight_sem = refs[3 * n + 4 :]
     place, col = meta[0], meta[2]
-    _, _, tokens, features = block_mem.shape
+    _, _, tokens, _ = block_mem.shape
     deep = kv_parts[0].shape[0] // 2
     copies = []
     for m in range(n):
@@ -213,49 +213,59 @@
             ):
                 sem = weight_sem.at[4 * m + 2 * half + k]
                 copies.append(pltpu.make_async_copy(source, target, sem))
+
+    def loads(m):
+        return [
+            pltpu.make_async_copy(blocks[m * 2 + side], block_mem.at[side, m], block_sem.at[m, side])
+            for side in range(2)
+        ]
+
+    ahead = 1
     for copy in copies:
         copy.start()
-    for m in range(n):
-        for side in range(2):
-            pltpu.make_async_copy(
-                blocks[m * 2 + side], block_mem.at[side, m], block_sem.at[m, side]
-            ).start()
+    for m in range(ahead):
+        for copy in loads(m):
+            copy.start()
     for copy in copies:
         copy.wait()
 
-    @pl.loop(0, n // 2)
+    @pl.loop(0, n)
     def _(t):
-        for m in range(2):
-            for side in range(2):
-                pltpu.make_async_copy(
-                    blocks[side], block_mem.at[side, 2 * t + m], block_sem.at[2 * t + m, side]
-                ).wait()
-        mine = block_mem[0, pl.ds(2 * t, 2)].reshape(2 * tokens, features)
-        theirs = block_mem[1, pl.ds(2 * t, 2)].reshape(2 * tokens, features)
-        kv_two, q_two = [
-            jnp.dot(mine, mem[col], preferred_element_type=jnp.float32)
-            + jnp.dot(theirs, mem[lax.bitwise_xor(col, 1)], preferred_element_type=jnp.float32)
+        for m in range(ahead, n):
+
+            @pl.when(t == m - ahead)
+            def _():
+                for copy in loads(m):
+                    copy.start()
+
+        for side in range(2):
+            pltpu.make_async_copy(blocks[side], block_mem.at[side, t], block_sem.at[t, side]).wait()
+        kv, q = [
+            jnp.dot(block_mem[0, t], mem[col], preferred_element_type=jnp.float32)
+            + jnp.dot(
+                block_mem[1, t],
+                mem[lax.bitwise_xor(col, 1)],
+                preferred_element_type=jnp.float32,
+            )
             for mem in (kv_mem, q_mem)
         ]
-        for m in range(2):
-            slot = 2 * t + m
-            at = lax.bitwise_xor(place, slot)
-            raw = kv_two[m * tokens : (m + 1) * tokens]
-            cosine_here, sine_here = cosine[at], sine[at]
-            keys = normed_rotated(raw[:, :HD], key_gain[...], cosine_here, sine_here)
-            keys = keys.astype(jnp.bfloat16)
-            values = raw[:, HD : 2 * HD].astype(jnp.bfloat16)
-            kv_out[at, :, :HD] = keys
-            kv_out[at, :, HD:] = values
-            for h in range(heads):
-                query = q_two[m * tokens : (m + 1) * tokens, h * HD : (h + 1) * HD]
-                query = normed_rotated(query, query_gain[...], cosine_here, sine_here)
-                q_out[at, pl.ds(h * tokens, tokens), :] = query.astype(jnp.bfloat16)
-
-            @pl.when(at >= n - reach)
-            def _():
-                tail_out[at - (n - reach), :, :HD] = keys
-                tail_out[at - (n - reach), :, HD:] = values
+        at = lax.bitwise_xor(place, t)
+        cosine_here, sine_here = cosine[at], sine[at]
+        keys = normed_rotated(kv[:, :HD], key_gain[...], cosine_here, sine_here)
+        keys = keys.astype(jnp.bfloat16)
+        values = kv[:, HD : 2 * HD].astype(jnp.bfloat16)
+        kv_out[at, :, :HD] = keys
+        kv_out[at, :, HD:] = values
+        for h in range(heads):
+            query = normed_rotated(
+                q[:, h * HD : (h + 1) * HD], query_gain[...], cosine_here, sine_here
+            )
+            q_out[at, pl.ds(h * tokens, tokens), :] = query.astype(jnp.bfloat16)
+
+        @pl.when(at >= n - reach)
+        def _():
+            tail_out[at - (n - reach), :, :HD] = keys
+            tail_out[at - (n - reach), :, HD:] = values
 
 
 def attend_kernel(low, count, reach, heads, meta, q_doc, k_doc, queries, kv_own, *refs):
@@ -320,11 +330,13 @@
                 weight_sem.at[k],
             )
         )
+    loads = []
     for s, (low, size) in enumerate(spans):
+        loads.append([])
         for m in range(n):
             for side in range(2):
                 first = lax.bitwise_xor(col, side) * deep + lax.bitwise_xor(place, m) * wide
-                copies.append(
+                loads[s].append(
                     pltpu.make_async_copy(
                         contexts[s * n + m].at[side],
                         context_mem.at[
@@ -333,24 +345,27 @@
                         context_sem.at[(s * n + m) * 2 + side],
                     )
                 )
-    for copy in copies:
+    for copy in copies + loads[0]:
         copy.start()
     for copy in copies:
         copy.wait()
-
-    @pl.loop(0, n // 4)
-    def _(t):
-        left = context_mem[pl.ds(4 * t, 4)].reshape(4 * part, 2 * deep)
+    for s, (low, size) in enumerate(spans):
+        for copy in loads[s]:
+            copy.wait()
+        if s + 1 < len(spans):
+            for copy in loads[s + 1]:
+                copy.start()
+        left = context_mem[low : low + size].reshape(size * part, 2 * deep)
         result = lax.dot_general(
             left, weight_mem[...], (((1,), (1,)), ((), ())), preferred_element_type=jnp.float32
         ).astype(jnp.bfloat16)
-        for k in range(4):
+        for k in range(size):
             slab = result[k * part : (k + 1) * part]
             if far:
-                out[2 * (4 * t + k) + lax.bitwise_xor(half, 1)] = slab
-                out[2 * (4 * t + k) + half] = before[4 * t + k]
+                out[2 * (low + k) + lax.bitwise_xor(half, 1)] = slab
+                out[2 * (low + k) + half] = before[low + k]
             else:
-                out[4 * t + k] = slab
+                out[low + k] = slab
 
 
 def close_kernel(n, activations, arrived, out):

time: 413 us -> 412 us (level)
  Pallas kernels: 75.2 us -> 68 us
  starting transfers between devices: 46.8 us -> 51.6 us
    pallas_call x1, Pallas kernels: 27.1 us -> 22.3 us  [split_body(): run(functools.partial(project_kernel, n, reach, heads), [shaped((n, token...]
    ppermute x49, starting transfers between devices: 43.4 us -> 48.2 us  [swapped(): return lax.ppermute(value, ('place', 'cols'), pairs)]
  transfers between devices with their start and end apart: 54 -> 54, of which waited for: 22 -> 22; matrix products, arithmetic and copies ran while one was open for 5% -> 5% of each run, Pallas kernels for 15% -> 13%
where the time goes in v4:
time: 412 us; the launch traced here: 411 us
  waiting for transfers between devices  226 us (55%)
  Pallas kernels  68 us (17%)
  starting transfers between devices  51.6 us (13%)
  blocking collectives  23.4 us (6%)
  local copies, waits for them, and re-layouts  20 us (5%)
  between operations  13.6 us (3%)
  other arithmetic  8.34 us (2%)
    ppermute x49, waiting for transfers between devices, swapped(): return lax.ppermute(value, ('place', 'cols'), pairs)  226 us
    ppermute x49, starting transfers between devices, swapped(): return lax.ppermute(value, ('place', 'cols'), pairs)  48.2 us
    all_to_all x1, blocking collectives, split_body(): arrived = lax.all_to_all(result[0], ('place', 'cols'), 0, 0, tiled=True)  23.4 us
    pallas_call x1, Pallas kernels, split_body(): run(functools.partial(project_kernel, n, reach, heads), [shaped((n, token...  22.3 us
    pallas_call x2, Pallas kernels, split_body(): run(functools.partial(output_kernel, n, spans, len(result)), shaped((*sha...  20.1 us
    pallas_call x2, Pallas kernels, split_body(): run(functools.partial(attend_kernel, low, count, reach, heads), [shape, s...  12.1 us
  transfers between devices with their start and end apart: 54, of which 22 were waited for; matrix products, arithmetic and copies ran while one was open for 5% of the time, Pallas kernels for 13%

profile of v4, /device:TPU:0, one launch (start us, length us, event | category | flops | bytes accessed | tf_op | source)
XLA Modules:
  0.0 411.2 jit_solution(15761769892069056331)
XLA Ops:
  6.5 1.7 fusion
  8.2 3.0 collective-permute-start
  11.9 3.8 shard_map.91
  22.7 3.7 collective-permute-done.24.refs_2_
  30.6 51.4 %collective-permute-done.26.refs_4_ = bf16[336,256]{1,0:T(8,128)(2,1)S(1)} collective-permute-done((bf16[336,256]{1,0:T(8,128)(2,1)S(1)}, bf16[336,256]{1,0:T(8,128)(2,1)S(1)}, u32[]{:S(2)}, u32[]{:S(2)}) %collective-permute-start.26) | collective-permute-done | bytes 172064 | tf_op jit(solution)/shard_map/ppermute | solution.py:151
  81.9 4.6 %collective-permute-done.27.refs_5_ = bf16[336,256]{1,0:T(8,128)(2,1)S(1)} collective-permute-done((bf16[336,256]{1,0:T(8,128)(2,1)S(1)}, bf16[336,256]{1,0:T(8,128)(2,1)S(1)}, u32[]{:S(2)}, u32[]{:S(2)}) %collective-permute-start.27) | collective-permute-done | bytes 172064 | tf_op jit(solution)/shard_map/ppermute | solution.py:151
  87.5 3.1 collective-permute-done.28.refs_6_
  92.0 5.5 %collective-permute-done.29.refs_7_ = bf16[336,256]{1,0:T(8,128)(2,1)S(1)} collective-permute-done((bf16[336,256]{1,0:T(8,128)(2,1)S(1)}, bf16[336,256]{1,0:T(8,128)(2,1)S(1)}, u32[]{:S(2)}, u32[]{:S(2)}) %collective-permute-start.29) | collective-permute-done | bytes 172064 | tf_op jit(solution)/shard_map/ppermute | solution.py:151
  99.5 15.5 %collective-permute-done.1.refs_1_ = bf16[256,2688]{1,0:T(8,128)(2,1)S(1)} collective-permute-done((bf16[256,2688]{1,0:T(8,128)(2,1)S(1)}, bf16[256,2688]{1,0:T(8,128)(2,1)S(1)}, u32[]{:S(2)}, u32[]{:S(2)}) %collective-permute-start.1) | collective-permute-done | bytes 1376288 | tf_op jit(solution)/shard_map/ppermute | solution.py:151
  117.2 2.7 shard_map.92
  120.0 7.0 %collective-permute-done.12.refs_12_ = bf16[256,2688]{1,0:T(8,128)(2,1)} collective-permute-done((bf16[256,2688]{1,0:T(8,128)(2,1)}, bf16[256,2688]{1,0:T(8,128)(2,1)}, u32[]{:S(2)}, u32[]{:S(2)}) %collective-permute-start.12) | collective-permute-done | bytes 1376288 | tf_op jit(solution)/shard_map/ppermute | solution.py:151
  127.1 17.5 %collective-permute-done.9.refs_9_ = bf16[256,2688]{1,0:T(8,128)(2,1)} collective-permute-done((bf16[256,2688]{1,0:T(8,128)(2,1)}, bf16[256,2688]{1,0:T(8,128)(2,1)}, u32[]{:S(2)}, u32[]{:S(2)}) %collective-permute-start.9) | collective-permute-done | bytes 1376288 | tf_op jit(solution)/shard_map/ppermute | solution.py:151
  144.7 3.7 fusion.3
  148.4 1.9 pad_maximum_fusion
  150.3 2.6 constant_dynamic-slice_fusion
  152.9 21.1 %collective-permute-done.5.refs_5_ = bf16[256,2688]{1,0:T(8,128)(2,1)} collective-permute-done((bf16[256,2688]{1,0:T(8,128)(2,1)}, bf16[256,2688]{1,0:T(8,128)(2,1)}, u32[]{:S(2)}, u32[]{:S(2)}) %collective-permute-start.5) | collective-permute-done | bytes 1376288 | tf_op jit(solution)/shard_map/ppermute | solution.py:151
  175.9 2.5 collective-permute-start.19
  178.4 6.6 %collective-permute-done.17.refs_18_ = bf16[672,256]{1,0:T(8,128)(2,1)S(1)} collective-permute-done((bf16[672,256]{1,0:T(8,128)(2,1)S(1)}, bf16[672,256]{1,0:T(8,128)(2,1)S(1)}, u32[]{:S(2)}, u32[]{:S(2)}) %collective-permute-start.17) | collective-permute-done | bytes 344096 | tf_op jit(solution)/shard_map/ppermute | solution.py:151
  185.0 6.4 %collective-permute-done.18.refs_19_ = bf16[672,256]{1,0:T(8,128)(2,1)S(1)} collective-permute-done((bf16[672,256]{1,0:T(8,128)(2,1)S(1)}, bf16[672,256]{1,0:T(8,128)(2,1)S(1)}, u32[]{:S(2)}, u32[]{:S(2)}) %collective-permute-start.18) | collective-permute-done | bytes 344096 | tf_op jit(solution)/shard_map/ppermute | solution.py:151
  192.1 4.9 %collective-permute-done.13.refs_13_ = bf16[256,2688]{1,0:T(8,128)(2,1)} collective-permute-done((bf16[256,2688]{1,0:T(8,128)(2,1)}, bf16[256,2688]{1,0:T(8,128)(2,1)}, u32[]{:S(2)}, u32[]{:S(2)}) %collective-permute-start.13) | collective-permute-done | bytes 1376288 | tf_op jit(solution)/shard_map/ppermute | solution.py:151
  197.0 2.6 collective-permute-done.19.refs_20_
  199.7 10.0 %collective-permute-done.20.refs_21_ = bf16[672,256]{1,0:T(8,128)(2,1)S(1)} collective-permute-done((bf16[672,256]{1,0:T(8,128)(2,1)S(1)}, bf16[672,256]{1,0:T(8,128)(2,1)S(1)}, u32[]{:S(2)}, u32[]{:S(2)}) %collective-permute-start.20) | collective-permute-done | bytes 344096 | tf_op jit(solution)/shard_map/ppermute | solution.py:151
  210.4 10.3 %collective-permute-done.21.refs_22_ = bf16[672,256]{1,0:T(8,128)(2,1)S(1)} collective-permute-done((bf16[672,256]{1,0:T(8,128)(2,1)S(1)}, bf16[672,256]{1,0:T(8,128)(2,1)S(1)}, u32[]{:S(2)}, u32[]{:S(2)}) %collective-permute-start.21) | collective-permute-done | bytes 344096 | tf_op jit(solution)/shard_map/ppermute | solution.py:151
  220.7 2.2 slice.21
  223.0 8.4 %collective-permute-done.22.refs_23_ = bf16[672,256]{1,0:T(8,128)(2,1)S(1)} collective-permute-done((bf16[672,256]{1,0:T(8,128)(2,1)S(1)}, bf16[672,256]{1,0:T(8,128)(2,1)S(1)}, u32[]{:S(2)}, u32[]{:S(2)}) %collective-permute-start.22) | collective-permute-done | bytes 344096 | tf_op jit(solution)/shard_map/ppermute | solution.py:151
  232.9 22.3 %shard_map.93 = (bf16[8,256,256]{2,1,0:T(8,128)(2,1)}, bf16[4,256,256]{2,1,0:T(8,128)(2,1)}, bf16[8,512,128]{2,1,0:T(8,128)(2,1)}) custom-call(s32[3]{0:T(128)} %pad_add_fusion.meta, f32[8,256,128]{2,1,0:T(8,128)} %get-tuple-element.28.cosine, f32[8,256,128]{2,1,0:T(8,128)} %get-tuple-element.29.sine, f32[1,128]{1,0:T(1,128)} %bitcast.22, ...), custom_call_target="tpu_custom_call" | custom-call | flops 11274289152 | bytes 22020096 | tf_op jit(solution)/shard_map/pallas_call | solution.py:467
  255.2 3.3 collective-permute-start.38
  260.5 6.0 %shard_map.94 = (bf16[4,128,256]{2,1,0:T(8,128)(2,1)}, bf16[4,128,256]{2,1,0:T(8,128)(2,1)}) custom-call(s32[3]{0:T(128)} %pad_add_fusion.meta, s32[8,256,1]{2,1,0:T(8,128)} %copy.12.q_doc, s32[12,1,256]{2,1,0:T(1,128)} %bitcast.19, bf16[8,512,128]{2,1,0:T(8,128)(2,1)} %get-tuple-element.39.queries, bf16[8,256,256]{2,1,0:T(8,128)(2,1)} %get-tuple-element.40.kv_own), custom_call_target="tpu_custom_call" | custom-call | flops 2684354560 | bytes 2097152 | tf_op jit(solution)/shard_map/pallas_call | solution.py:511
  267.8 6.9 %collective-permute-done.30.second = bf16[4,128,256]{2,1,0:T(8,128)(2,1)} collective-permute-done((bf16[4,128,256]{2,1,0:T(8,128)(2,1)}, bf16[4,128,256]{2,1,0:T(8,128)(2,1)}, u32[]{:S(2)}, u32[]{:S(2)}) %collective-permute-start.30) | collective-permute-done | bytes 262176 | tf_op jit(solution)/shard_map/ppermute | solution.py:151
  274.7 1.9 shard_map.95.refs_0_
  278.0 6.1 %shard_map.96 = (bf16[4,128,256]{2,1,0:T(8,128)(2,1)}, bf16[4,128,256]{2,1,0:T(8,128)(2,1)}) custom-call(s32[3]{0:T(128)} %pad_add_fusion.meta, s32[8,256,1]{2,1,0:T(8,128)} %copy.12.q_doc, s32[12,1,256]{2,1,0:T(1,128)} %bitcast.20, bf16[8,512,128]{2,1,0:T(8,128)(2,1)} %get-tuple-element.39.queries, bf16[8,256,256]{2,1,0:T(8,128)(2,1)} %get-tuple-element.40.kv_own, ...), custom_call_target="tpu_custom_call" | custom-call | flops 2684354560 | bytes 2097152 | tf_op jit(solution)/shard_map/pallas_call | solution.py:511
  285.3 1.9 slice.22
  287.2 1.7 collective-permute-start.32
  289.0 2.2 collective-permute-done.39.second
  291.1 1.9 shard_map.97.refs_8_
  293.0 11.7 %collective-permute-start.43 = (bf16[2,4,128,256]{3,2,1,0:T(8,128)(2,1)}, bf16[2,4,128,256]{3,2,1,0:T(8,128)(2,1)S(1)}, u32[]{:S(2)}, u32[]{:S(2)}) collective-permute-start(bf16[2,4,128,256]{3,2,1,0:T(8,128)(2,1)} %shard_map.97.refs_8_), channel_id=1, source_target_pairs={{0,8},{1,9},{2,10},{3,11},{4,12},{5,13},{6,14},{7,15},{8,0},{9,1},... | collective-permute-start | bytes 1572872 | tf_op jit(solution)/shard_map/ppermute | solution.py:151
  304.7 1.7 collective-permute-start.41
  307.0 20.1 %collective-permute-done.43.refs_12_ = bf16[2,4,128,256]{3,2,1,0:T(8,128)(2,1)S(1)} collective-permute-done((bf16[2,4,128,256]{3,2,1,0:T(8,128)(2,1)}, bf16[2,4,128,256]{3,2,1,0:T(8,128)(2,1)S(1)}, u32[]{:S(2)}, u32[]{:S(2)}) %collective-permute-start.43) | collective-permute-done | bytes 524320 | tf_op jit(solution)/shard_map/ppermute | solution.py:151
  327.1 1.7 collective-permute-start.45
  329.0 2.1 dynamic-slice_bitcast_fusion.refs_16_
  333.1 8.4 %collective-permute-done.45.refs_14_ = bf16[2,4,128,256]{3,2,1,0:T(8,128)(2,1)S(1)} collective-permute-done((bf16[2,4,128,256]{3,2,1,0:T(8,128)(2,1)S(1)}, bf16[2,4,128,256]{3,2,1,0:T(8,128)(2,1)S(1)}, u32[]{:S(2)}, u32[]{:S(2)}) %collective-permute-start.45) | collective-permute-done | bytes 524320 | tf_op jit(solution)/shard_map/ppermute | solution.py:151
  341.5 2.1 dynamic-slice_bitcast_fusion.1.refs_18_
  345.3 9.6 %shard_map.98.refs_20_ = bf16[8,128,336]{2,1,0:T(8,128)(2,1)} custom-call(s32[3]{0:T(128)} %pad_add_fusion.meta, bf16[2,4,128,256]{3,2,1,0:T(8,128)(2,1)} %shard_map.95.refs_0_, bf16[2,4,128,256]{3,2,1,0:T(8,128)(2,1)} %collective-permute-done.31.refs_1_, bf16[2,4,128,256]{3,2,1,0:T(8,128)(2,1)} %collective-permute-done.32.refs_2_, ...), custom_call_target="tpu_custom_call" | custom-call | flops 2818572288 | bytes 5505024 | tf_op jit(solution)/shard_map/pallas_call | solution.py:543
  354.9 9.0 %collective-permute-done.48.refs_19_ = bf16[144,2048]{1,0:T(8,128)(2,1)} collective-permute-done((bf16[144,2048]{1,0:T(8,128)(2,1)}, bf16[144,2048]{1,0:T(8,128)(2,1)}, u32[]{:S(2)}, u32[]{:S(2)}) %collective-permute-start.48) | collective-permute-done | bytes 589856 | tf_op jit(solution)/shard_map/ppermute | solution.py:151
  363.9 10.5 %shard_map.99 = bf16[16,128,336]{2,1,0:T(8,128)(2,1)} custom-call(s32[3]{0:T(128)} %pad_add_fusion.meta, bf16[2,4,128,256]{3,2,1,0:T(8,128)(2,1)} %shard_map.95.refs_0_, bf16[2,4,128,256]{3,2,1,0:T(8,128)(2,1)} %collective-permute-done.31.refs_1_, bf16[2,4,128,256]{3,2,1,0:T(8,128)(2,1)} %collective-permute-done.32.refs_2_, ...), custom_call_target="tpu_custom_call" | custom-call | flops 2818572288 | bytes 5505024 | tf_op jit(solution)/shard_map/pallas_call | solution.py:543
  374.4 1.9 copy.14
  376.3 23.4 %all_to_all.5 = bf16[16,128,336]{1,2,0:T(8,128)(2,1)S(1)} all-to-all(bf16[16,128,336]{1,2,0:T(8,128)(2,1)S(1)} %copy.14), channel_id=1, replica_groups=mesh['groups'=1,'half'=2,'place'=8,'cols'=2,'sub'=1] {'place','cols'}, dimensions={0} | all-to-all | bytes 2752512 | tf_op jit(solution)/shard_map/all_to_all | solution.py:559
  401.3 3.4 shard_map.100
  (167 shorter events, 35.4 us)
Async XLA Ops:
  6.5 143.8 %all-gather.7.cloned.1.call-start = ((), (), s32[]{:S(2)}) async-start(), calls=%async_computation.1 | async-start | bytes 4128768 | tf_op jit(solution)/shard_map/all_gather | solution.py:412
  8.2 7.6 %collective-permute-start = (f32[2,128]{1,0:T(2,128)S(1)}, f32[2,128]{1,0:T(2,128)S(1)}, u32[]{:S(2)}, u32[]{:S(2)}) collective-permute-start(f32[2,128]{1,0:T(2,128)S(1)} %bitcast.21), channel_id=1, source_target_pairs={{0,1},{1,0},{2,3},{3,2},{4,5},{5,4},{6,7},{7,6},{8,9},{9,8},{10,11... | collective-permute-start | bytes 3080 | tf_op jit(solution)/shard_map/ppermute | solution.py:151
  15.7 217.2 %all-gather.9.cloned.1.call-start = ((), (), s32[]{:S(2)}) async-start(), calls=%async_computation.2 | async-start | bytes 4128768 | tf_op jit(solution)/shard_map/all_gather | solution.py:458
  17.4 73.2 %collective-permute-start.8 = (bf16[256,2688]{1,0:T(8,128)(2,1)S(1)}, bf16[256,2688]{1,0:T(8,128)(2,1)}, u32[]{:S(2)}, u32[]{:S(2)}) collective-permute-start(bf16[256,2688]{1,0:T(8,128)(2,1)S(1)} %fusion.2.refs_0_), channel_id=1, source_target_pairs={{0,8},{1,9},{2,10},{3,11},{4,12},{5,13},{6,14},{7,15},{8,0},{9,1},... | collective-permute-start | bytes 4128776 | tf_op jit(solution)/shard_map/ppermute | solution.py:151
  19.1 7.3 %collective-permute-start.24 = (bf16[336,256]{1,0:T(8,128)(2,1)S(1)}, bf16[336,256]{1,0:T(8,128)(2,1)S(1)}, u32[]{:S(2)}, u32[]{:S(2)}) collective-permute-start(bf16[336,256]{1,0:T(8,128)(2,1)S(1)} %copy-done.33), channel_id=1, source_target_pairs={{0,4},{1,5},{2,6},{3,7},{4,0},{5,1},{6,2},{7,3},{8,12},{9,13},{10,... | collective-permute-start | bytes 516104 | tf_op jit(solution)/shard_map/ppermute | solution.py:151
  20.7 8.3 %collective-permute-start.25 = (bf16[336,256]{1,0:T(8,128)(2,1)S(1)}, bf16[336,256]{1,0:T(8,128)(2,1)S(1)}, u32[]{:S(2)}, u32[]{:S(2)}) collective-permute-start(bf16[336,256]{1,0:T(8,128)(2,1)S(1)} %copy-done.32), channel_id=1, source_target_pairs={{0,6},{1,7},{2,4},{3,5},{4,2},{5,3},{6,0},{7,1},{8,14},{9,15},{10,... | collective-permute-start | bytes 516104 | tf_op jit(solution)/shard_map/ppermute | solution.py:151
  20.9 61.0 %collective-permute-start.26 = (bf16[336,256]{1,0:T(8,128)(2,1)S(1)}, bf16[336,256]{1,0:T(8,128)(2,1)S(1)}, u32[]{:S(2)}, u32[]{:S(2)}) collective-permute-start(bf16[336,256]{1,0:T(8,128)(2,1)S(1)} %copy-done.31), channel_id=1, source_target_pairs={{0,8},{1,9},{2,10},{3,11},{4,12},{5,13},{6,14},{7,15},{8,0},{9,1},... | collective-permute-start | bytes 516104 | tf_op jit(solution)/shard_map/ppermute | solution.py:151
  21.4 65.1 %collective-permute-start.27 = (bf16[336,256]{1,0:T(8,128)(2,1)S(1)}, bf16[336,256]{1,0:T(8,128)(2,1)S(1)}, u32[]{:S(2)}, u32[]{:S(2)}) collective-permute-start(bf16[336,256]{1,0:T(8,128)(2,1)S(1)} %copy-done.30), channel_id=1, source_target_pairs={{0,10},{1,11},{2,8},{3,9},{4,14},{5,15},{6,12},{7,13},{8,2},{9,3},... | collective-permute-start | bytes 516104 | tf_op jit(solution)/shard_map/ppermute | solution.py:151
  26.4 64.2 %collective-permute-start.28 = (bf16[336,256]{1,0:T(8,128)(2,1)S(1)}, bf16[336,256]{1,0:T(8,128)(2,1)S(1)}, u32[]{:S(2)}, u32[]{:S(2)}) collective-permute-start(bf16[336,256]{1,0:T(8,128)(2,1)S(1)} %copy-done.29), channel_id=1, source_target_pairs={{0,12},{1,13},{2,14},{3,15},{4,8},{5,9},{6,10},{7,11},{8,4},{9,5},... | collective-permute-start | bytes 516104 | tf_op jit(solution)/shard_map/ppermute | solution.py:151
  29.0 69.0 %collective-permute-start.4 = (bf16[256,2688]{1,0:T(8,128)(2,1)S(1)}, bf16[256,2688]{1,0:T(8,128)(2,1)}, u32[]{:S(2)}, u32[]{:S(2)}) collective-permute-start(bf16[256,2688]{1,0:T(8,128)(2,1)S(1)} %fusion.2.refs_0_), channel_id=1, source_target_pairs={{0,4},{1,5},{2,6},{3,7},{4,0},{5,1},{6,2},{7,3},{8,12},{9,13},{10,... | collective-permute-start | bytes 4128776 | tf_op jit(solution)/shard_map/ppermute | solution.py:151
  81.9 33.1 %collective-permute-start.1 = (bf16[256,2688]{1,0:T(8,128)(2,1)S(1)}, bf16[256,2688]{1,0:T(8,128)(2,1)S(1)}, u32[]{:S(2)}, u32[]{:S(2)}) collective-permute-start(bf16[256,2688]{1,0:T(8,128)(2,1)S(1)} %fusion.2.refs_0_), channel_id=1, source_target_pairs={{0,1},{1,0},{2,3},{3,2},{4,5},{5,4},{6,7},{7,6},{8,9},{9,8},{10,11... | collective-permute-start | bytes 4128776 | tf_op jit(solution)/shard_map/ppermute | solution.py:151
  86.5 28.5 %collective-permute-start.2 = (bf16[256,2688]{1,0:T(8,128)(2,1)S(1)}, bf16[256,2688]{1,0:T(8,128)(2,1)S(1)}, u32[]{:S(2)}, u32[]{:S(2)}) collective-permute-start(bf16[256,2688]{1,0:T(8,128)(2,1)S(1)} %fusion.2.refs_0_), channel_id=1, source_target_pairs={{0,2},{1,3},{2,0},{3,1},{4,6},{5,7},{6,4},{7,5},{8,10},{9,11},{10,... | collective-permute-start | bytes 4128776 | tf_op jit(solution)/shard_map/ppermute | solution.py:151
  90.7 36.3 %collective-permute-start.12 = (bf16[256,2688]{1,0:T(8,128)(2,1)}, bf16[256,2688]{1,0:T(8,128)(2,1)}, u32[]{:S(2)}, u32[]{:S(2)}) collective-permute-start(bf16[256,2688]{1,0:T(8,128)(2,1)} %collective-permute-done.8.refs_8_), channel_id=1, source_target_pairs={{0,4},{1,5},{2,6},{3,7},{4,0},{5,1},{6,2},{7,3},{8,12},{9,13},{10,... | collective-permute-start | bytes 4128776 | tf_op jit(solution)/shard_map/ppermute | solution.py:151
  97.5 47.1 %collective-permute-start.9 = (bf16[256,2688]{1,0:T(8,128)(2,1)}, bf16[256,2688]{1,0:T(8,128)(2,1)}, u32[]{:S(2)}, u32[]{:S(2)}) collective-permute-start(bf16[256,2688]{1,0:T(8,128)(2,1)} %collective-permute-done.8.refs_8_), channel_id=1, source_target_pairs={{0,1},{1,0},{2,3},{3,2},{4,5},{5,4},{6,7},{7,6},{8,9},{9,8},{10,11... | collective-permute-start | bytes 4128776 | tf_op jit(solution)/shard_map/ppermute | solution.py:151
  98.0 76.0 %collective-permute-start.5 = (bf16[256,2688]{1,0:T(8,128)(2,1)}, bf16[256,2688]{1,0:T(8,128)(2,1)}, u32[]{:S(2)}, u32[]{:S(2)}) collective-permute-start(bf16[256,2688]{1,0:T(8,128)(2,1)} %collective-permute-done.4.refs_4_), channel_id=1, source_target_pairs={{0,1},{1,0},{2,3},{3,2},{4,5},{5,4},{6,7},{7,6},{8,9},{9,8},{10,11... | collective-permute-start | bytes 4128776 | tf_op jit(solution)/shard_map/ppermute | solution.py:151
  115.0 59.1 %collective-permute-start.10 = (bf16[256,2688]{1,0:T(8,128)(2,1)}, bf16[256,2688]{1,0:T(8,128)(2,1)}, u32[]{:S(2)}, u32[]{:S(2)}) collective-permute-start(bf16[256,2688]{1,0:T(8,128)(2,1)} %collective-permute-done.8.refs_8_), channel_id=1, source_target_pairs={{0,2},{1,3},{2,0},{3,1},{4,6},{5,7},{6,4},{7,5},{8,10},{9,11},{10,... | collective-permute-start | bytes 4128776 | tf_op jit(solution)/shard_map/ppermute | solution.py:151
  117.2 58.2 %collective-permute-start.6 = (bf16[256,2688]{1,0:T(8,128)(2,1)}, bf16[256,2688]{1,0:T(8,128)(2,1)}, u32[]{:S(2)}, u32[]{:S(2)}) collective-permute-start(bf16[256,2688]{1,0:T(8,128)(2,1)} %collective-permute-done.4.refs_4_), channel_id=1, source_target_pairs={{0,2},{1,3},{2,0},{3,1},{4,6},{5,7},{6,4},{7,5},{8,10},{9,11},{10,... | collective-permute-start | bytes 4128776 | tf_op jit(solution)/shard_map/ppermute | solution.py:151
  119.9 209.1 %all-gather.11.cloned.1.call-start = ((), (), s32[]{:S(2)}) async-start(), calls=%async_computation.3 | async-start | bytes 2359296 | tf_op jit(solution)/shard_map/all_gather | solution.py:502
  126.9 49.0 %collective-permute-start.3 = (bf16[256,2688]{1,0:T(8,128)(2,1)S(1)}, bf16[256,2688]{1,0:T(8,128)(2,1)S(1)}, u32[]{:S(2)}, u32[]{:S(2)}) collective-permute-start(bf16[256,2688]{1,0:T(8,128)(2,1)S(1)} %copy-done.18), channel_id=1, source_target_pairs={{0,2},{1,3},{2,0},{3,1},{4,6},{5,7},{6,4},{7,5},{8,10},{9,11},{10,... | collective-permute-start | bytes 4128776 | tf_op jit(solution)/shard_map/ppermute | solution.py:151
  144.6 52.4 %collective-permute-start.13 = (bf16[256,2688]{1,0:T(8,128)(2,1)}, bf16[256,2688]{1,0:T(8,128)(2,1)}, u32[]{:S(2)}, u32[]{:S(2)}) collective-permute-start(bf16[256,2688]{1,0:T(8,128)(2,1)} %collective-permute-done.12.refs_12_), channel_id=1, source_target_pairs={{0,1},{1,0},{2,3},{3,2},{4,5},{5,4},{6,7},{7,6},{8,9},{9,8},{10,11... | collective-permute-start | bytes 4128776 | tf_op jit(solution)/shard_map/ppermute | solution.py:151
  174.1 10.9 %collective-permute-start.17 = (bf16[672,256]{1,0:T(8,128)(2,1)S(1)}, bf16[672,256]{1,0:T(8,128)(2,1)S(1)}, u32[]{:S(2)}, u32[]{:S(2)}) collective-permute-start(bf16[672,256]{1,0:T(8,128)(2,1)S(1)} %get-tuple-element.52), channel_id=1, source_target_pairs={{0,4},{1,5},{2,6},{3,7},{4,0},{5,1},{6,2},{7,3},{8,12},{9,13},{10,... | collective-permute-start | bytes 1032200 | tf_op jit(solution)/shard_map/ppermute | solution.py:151
  175.4 16.0 %collective-permute-start.18 = (bf16[672,256]{1,0:T(8,128)(2,1)S(1)}, bf16[672,256]{1,0:T(8,128)(2,1)S(1)}, u32[]{:S(2)}, u32[]{:S(2)}) collective-permute-start(bf16[672,256]{1,0:T(8,128)(2,1)S(1)} %get-tuple-element.51), channel_id=1, source_target_pairs={{0,6},{1,7},{2,4},{3,5},{4,2},{5,3},{6,0},{7,1},{8,14},{9,15},{10,... | collective-permute-start | bytes 1032200 | tf_op jit(solution)/shard_map/ppermute | solution.py:151
  175.9 23.6 %collective-permute-start.19 = (bf16[672,256]{1,0:T(8,128)(2,1)S(1)}, bf16[672,256]{1,0:T(8,128)(2,1)S(1)}, u32[]{:S(2)}, u32[]{:S(2)}) collective-permute-start(bf16[672,256]{1,0:T(8,128)(2,1)S(1)} %get-tuple-element.50), channel_id=1, source_target_pairs={{0,8},{1,9},{2,10},{3,11},{4,12},{5,13},{6,14},{7,15},{8,0},{9,1},... | collective-permute-start | bytes 1032200 | tf_op jit(solution)/shard_map/ppermute | solution.py:151
  178.4 54.4 %collective-permute-start.14 = (bf16[256,2688]{1,0:T(8,128)(2,1)}, bf16[256,2688]{1,0:T(8,128)(2,1)}, u32[]{:S(2)}, u32[]{:S(2)}) collective-permute-start(bf16[256,2688]{1,0:T(8,128)(2,1)} %collective-permute-done.12.refs_12_), channel_id=1, source_target_pairs={{0,2},{1,3},{2,0},{3,1},{4,6},{5,7},{6,4},{7,5},{8,10},{9,11},{10,... | collective-permute-start | bytes 4128776 | tf_op jit(solution)/shard_map/ppermute | solution.py:151
  185.0 47.9 %collective-permute-start.11 = (bf16[256,2688]{1,0:T(8,128)(2,1)}, bf16[256,2688]{1,0:T(8,128)(2,1)}, u32[]{:S(2)}, u32[]{:S(2)}) collective-permute-start(bf16[256,2688]{1,0:T(8,128)(2,1)} %collective-permute-done.9.refs_9_), channel_id=1, source_target_pairs={{0,2},{1,3},{2,0},{3,1},{4,6},{5,7},{6,4},{7,5},{8,10},{9,11},{10,... | collective-permute-start | bytes 4128776 | tf_op jit(solution)/shard_map/ppermute | solution.py:151
  191.5 41.4 %collective-permute-start.7 = (bf16[256,2688]{1,0:T(8,128)(2,1)}, bf16[256,2688]{1,0:T(8,128)(2,1)}, u32[]{:S(2)}, u32[]{:S(2)}) collective-permute-start(bf16[256,2688]{1,0:T(8,128)(2,1)} %collective-permute-done.5.refs_5_), channel_id=1, source_target_pairs={{0,2},{1,3},{2,0},{3,1},{4,6},{5,7},{6,4},{7,5},{8,10},{9,11},{10,... | collective-permute-start | bytes 4128776 | tf_op jit(solution)/shard_map/ppermute | solution.py:151
  197.0 35.9 %collective-permute-start.15 = (bf16[256,2688]{1,0:T(8,128)(2,1)}, bf16[256,2688]{1,0:T(8,128)(2,1)}, u32[]{:S(2)}, u32[]{:S(2)}) collective-permute-start(bf16[256,2688]{1,0:T(8,128)(2,1)} %collective-permute-done.13.refs_13_), channel_id=1, source_target_pairs={{0,2},{1,3},{2,0},{3,1},{4,6},{5,7},{6,4},{7,5},{8,10},{9,11},{10,... | collective-permute-start | bytes 4128776 | tf_op jit(solution)/shard_map/ppermute | solution.py:151
  199.6 10.1 %collective-permute-start.20 = (bf16[672,256]{1,0:T(8,128)(2,1)S(1)}, bf16[672,256]{1,0:T(8,128)(2,1)S(1)}, u32[]{:S(2)}, u32[]{:S(2)}) collective-permute-start(bf16[672,256]{1,0:T(8,128)(2,1)S(1)} %get-tuple-element.49), channel_id=1, source_target_pairs={{0,10},{1,11},{2,8},{3,9},{4,14},{5,15},{6,12},{7,13},{8,2},{9,3},... | collective-permute-start | bytes 1032200 | tf_op jit(solution)/shard_map/ppermute | solution.py:151
  209.7 11.0 %collective-permute-start.21 = (bf16[672,256]{1,0:T(8,128)(2,1)S(1)}, bf16[672,256]{1,0:T(8,128)(2,1)S(1)}, u32[]{:S(2)}, u32[]{:S(2)}) collective-permute-start(bf16[672,256]{1,0:T(8,128)(2,1)S(1)} %get-tuple-element.48), channel_id=1, source_target_pairs={{0,12},{1,13},{2,14},{3,15},{4,8},{5,9},{6,10},{7,11},{8,4},{9,5},... | collective-permute-start | bytes 1032200 | tf_op jit(solution)/shard_map/ppermute | solution.py:151
  220.7 10.7 %collective-permute-start.22 = (bf16[672,256]{1,0:T(8,128)(2,1)S(1)}, bf16[672,256]{1,0:T(8,128)(2,1)S(1)}, u32[]{:S(2)}, u32[]{:S(2)}) collective-permute-start(bf16[672,256]{1,0:T(8,128)(2,1)S(1)} %get-tuple-element.47), channel_id=1, source_target_pairs={{0,14},{1,15},{2,12},{3,13},{4,10},{5,11},{6,8},{7,9},{8,6},{9,7},... | collective-permute-start | bytes 1032200 | tf_op jit(solution)/shard_map/ppermute | solution.py:151
  223.0 118.5 %all-gather.13.cloned.1.call-start = ((), (), s32[]{:S(2)}) async-start(), calls=%async_computation.4 | async-start | bytes 1769472 | tf_op jit(solution)/shard_map/all_gather | solution.py:502
  231.4 73.3 %collective-permute-start.49 = (bf16[336,2048]{1,0:T(8,128)(2,1)}, bf16[336,2048]{1,0:T(8,128)(2,1)}, u32[]{:S(2)}, u32[]{:S(2)}) collective-permute-start(bf16[336,2048]{1,0:T(8,128)(2,1)} %bitcast.8.refs_16_), channel_id=1, source_target_pairs={{0,1},{1,0},{2,3},{3,2},{4,5},{5,4},{6,7},{7,6},{8,9},{9,8},{10,11... | collective-permute-start | bytes 4128776 | tf_op jit(solution)/shard_map/ppermute | solution.py:151
  255.2 22.8 %collective-permute-start.38 = (bf16[4,256,256]{2,1,0:T(8,128)(2,1)}, bf16[4,256,256]{2,1,0:T(8,128)(2,1)}, u32[]{:S(2)}, u32[]{:S(2)}) collective-permute-start(bf16[4,256,256]{2,1,0:T(8,128)(2,1)} %get-tuple-element.43), channel_id=1, source_target_pairs={{0,16},{1,17},{2,18},{3,19},{4,20},{5,21},{6,22},{7,23},{8,24},{9,... | collective-permute-start | bytes 1572872 | tf_op jit(solution)/shard_map/ppermute | solution.py:495
  266.4 8.3 %collective-permute-start.30 = (bf16[4,128,256]{2,1,0:T(8,128)(2,1)}, bf16[4,128,256]{2,1,0:T(8,128)(2,1)}, u32[]{:S(2)}, u32[]{:S(2)}) collective-permute-start(bf16[4,128,256]{2,1,0:T(8,128)(2,1)} %get-tuple-element.42), channel_id=1, source_target_pairs={{0,1},{1,0},{2,3},{3,2},{4,5},{5,4},{6,7},{7,6},{8,9},{9,8},{10,11... | collective-permute-start | bytes 786440 | tf_op jit(solution)/shard_map/ppermute | solution.py:151
  276.6 29.8 %collective-permute-start.34 = (bf16[2,4,128,256]{3,2,1,0:T(8,128)(2,1)}, bf16[2,4,128,256]{3,2,1,0:T(8,128)(2,1)}, u32[]{:S(2)}, u32[]{:S(2)}) collective-permute-start(bf16[2,4,128,256]{3,2,1,0:T(8,128)(2,1)} %shard_map.95.refs_0_), channel_id=1, source_target_pairs={{0,8},{1,9},{2,10},{3,11},{4,12},{5,13},{6,14},{7,15},{8,0},{9,1},... | collective-permute-start | bytes 1572872 | tf_op jit(solution)/shard_map/ppermute | solution.py:151
  287.2 19.2 %collective-permute-start.32 = (bf16[2,4,128,256]{3,2,1,0:T(8,128)(2,1)}, bf16[2,4,128,256]{3,2,1,0:T(8,128)(2,1)}, u32[]{:S(2)}, u32[]{:S(2)}) collective-permute-start(bf16[2,4,128,256]{3,2,1,0:T(8,128)(2,1)} %shard_map.95.refs_0_), channel_id=1, source_target_pairs={{0,4},{1,5},{2,6},{3,7},{4,0},{5,1},{6,2},{7,3},{8,12},{9,13},{10,... | collective-permute-start | bytes 1572872 | tf_op jit(solution)/shard_map/ppermute | solution.py:151
  289.0 17.8 %collective-permute-start.31 = (bf16[2,4,128,256]{3,2,1,0:T(8,128)(2,1)}, bf16[2,4,128,256]{3,2,1,0:T(8,128)(2,1)}, u32[]{:S(2)}, u32[]{:S(2)}) collective-permute-start(bf16[2,4,128,256]{3,2,1,0:T(8,128)(2,1)} %shard_map.95.refs_0_), channel_id=1, source_target_pairs={{0,2},{1,3},{2,0},{3,1},{4,6},{5,7},{6,4},{7,5},{8,10},{9,11},{10,... | collective-permute-start | bytes 1572872 | tf_op jit(solution)/shard_map/ppermute | solution.py:151
  293.0 34.1 %collective-permute-start.43 = (bf16[2,4,128,256]{3,2,1,0:T(8,128)(2,1)}, bf16[2,4,128,256]{3,2,1,0:T(8,128)(2,1)S(1)}, u32[]{:S(2)}, u32[]{:S(2)}) collective-permute-start(bf16[2,4,128,256]{3,2,1,0:T(8,128)(2,1)} %shard_map.97.refs_8_), channel_id=1, source_target_pairs={{0,8},{1,9},{2,10},{3,11},{4,12},{5,13},{6,14},{7,15},{8,0},{9,1},... | collective-permute-start | bytes 1572872 | tf_op jit(solution)/shard_map/ppermute | solution.py:151
  304.7 22.4 %collective-permute-start.41 = (bf16[2,4,128,256]{3,2,1,0:T(8,128)(2,1)}, bf16[2,4,128,256]{3,2,1,0:T(8,128)(2,1)S(1)}, u32[]{:S(2)}, u32[]{:S(2)}) collective-permute-start(bf16[2,4,128,256]{3,2,1,0:T(8,128)(2,1)} %shard_map.97.refs_8_), channel_id=1, source_target_pairs={{0,4},{1,5},{2,6},{3,7},{4,0},{5,1},{6,2},{7,3},{8,12},{9,13},{10,... | collective-permute-start | bytes 1572872 | tf_op jit(solution)/shard_map/ppermute | solution.py:151
  306.4 22.5 %collective-permute-start.40 = (bf16[2,4,128,256]{3,2,1,0:T(8,128)(2,1)}, bf16[2,4,128,256]{3,2,1,0:T(8,128)(2,1)}, u32[]{:S(2)}, u32[]{:S(2)}) collective-permute-start(bf16[2,4,128,256]{3,2,1,0:T(8,128)(2,1)} %shard_map.97.refs_8_), channel_id=1, source_target_pairs={{0,2},{1,3},{2,0},{3,1},{4,6},{5,7},{6,4},{7,5},{8,10},{9,11},{10,... | collective-permute-start | bytes 1572872 | tf_op jit(solution)/shard_map/ppermute | solution.py:151
  306.4 24.7 %collective-permute-start.36 = (bf16[2,4,128,256]{3,2,1,0:T(8,128)(2,1)}, bf16[2,4,128,256]{3,2,1,0:T(8,128)(2,1)S(1)}, u32[]{:S(2)}, u32[]{:S(2)}) collective-permute-start(bf16[2,4,128,256]{3,2,1,0:T(8,128)(2,1)} %collective-permute-done.34.refs_4_), channel_id=1, source_target_pairs={{0,4},{1,5},{2,6},{3,7},{4,0},{5,1},{6,2},{7,3},{8,12},{9,13},{10,... | collective-permute-start | bytes 1572872 | tf_op jit(solution)/shard_map/ppermute | solution.py:151
  306.8 25.8 %collective-permute-start.33 = (bf16[2,4,128,256]{3,2,1,0:T(8,128)(2,1)}, bf16[2,4,128,256]{3,2,1,0:T(8,128)(2,1)S(1)}, u32[]{:S(2)}, u32[]{:S(2)}) collective-permute-start(bf16[2,4,128,256]{3,2,1,0:T(8,128)(2,1)} %collective-permute-done.32.refs_2_), channel_id=1, source_target_pairs={{0,2},{1,3},{2,0},{3,1},{4,6},{5,7},{6,4},{7,5},{8,10},{9,11},{10,... | collective-permute-start | bytes 1572872 | tf_op jit(solution)/shard_map/ppermute | solution.py:151
  327.1 14.3 %collective-permute-start.45 = (bf16[2,4,128,256]{3,2,1,0:T(8,128)(2,1)S(1)}, bf16[2,4,128,256]{3,2,1,0:T(8,128)(2,1)S(1)}, u32[]{:S(2)}, u32[]{:S(2)}) collective-permute-start(bf16[2,4,128,256]{3,2,1,0:T(8,128)(2,1)S(1)} %collective-permute-done.43.refs_12_), channel_id=1, source_target_pairs={{0,4},{1,5},{2,6},{3,7},{4,0},{5,1},{6,2},{7,3},{8,12},{9,13},{10,... | collective-permute-start | bytes 1572872 | tf_op jit(solution)/shard_map/ppermute | solution.py:151
  328.8 14.8 %collective-permute-start.42 = (bf16[2,4,128,256]{3,2,1,0:T(8,128)(2,1)S(1)}, bf16[2,4,128,256]{3,2,1,0:T(8,128)(2,1)}, u32[]{:S(2)}, u32[]{:S(2)}) collective-permute-start(bf16[2,4,128,256]{3,2,1,0:T(8,128)(2,1)S(1)} %collective-permute-done.41.refs_10_), channel_id=1, source_target_pairs={{0,2},{1,3},{2,0},{3,1},{4,6},{5,7},{6,4},{7,5},{8,10},{9,11},{10,... | collective-permute-start | bytes 1572872 | tf_op jit(solution)/shard_map/ppermute | solution.py:151
  331.1 32.8 %collective-permute-start.47 = (bf16[192,2048]{1,0:T(8,128)(2,1)}, bf16[192,2048]{1,0:T(8,128)(2,1)}, u32[]{:S(2)}, u32[]{:S(2)}) collective-permute-start(bf16[192,2048]{1,0:T(8,128)(2,1)} %dynamic-slice_bitcast_fusion.refs_16_), channel_id=1, source_target_pairs={{0,1},{1,0},{2,3},{3,2},{4,5},{5,4},{6,7},{7,6},{8,9},{9,8},{10,11... | collective-permute-start | bytes 2359304 | tf_op jit(solution)/shard_map/ppermute | solution.py:151
  332.6 12.7 %collective-permute-start.44 = (bf16[2,4,128,256]{3,2,1,0:T(8,128)(2,1)S(1)}, bf16[2,4,128,256]{3,2,1,0:T(8,128)(2,1)}, u32[]{:S(2)}, u32[]{:S(2)}) collective-permute-start(bf16[2,4,128,256]{3,2,1,0:T(8,128)(2,1)S(1)} %collective-permute-done.43.refs_12_), channel_id=1, source_target_pairs={{0,2},{1,3},{2,0},{3,1},{4,6},{5,7},{6,4},{7,5},{8,10},{9,11},{10,... | collective-permute-start | bytes 1572872 | tf_op jit(solution)/shard_map/ppermute | solution.py:151
  332.7 12.6 %collective-permute-start.37 = (bf16[2,4,128,256]{3,2,1,0:T(8,128)(2,1)S(1)}, bf16[2,4,128,256]{3,2,1,0:T(8,128)(2,1)}, u32[]{:S(2)}, u32[]{:S(2)}) collective-permute-start(bf16[2,4,128,256]{3,2,1,0:T(8,128)(2,1)S(1)} %collective-permute-done.36.refs_6_), channel_id=1, source_target_pairs={{0,2},{1,3},{2,0},{3,1},{4,6},{5,7},{6,4},{7,5},{8,10},{9,11},{10,... | collective-permute-start | bytes 1572872 | tf_op jit(solution)/shard_map/ppermute | solution.py:151
  343.6 20.2 %collective-permute-start.48 = (bf16[144,2048]{1,0:T(8,128)(2,1)}, bf16[144,2048]{1,0:T(8,128)(2,1)}, u32[]{:S(2)}, u32[]{:S(2)}) collective-permute-start(bf16[144,2048]{1,0:T(8,128)(2,1)} %dynamic-slice_bitcast_fusion.1.refs_18_), channel_id=1, source_target_pairs={{0,1},{1,0},{2,3},{3,2},{4,5},{5,4},{6,7},{7,6},{8,9},{9,8},{10,11... | collective-permute-start | bytes 1769480 | tf_op jit(solution)/shard_map/ppermute | solution.py:151
  (41 other events, 1005.9 us)
Sparse Core Ops, SparseCore 0:
  15.8 70.2 all-gather.6
  120.0 72.4 all-gather.8
  223.1 44.1 all-gather.10
  287.4 46.4 all-gather.12

commit v5 on v4

--- a/solution.py
+++ b/solution.py
@@ -309,72 +309,63 @@
             send_out[g, :, h * HD : (h + 1) * HD] = jnp.where(col == 0, bottom, top)
 
 
-def output_kernel(n, spans, far, meta, *refs):
-    count = n * len(spans)
-    contexts, weights = refs[:count], refs[count:-5]
-    if far:
-        weights, before = weights[:-1], weights[-1]
+def output_kernel(n, size, meta, *refs):
+    contexts, weights, after = refs[:n], refs[n : n + 6], refs[n + 6 : -5]
     out, context_mem, weight_mem, context_sem, weight_sem = refs[-5:]
     place, half, col = meta[0], meta[1], meta[2]
-    deep = weights[0].shape[1]
+    rows_all, deep = weights[0].shape
     wide = contexts[0].shape[3]
     part = contexts[0].shape[2]
     copies = []
     for k, source in enumerate(weights):
-        first = sum(weights[j].shape[0] for j in range(k % 2, k, 2))
+        first = (half if k < 2 else lax.bitwise_xor(half, 1)) * rows_all
+        first = first + (0 if k < 4 else weights[2].shape[0])
         side = pl.multiple_of(lax.bitwise_xor(col, k % 2) * deep, 128)
         copies.append(
             pltpu.make_async_copy(
                 source,
-                weight_mem.at[pl.ds(first, source.shape[0]), pl.ds(side, deep)],
+                weight_mem.at[
+                    pl.ds(pl.multiple_of(first, 16), source.shape[0]), pl.ds(side, deep)
+                ],
                 weight_sem.at[k],
             )
         )
-    loads = []
-    for s, (low, size) in enumerate(spans):
-        loads.append([])
-        for m in range(n):
-            for side in range(2):
-                first = lax.bitwise_xor(col, side) * deep + lax.bitwise_xor(place, m) * wide
-                loads[s].append(
-                    pltpu.make_async_copy(
-                        contexts[s * n + m].at[side],
-                        context_mem.at[
-                            pl.ds(low, size), :, pl.ds(pl.multiple_of(first, 128), wide)
-                        ],
-                        context_sem.at[(s * n + m) * 2 + side],
-                    )
+    for m in range(n):
+        for side in range(2):
+            first = lax.bitwise_xor(col, side) * deep + lax.bitwise_xor(place, m) * wide
+            copies.append(
+                pltpu.make_async_copy(
+                    contexts[m].at[side],
+                    context_mem.at[:, :, pl.ds(pl.multiple_of(first, 128), wide)],
+                    context_sem.at[m * 2 + side],
                 )
-    for copy in copies + loads[0]:
+            )
+    for copy in copies:
         copy.start()
     for copy in copies:
         copy.wait()
-    for s, (low, size) in enumerate(spans):
-        for copy in loads[s]:
-            copy.wait()
-        if s + 1 < len(spans):
-            for copy in loads[s + 1]:
-                copy.start()
-        left = context_mem[low : low + size].reshape(size * part, 2 * deep)
-        result = lax.dot_general(
-            left, weight_mem[...], (((1,), (1,)), ((), ())), preferred_element_type=jnp.float32
-        ).astype(jnp.bfloat16)
-        for k in range(size):
-            slab = result[k * part : (k + 1) * part]
-            if far:
-                out[2 * (low + k) + lax.bitwise_xor(half, 1)] = slab
-                out[2 * (low + k) + half] = before[low + k]
-            else:
-                out[low + k] = slab
+    result = lax.dot_general(
+        weight_mem[...],
+        context_mem[...].reshape(size * part, 2 * deep),
+        (((1,), (1,)), ((), ())),
+        preferred_element_type=jnp.float32,
+    ).astype(jnp.bfloat16)
+    for k in range(size):
+        for block in range(2):
+            out[2 * k + block] = result[
+                block * rows_all : (block + 1) * rows_all, k * part : (k + 1) * part
+            ]
+    if after:
+        out[2 * size :] = after[0][...]
 
 
 def close_kernel(n, activations, arrived, out):
-    part = arrived.shape[1]
+    _, _, part = arrived.shape
     for col in range(2):
         rows = pl.ds(col * part, part)
-        whole = jnp.concatenate([arrived[2 * p + col] for p in range(n)], axis=1)
+        whole = jnp.concatenate([arrived[2 * p + col] for p in range(n)], axis=0)
         out[rows, :] = (
-            activations[rows, :].astype(jnp.float32) + whole.astype(jnp.float32)
+            activations[rows, :].astype(jnp.float32) + whole.astype(jnp.float32).T
         ).astype(jnp.bfloat16)
 
 
@@ -496,12 +487,11 @@
 
     own_weight, _ = lax.optimization_barrier((output_weight.T, q_own))
     ahead = own_weight.shape[0] * 4 // 7 // 16 * 16
-    near_weights = [own_weight, swapped(own_weight, 0, 1)]
-    far_weights = []
+    out_weights = [own_weight, swapped(own_weight, 0, 1)]
     for rows in [own_weight[:ahead], own_weight[ahead:]]:
         both = lax.all_gather(rows, "half", axis=0)
         piece = lax.dynamic_index_in_dim(both, 1 - half, 0, keepdims=False)
-        far_weights += [piece, swapped(piece, 0, 1)]
+        out_weights += [piece, swapped(piece, 0, 1)]
 
     contexts = []
     spans = [(reach, n - reach), (0, reach)]
@@ -533,27 +523,28 @@
         pairs[z + y] = swapped(pairs[z], y, 0)
         for m in list(pairs):
             pairs[m + c] = swapped(pairs[m], c, 0)
-        contexts += [pairs[m] for m in range(n)]
+        contexts.append([pairs[m] for m in range(n)])
 
     out_cols = output_weight.shape[1]
     deep_out = output_weight.shape[0]
     result = []
-    for weights, shape in ((near_weights, (n,)), (far_weights, (2 * n,))):
+    for s, (low, count) in enumerate(spans):
+        blocks_out = 2 * count + sum(r.shape[0] for r in result)
         result = [
             run(
-                functools.partial(output_kernel, n, spans, len(result)),
-                shaped((*shape, part, out_cols), bf16),
-                [SMEM] + [ANY] * (2 * n + len(weights)) + [VMEM] * len(result),
+                functools.partial(output_kernel, n, count),
+                shaped((blocks_out, out_cols, part), bf16),
+                [SMEM] + [ANY] * (n + 6) + [VMEM] * len(result),
                 VMEM,
                 [
-                    pltpu.VMEM((n, part, 2 * deep_out), bf16),
-                    pltpu.VMEM((out_cols, 2 * deep_out), bf16),
-                    pltpu.SemaphoreType.DMA((4 * n,)),
-                    pltpu.SemaphoreType.DMA((len(weights),)),
+                    pltpu.VMEM((count, part, 2 * deep_out), bf16),
+                    pltpu.VMEM((2 * out_cols, 2 * deep_out), bf16),
+                    pltpu.SemaphoreType.DMA((2 * n,)),
+                    pltpu.SemaphoreType.DMA((6,)),
                 ],
-                2 * n * part * 2 * deep_out * out_cols,
+                8 * count * part * deep_out * out_cols,
                 8 * deep_out * out_cols,
-            )(meta, *contexts, *weights, *result)
+            )(meta, *contexts[s], *out_weights, *result)
         ]
 
     arrived = lax.all_to_all(result[0], ("place", "cols"), 0, 0, tiled=True)

time: 412 us -> 420 us (1.019)
  starting transfers between devices: 51.6 us -> 60.1 us
  blocking collectives: 23.4 us -> 28.5 us
  local copies, waits for them, and re-layouts: 20 us -> 14.9 us
    ppermute x49, starting transfers between devices: 48.2 us -> 55.4 us  [swapped(): return lax.ppermute(value, ('place', 'cols'), pairs)]
    all_to_all x1, blocking collectives: 23.4 us -> 28.5 us  [split_body(): arrived = lax.all_to_all(result[0], ('place', 'cols'), 0, 0, tiled=True)]
  transfers between devices with their start and end apart: 54 -> 54, of which waited for: 22 -> 23; matrix products, arithmetic and copies ran while one was open for 5% -> 5% of each run, Pallas kernels for 13% -> 12%
where the time goes in v5:
time: 420 us; the launch traced here: 419 us
  waiting for transfers between devices  228 us (54%)
  Pallas kernels  65.8 us (16%)
  starting transfers between devices  60.1 us (14%)
  blocking collectives  28.5 us (7%)
  local copies, waits for them, and re-layouts  14.9 us (4%)
  between operations  13.4 us (3%)
  other arithmetic  8.12 us (2%)
    ppermute x49, waiting for transfers between devices, swapped(): return lax.ppermute(value, ('place', 'cols'), pairs)  228 us
    ppermute x49, starting transfers between devices, swapped(): return lax.ppermute(value, ('place', 'cols'), pairs)  55.4 us
    all_to_all x1, blocking collectives, split_body(): arrived = lax.all_to_all(result[0], ('place', 'cols'), 0, 0, tiled=True)  28.5 us
    pallas_call x1, Pallas kernels, split_body(): run(functools.partial(project_kernel, n, reach, heads), [shaped((n, token...  22.6 us
    pallas_call x2, Pallas kernels, split_body(): run(functools.partial(output_kernel, n, count), shaped((blocks_out, out_c...  17.7 us
    pallas_call x2, Pallas kernels, split_body(): run(functools.partial(attend_kernel, low, count, reach, heads), [shape, s...  12.1 us
  transfers between devices with their start and end apart: 54, of which 23 were waited for; matrix products, arithmetic and copies ran while one was open for 5% of the time, Pallas kernels for 12%

profile of v5, /device:TPU:0, one launch (start us, length us, event | category | flops | bytes accessed | tf_op | source)
XLA Modules:
  0.0 419.2 jit_solution(10025374110748207092)
XLA Ops:
  7.2 3.7 shard_map.91
  12.5 3.0 collective-permute-start
  18.7 2.1 collective-permute-start.8
  24.3 3.8 collective-permute-done.24.refs_2_
  32.3 52.9 %collective-permute-done.26.refs_4_ = bf16[336,256]{1,0:T(8,128)(2,1)} collective-permute-done((bf16[336,256]{1,0:T(8,128)(2,1)S(1)}, bf16[336,256]{1,0:T(8,128)(2,1)}, u32[]{:S(2)}, u32[]{:S(2)}) %collective-permute-start.26) | collective-permute-done | bytes 172064 | tf_op jit(solution)/shard_map/ppermute | solution.py:151
  85.3 1.9 collective-permute-start.1
  88.6 3.1 collective-permute-done.28.refs_6_
  92.2 6.5 %collective-permute-done.29.refs_7_ = bf16[336,256]{1,0:T(8,128)(2,1)} collective-permute-done((bf16[336,256]{1,0:T(8,128)(2,1)S(1)}, bf16[336,256]{1,0:T(8,128)(2,1)}, u32[]{:S(2)}, u32[]{:S(2)}) %collective-permute-start.29) | collective-permute-done | bytes 172064 | tf_op jit(solution)/shard_map/ppermute | solution.py:151
  100.2 2.6 shard_map.92
  103.5 15.1 %collective-permute-done.1.refs_1_ = bf16[256,2688]{1,0:T(8,128)(2,1)} collective-permute-done((bf16[256,2688]{1,0:T(8,128)(2,1)}, bf16[256,2688]{1,0:T(8,128)(2,1)}, u32[]{:S(2)}, u32[]{:S(2)}) %collective-permute-start.1) | collective-permute-done | bytes 1376288 | tf_op jit(solution)/shard_map/ppermute | solution.py:151
  119.2 8.9 %collective-permute-done.12.refs_12_ = bf16[256,2688]{1,0:T(8,128)(2,1)} collective-permute-done((bf16[256,2688]{1,0:T(8,128)(2,1)}, bf16[256,2688]{1,0:T(8,128)(2,1)}, u32[]{:S(2)}, u32[]{:S(2)}) %collective-permute-start.12) | collective-permute-done | bytes 1376288 | tf_op jit(solution)/shard_map/ppermute | solution.py:151
  128.2 19.9 %collective-permute-done.9.refs_9_ = bf16[256,2688]{1,0:T(8,128)(2,1)} collective-permute-done((bf16[256,2688]{1,0:T(8,128)(2,1)}, bf16[256,2688]{1,0:T(8,128)(2,1)}, u32[]{:S(2)}, u32[]{:S(2)}) %collective-permute-start.9) | collective-permute-done | bytes 1376288 | tf_op jit(solution)/shard_map/ppermute | solution.py:151
  148.2 1.9 collective-permute-start.13
  150.2 3.7 fusion.3
  153.9 1.9 pad_maximum_fusion
  155.8 2.6 constant_dynamic-slice_fusion
  158.4 19.1 %collective-permute-done.5.refs_5_ = bf16[256,2688]{1,0:T(8,128)(2,1)S(1)} collective-permute-done((bf16[256,2688]{1,0:T(8,128)(2,1)}, bf16[256,2688]{1,0:T(8,128)(2,1)S(1)}, u32[]{:S(2)}, u32[]{:S(2)}) %collective-permute-start.5) | collective-permute-done | bytes 1376288 | tf_op jit(solution)/shard_map/ppermute | solution.py:151
  177.6 2.0 collective-permute-start.17
  181.5 7.0 %collective-permute-done.17.refs_18_ = bf16[672,256]{1,0:T(8,128)(2,1)S(1)} collective-permute-done((bf16[672,256]{1,0:T(8,128)(2,1)S(1)}, bf16[672,256]{1,0:T(8,128)(2,1)S(1)}, u32[]{:S(2)}, u32[]{:S(2)}) %collective-permute-start.17) | collective-permute-done | bytes 344096 | tf_op jit(solution)/shard_map/ppermute | solution.py:151
  188.6 6.8 %collective-permute-done.18.refs_19_ = bf16[672,256]{1,0:T(8,128)(2,1)S(1)} collective-permute-done((bf16[672,256]{1,0:T(8,128)(2,1)S(1)}, bf16[672,256]{1,0:T(8,128)(2,1)S(1)}, u32[]{:S(2)}, u32[]{:S(2)}) %collective-permute-start.18) | collective-permute-done | bytes 344096 | tf_op jit(solution)/shard_map/ppermute | solution.py:151
  195.8 4.1 collective-permute-done.13.refs_13_
  199.9 2.0 slice.22
  202.0 2.8 collective-permute-start.20
  204.7 8.4 %collective-permute-done.20.refs_21_ = bf16[672,256]{1,0:T(8,128)(2,1)S(1)} collective-permute-done((bf16[672,256]{1,0:T(8,128)(2,1)S(1)}, bf16[672,256]{1,0:T(8,128)(2,1)S(1)}, u32[]{:S(2)}, u32[]{:S(2)}) %collective-permute-start.20) | collective-permute-done | bytes 344096 | tf_op jit(solution)/shard_map/ppermute | solution.py:151
  213.2 1.9 collective-permute-start.21
  215.0 15.7 %collective-permute-done.21.refs_22_ = bf16[672,256]{1,0:T(8,128)(2,1)S(1)} collective-permute-done((bf16[672,256]{1,0:T(8,128)(2,1)S(1)}, bf16[672,256]{1,0:T(8,128)(2,1)S(1)}, u32[]{:S(2)}, u32[]{:S(2)}) %collective-permute-start.21) | collective-permute-done | bytes 344096 | tf_op jit(solution)/shard_map/ppermute | solution.py:151
  230.7 2.9 collective-permute-start.22
  233.6 2.1 slice.21
  235.8 10.0 %collective-permute-done.22.refs_23_ = bf16[672,256]{1,0:T(8,128)(2,1)S(1)} collective-permute-done((bf16[672,256]{1,0:T(8,128)(2,1)S(1)}, bf16[672,256]{1,0:T(8,128)(2,1)S(1)}, u32[]{:S(2)}, u32[]{:S(2)}) %collective-permute-start.22) | collective-permute-done | bytes 344096 | tf_op jit(solution)/shard_map/ppermute | solution.py:151
  247.3 22.6 %shard_map.93 = (bf16[8,256,256]{2,1,0:T(8,128)(2,1)}, bf16[4,256,256]{2,1,0:T(8,128)(2,1)}, bf16[8,512,128]{2,1,0:T(8,128)(2,1)}) custom-call(s32[3]{0:T(128)} %pad_add_fusion.meta, f32[8,256,128]{2,1,0:T(8,128)} %get-tuple-element.28.cosine, f32[8,256,128]{2,1,0:T(8,128)} %get-tuple-element.29.sine, f32[1,128]{1,0:T(1,128)} %bitcast.22, ...), custom_call_target="tpu_custom_call" | custom-call | flops 11274289152 | bytes 22020096 | tf_op jit(solution)/shard_map/pallas_call | solution.py:458
  270.0 4.6 %collective-permute-start.30 = (bf16[4,256,256]{2,1,0:T(8,128)(2,1)}, bf16[4,256,256]{2,1,0:T(8,128)(2,1)}, u32[]{:S(2)}, u32[]{:S(2)}) collective-permute-start(bf16[4,256,256]{2,1,0:T(8,128)(2,1)} %get-tuple-element.41), channel_id=1, source_target_pairs={{0,16},{1,17},{2,18},{3,19},{4,20},{5,21},{6,22},{7,23},{8,24},{9,... | collective-permute-start | bytes 1572872 | tf_op jit(solution)/shard_map/ppermute | solution.py:486
  276.5 6.0 %shard_map.96 = (bf16[4,128,256]{2,1,0:T(8,128)(2,1)}, bf16[4,128,256]{2,1,0:T(8,128)(2,1)}) custom-call(s32[3]{0:T(128)} %pad_add_fusion.meta, s32[8,256,1]{2,1,0:T(8,128)} %copy.10.q_doc, s32[12,1,256]{2,1,0:T(1,128)} %bitcast.19, bf16[8,512,128]{2,1,0:T(8,128)(2,1)} %get-tuple-element.39.queries, bf16[8,256,256]{2,1,0:T(8,128)(2,1)} %get-tuple-element.40.kv_own), custom_call_target="tpu_custom_call" | custom-call | flops 2684354560 | bytes 2097152 | tf_op jit(solution)/shard_map/pallas_call | solution.py:501
  283.2 1.9 dynamic-slice_bitcast_fusion.1.refs_12_
  286.4 5.5 %collective-permute-done.42.second = bf16[4,128,256]{2,1,0:T(8,128)(2,1)} collective-permute-done((bf16[4,128,256]{2,1,0:T(8,128)(2,1)}, bf16[4,128,256]{2,1,0:T(8,128)(2,1)}, u32[]{:S(2)}, u32[]{:S(2)}) %collective-permute-start.42) | collective-permute-done | bytes 262176 | tf_op jit(solution)/shard_map/ppermute | solution.py:151
  292.0 1.9 shard_map.97.refs_0_
  293.9 3.0 collective-permute-start.46
  296.9 6.1 %shard_map.94 = (bf16[4,128,256]{2,1,0:T(8,128)(2,1)}, bf16[4,128,256]{2,1,0:T(8,128)(2,1)}) custom-call(s32[3]{0:T(128)} %pad_add_fusion.meta, s32[8,256,1]{2,1,0:T(8,128)} %copy.10.q_doc, s32[12,1,256]{2,1,0:T(1,128)} %bitcast.20, bf16[8,512,128]{2,1,0:T(8,128)(2,1)} %get-tuple-element.39.queries, bf16[8,256,256]{2,1,0:T(8,128)(2,1)} %get-tuple-element.40.kv_own, ...), custom_call_target="tpu_custom_call" | custom-call | flops 2684354560 | bytes 2097152 | tf_op jit(solution)/shard_map/pallas_call | solution.py:501
  303.8 2.1 dynamic-slice_bitcast_fusion.refs_10_
  307.1 5.4 %collective-permute-done.31.second = bf16[4,128,256]{2,1,0:T(8,128)(2,1)} collective-permute-done((bf16[4,128,256]{2,1,0:T(8,128)(2,1)}, bf16[4,128,256]{2,1,0:T(8,128)(2,1)}, u32[]{:S(2)}, u32[]{:S(2)}) %collective-permute-start.31) | collective-permute-done | bytes 262176 | tf_op jit(solution)/shard_map/ppermute | solution.py:151
  313.3 1.9 shard_map.95.refs_0_
  315.1 11.2 %collective-permute-start.35 = (bf16[2,4,128,256]{3,2,1,0:T(8,128)(2,1)}, bf16[2,4,128,256]{3,2,1,0:T(8,128)(2,1)}, u32[]{:S(2)}, u32[]{:S(2)}) collective-permute-start(bf16[2,4,128,256]{3,2,1,0:T(8,128)(2,1)} %shard_map.95.refs_0_), channel_id=1, source_target_pairs={{0,8},{1,9},{2,10},{3,11},{4,12},{5,13},{6,14},{7,15},{8,0},{9,1},... | collective-permute-start | bytes 1572872 | tf_op jit(solution)/shard_map/ppermute | solution.py:151
  328.9 10.3 %collective-permute-done.35.refs_4_ = bf16[2,4,128,256]{3,2,1,0:T(8,128)(2,1)} collective-permute-done((bf16[2,4,128,256]{3,2,1,0:T(8,128)(2,1)}, bf16[2,4,128,256]{3,2,1,0:T(8,128)(2,1)}, u32[]{:S(2)}, u32[]{:S(2)}) %collective-permute-start.35) | collective-permute-done | bytes 524320 | tf_op jit(solution)/shard_map/ppermute | solution.py:151
  342.8 10.0 %collective-permute-done.33.refs_2_ = bf16[2,4,128,256]{3,2,1,0:T(8,128)(2,1)} collective-permute-done((bf16[2,4,128,256]{3,2,1,0:T(8,128)(2,1)}, bf16[2,4,128,256]{3,2,1,0:T(8,128)(2,1)}, u32[]{:S(2)}, u32[]{:S(2)}) %collective-permute-start.33) | collective-permute-done | bytes 524320 | tf_op jit(solution)/shard_map/ppermute | solution.py:151
  352.7 10.4 %collective-permute-done.37.refs_6_ = bf16[2,4,128,256]{3,2,1,0:T(8,128)(2,1)} collective-permute-done((bf16[2,4,128,256]{3,2,1,0:T(8,128)(2,1)}, bf16[2,4,128,256]{3,2,1,0:T(8,128)(2,1)}, u32[]{:S(2)}, u32[]{:S(2)}) %collective-permute-start.37) | collective-permute-done | bytes 524320 | tf_op jit(solution)/shard_map/ppermute | solution.py:151
  363.2 8.5 %shard_map.98.refs_14_ = bf16[8,336,128]{2,1,0:T(8,128)(2,1)} custom-call(s32[3]{0:T(128)} %pad_add_fusion.meta, bf16[2,4,128,256]{3,2,1,0:T(8,128)(2,1)} %shard_map.97.refs_0_, bf16[2,4,128,256]{3,2,1,0:T(8,128)(2,1)} %collective-permute-done.43.refs_1_, bf16[2,4,128,256]{3,2,1,0:T(8,128)(2,1)} %collective-permute-done.44.refs_2_, ...), custom_call_target="tpu_custom_call" | custom-call | flops 2818572288 | bytes 5505024 | tf_op jit(solution)/shard_map/pallas_call | solution.py:534
  371.7 9.2 %shard_map.99 = bf16[16,336,128]{2,1,0:T(8,128)(2,1)} custom-call(s32[3]{0:T(128)} %pad_add_fusion.meta, bf16[2,4,128,256]{3,2,1,0:T(8,128)(2,1)} %shard_map.95.refs_0_, bf16[2,4,128,256]{3,2,1,0:T(8,128)(2,1)} %collective-permute-done.32.refs_1_, bf16[2,4,128,256]{3,2,1,0:T(8,128)(2,1)} %collective-permute-done.33.refs_2_, ...), custom_call_target="tpu_custom_call" | custom-call | flops 2818572288 | bytes 5505024 | tf_op jit(solution)/shard_map/pallas_call | solution.py:534
  381.0 28.5 %all_to_all.5.arrived = bf16[16,336,128]{2,1,0:T(8,128)(2,1)} all-to-all(bf16[16,336,128]{2,1,0:T(8,128)(2,1)} %shard_map.99), channel_id=1, replica_groups=mesh['groups'=1,'half'=2,'place'=8,'cols'=2,'sub'=1] {'place','cols'}, dimensions={0} | all-to-all | bytes 2752512 | tf_op jit(solution)/shard_map/all_to_all | solution.py:550
  409.4 3.3 shard_map.100
  (131 shorter events, 34.8 us)
Async XLA Ops:
  6.5 149.3 %all-gather.7.cloned.1.call-start = ((), (), s32[]{:S(2)}) async-start(), calls=%async_computation.1 | async-start | bytes 4128768 | tf_op jit(solution)/shard_map/all_gather | solution.py:403
  10.9 236.4 %all-gather.9.cloned.1.call-start = ((), (), s32[]{:S(2)}) async-start(), calls=%async_computation.2 | async-start | bytes 4128768 | tf_op jit(solution)/shard_map/all_gather | solution.py:449
  18.7 73.1 %collective-permute-start.8 = (bf16[256,2688]{1,0:T(8,128)(2,1)}, bf16[256,2688]{1,0:T(8,128)(2,1)}, u32[]{:S(2)}, u32[]{:S(2)}) collective-permute-start(bf16[256,2688]{1,0:T(8,128)(2,1)} %fusion.2.refs_0_), channel_id=1, source_target_pairs={{0,8},{1,9},{2,10},{3,11},{4,12},{5,13},{6,14},{7,15},{8,0},{9,1},... | collective-permute-start | bytes 4128776 | tf_op jit(solution)/shard_map/ppermute | solution.py:151
  22.6 62.7 %collective-permute-start.26 = (bf16[336,256]{1,0:T(8,128)(2,1)S(1)}, bf16[336,256]{1,0:T(8,128)(2,1)}, u32[]{:S(2)}, u32[]{:S(2)}) collective-permute-start(bf16[336,256]{1,0:T(8,128)(2,1)S(1)} %copy-done.14), channel_id=1, source_target_pairs={{0,8},{1,9},{2,10},{3,11},{4,12},{5,13},{6,14},{7,15},{8,0},{9,1},... | collective-permute-start | bytes 516104 | tf_op jit(solution)/shard_map/ppermute | solution.py:151
  22.9 65.0 %collective-permute-start.27 = (bf16[336,256]{1,0:T(8,128)(2,1)S(1)}, bf16[336,256]{1,0:T(8,128)(2,1)}, u32[]{:S(2)}, u32[]{:S(2)}) collective-permute-start(bf16[336,256]{1,0:T(8,128)(2,1)S(1)} %copy-done.13), channel_id=1, source_target_pairs={{0,10},{1,11},{2,8},{3,9},{4,14},{5,15},{6,12},{7,13},{8,2},{9,3},... | collective-permute-start | bytes 516104 | tf_op jit(solution)/shard_map/ppermute | solution.py:151
  28.2 63.6 %collective-permute-start.28 = (bf16[336,256]{1,0:T(8,128)(2,1)S(1)}, bf16[336,256]{1,0:T(8,128)(2,1)}, u32[]{:S(2)}, u32[]{:S(2)}) collective-permute-start(bf16[336,256]{1,0:T(8,128)(2,1)S(1)} %copy-done.12), channel_id=1, source_target_pairs={{0,12},{1,13},{2,14},{3,15},{4,8},{5,9},{6,10},{7,11},{8,4},{9,5},... | collective-permute-start | bytes 516104 | tf_op jit(solution)/shard_map/ppermute | solution.py:151
  30.8 72.1 %collective-permute-start.4 = (bf16[256,2688]{1,0:T(8,128)(2,1)}, bf16[256,2688]{1,0:T(8,128)(2,1)}, u32[]{:S(2)}, u32[]{:S(2)}) collective-permute-start(bf16[256,2688]{1,0:T(8,128)(2,1)} %fusion.2.refs_0_), channel_id=1, source_target_pairs={{0,4},{1,5},{2,6},{3,7},{4,0},{5,1},{6,2},{7,3},{8,12},{9,13},{10,... | collective-permute-start | bytes 4128776 | tf_op jit(solution)/shard_map/ppermute | solution.py:151
  85.3 33.4 %collective-permute-start.1 = (bf16[256,2688]{1,0:T(8,128)(2,1)}, bf16[256,2688]{1,0:T(8,128)(2,1)}, u32[]{:S(2)}, u32[]{:S(2)}) collective-permute-start(bf16[256,2688]{1,0:T(8,128)(2,1)} %fusion.2.refs_0_), channel_id=1, source_target_pairs={{0,1},{1,0},{2,3},{3,2},{4,5},{5,4},{6,7},{7,6},{8,9},{9,8},{10,11... | collective-permute-start | bytes 4128776 | tf_op jit(solution)/shard_map/ppermute | solution.py:151
  88.0 30.7 %collective-permute-start.2 = (bf16[256,2688]{1,0:T(8,128)(2,1)}, bf16[256,2688]{1,0:T(8,128)(2,1)}, u32[]{:S(2)}, u32[]{:S(2)}) collective-permute-start(bf16[256,2688]{1,0:T(8,128)(2,1)} %fusion.2.refs_0_), channel_id=1, source_target_pairs={{0,2},{1,3},{2,0},{3,1},{4,6},{5,7},{6,4},{7,5},{8,10},{9,11},{10,... | collective-permute-start | bytes 4128776 | tf_op jit(solution)/shard_map/ppermute | solution.py:151
  91.8 36.3 %collective-permute-start.12 = (bf16[256,2688]{1,0:T(8,128)(2,1)}, bf16[256,2688]{1,0:T(8,128)(2,1)}, u32[]{:S(2)}, u32[]{:S(2)}) collective-permute-start(bf16[256,2688]{1,0:T(8,128)(2,1)} %collective-permute-done.8.refs_8_), channel_id=1, source_target_pairs={{0,4},{1,5},{2,6},{3,7},{4,0},{5,1},{6,2},{7,3},{8,12},{9,13},{10,... | collective-permute-start | bytes 4128776 | tf_op jit(solution)/shard_map/ppermute | solution.py:151
  98.7 49.4 %collective-permute-start.9 = (bf16[256,2688]{1,0:T(8,128)(2,1)}, bf16[256,2688]{1,0:T(8,128)(2,1)}, u32[]{:S(2)}, u32[]{:S(2)}) collective-permute-start(bf16[256,2688]{1,0:T(8,128)(2,1)} %collective-permute-done.8.refs_8_), channel_id=1, source_target_pairs={{0,1},{1,0},{2,3},{3,2},{4,5},{5,4},{6,7},{7,6},{8,9},{9,8},{10,11... | collective-permute-start | bytes 4128776 | tf_op jit(solution)/shard_map/ppermute | solution.py:151
  102.9 180.3 %all-gather.13.cloned.1.call-start = ((), (), s32[]{:S(2)}) async-start(), calls=%async_computation.4 | async-start | bytes 1769472 | tf_op jit(solution)/shard_map/all_gather | solution.py:492
  102.9 74.6 %collective-permute-start.5 = (bf16[256,2688]{1,0:T(8,128)(2,1)}, bf16[256,2688]{1,0:T(8,128)(2,1)S(1)}, u32[]{:S(2)}, u32[]{:S(2)}) collective-permute-start(bf16[256,2688]{1,0:T(8,128)(2,1)} %collective-permute-done.4.refs_4_), channel_id=1, source_target_pairs={{0,1},{1,0},{2,3},{3,2},{4,5},{5,4},{6,7},{7,6},{8,9},{9,8},{10,11... | collective-permute-start | bytes 4128776 | tf_op jit(solution)/shard_map/ppermute | solution.py:151
  118.7 58.9 %collective-permute-start.10 = (bf16[256,2688]{1,0:T(8,128)(2,1)}, bf16[256,2688]{1,0:T(8,128)(2,1)}, u32[]{:S(2)}, u32[]{:S(2)}) collective-permute-start(bf16[256,2688]{1,0:T(8,128)(2,1)} %collective-permute-done.8.refs_8_), channel_id=1, source_target_pairs={{0,2},{1,3},{2,0},{3,1},{4,6},{5,7},{6,4},{7,5},{8,10},{9,11},{10,... | collective-permute-start | bytes 4128776 | tf_op jit(solution)/shard_map/ppermute | solution.py:151
  118.7 60.9 %collective-permute-start.6 = (bf16[256,2688]{1,0:T(8,128)(2,1)}, bf16[256,2688]{1,0:T(8,128)(2,1)}, u32[]{:S(2)}, u32[]{:S(2)}) collective-permute-start(bf16[256,2688]{1,0:T(8,128)(2,1)} %collective-permute-done.4.refs_4_), channel_id=1, source_target_pairs={{0,2},{1,3},{2,0},{3,1},{4,6},{5,7},{6,4},{7,5},{8,10},{9,11},{10,... | collective-permute-start | bytes 4128776 | tf_op jit(solution)/shard_map/ppermute | solution.py:151
  128.1 51.6 %collective-permute-start.3 = (bf16[256,2688]{1,0:T(8,128)(2,1)}, bf16[256,2688]{1,0:T(8,128)(2,1)}, u32[]{:S(2)}, u32[]{:S(2)}) collective-permute-start(bf16[256,2688]{1,0:T(8,128)(2,1)} %collective-permute-done.1.refs_1_), channel_id=1, source_target_pairs={{0,2},{1,3},{2,0},{3,1},{4,6},{5,7},{6,4},{7,5},{8,10},{9,11},{10,... | collective-permute-start | bytes 4128776 | tf_op jit(solution)/shard_map/ppermute | solution.py:151
  148.2 51.8 %collective-permute-start.13 = (bf16[256,2688]{1,0:T(8,128)(2,1)}, bf16[256,2688]{1,0:T(8,128)(2,1)}, u32[]{:S(2)}, u32[]{:S(2)}) collective-permute-start(bf16[256,2688]{1,0:T(8,128)(2,1)} %collective-permute-done.12.refs_12_), channel_id=1, source_target_pairs={{0,1},{1,0},{2,3},{3,2},{4,5},{5,4},{6,7},{7,6},{8,9},{9,8},{10,11... | collective-permute-start | bytes 4128776 | tf_op jit(solution)/shard_map/ppermute | solution.py:151
  177.6 11.0 %collective-permute-start.17 = (bf16[672,256]{1,0:T(8,128)(2,1)S(1)}, bf16[672,256]{1,0:T(8,128)(2,1)S(1)}, u32[]{:S(2)}, u32[]{:S(2)}) collective-permute-start(bf16[672,256]{1,0:T(8,128)(2,1)S(1)} %get-tuple-element.52), channel_id=1, source_target_pairs={{0,4},{1,5},{2,6},{3,7},{4,0},{5,1},{6,2},{7,3},{8,12},{9,13},{10,... | collective-permute-start | bytes 1032200 | tf_op jit(solution)/shard_map/ppermute | solution.py:151
  179.6 15.7 %collective-permute-start.18 = (bf16[672,256]{1,0:T(8,128)(2,1)S(1)}, bf16[672,256]{1,0:T(8,128)(2,1)S(1)}, u32[]{:S(2)}, u32[]{:S(2)}) collective-permute-start(bf16[672,256]{1,0:T(8,128)(2,1)S(1)} %get-tuple-element.51), channel_id=1, source_target_pairs={{0,6},{1,7},{2,4},{3,5},{4,2},{5,3},{6,0},{7,1},{8,14},{9,15},{10,... | collective-permute-start | bytes 1032200 | tf_op jit(solution)/shard_map/ppermute | solution.py:151
  179.7 22.3 %collective-permute-start.19 = (bf16[672,256]{1,0:T(8,128)(2,1)S(1)}, bf16[672,256]{1,0:T(8,128)(2,1)}, u32[]{:S(2)}, u32[]{:S(2)}) collective-permute-start(bf16[672,256]{1,0:T(8,128)(2,1)S(1)} %get-tuple-element.50), channel_id=1, source_target_pairs={{0,8},{1,9},{2,10},{3,11},{4,12},{5,13},{6,14},{7,15},{8,0},{9,1},... | collective-permute-start | bytes 1032200 | tf_op jit(solution)/shard_map/ppermute | solution.py:151
  181.4 65.8 %collective-permute-start.14 = (bf16[256,2688]{1,0:T(8,128)(2,1)}, bf16[256,2688]{1,0:T(8,128)(2,1)}, u32[]{:S(2)}, u32[]{:S(2)}) collective-permute-start(bf16[256,2688]{1,0:T(8,128)(2,1)} %collective-permute-done.12.refs_12_), channel_id=1, source_target_pairs={{0,2},{1,3},{2,0},{3,1},{4,6},{5,7},{6,4},{7,5},{8,10},{9,11},{10,... | collective-permute-start | bytes 4128776 | tf_op jit(solution)/shard_map/ppermute | solution.py:151
  188.6 58.7 %collective-permute-start.11 = (bf16[256,2688]{1,0:T(8,128)(2,1)}, bf16[256,2688]{1,0:T(8,128)(2,1)}, u32[]{:S(2)}, u32[]{:S(2)}) collective-permute-start(bf16[256,2688]{1,0:T(8,128)(2,1)} %collective-permute-done.9.refs_9_), channel_id=1, source_target_pairs={{0,2},{1,3},{2,0},{3,1},{4,6},{5,7},{6,4},{7,5},{8,10},{9,11},{10,... | collective-permute-start | bytes 4128776 | tf_op jit(solution)/shard_map/ppermute | solution.py:151
  195.3 51.9 %collective-permute-start.7 = (bf16[256,2688]{1,0:T(8,128)(2,1)S(1)}, bf16[256,2688]{1,0:T(8,128)(2,1)}, u32[]{:S(2)}, u32[]{:S(2)}) collective-permute-start(bf16[256,2688]{1,0:T(8,128)(2,1)S(1)} %collective-permute-done.5.refs_5_), channel_id=1, source_target_pairs={{0,2},{1,3},{2,0},{3,1},{4,6},{5,7},{6,4},{7,5},{8,10},{9,11},{10,... | collective-permute-start | bytes 4128776 | tf_op jit(solution)/shard_map/ppermute | solution.py:151
  199.9 47.4 %collective-permute-start.15 = (bf16[256,2688]{1,0:T(8,128)(2,1)}, bf16[256,2688]{1,0:T(8,128)(2,1)}, u32[]{:S(2)}, u32[]{:S(2)}) collective-permute-start(bf16[256,2688]{1,0:T(8,128)(2,1)} %collective-permute-done.13.refs_13_), channel_id=1, source_target_pairs={{0,2},{1,3},{2,0},{3,1},{4,6},{5,7},{6,4},{7,5},{8,10},{9,11},{10,... | collective-permute-start | bytes 4128776 | tf_op jit(solution)/shard_map/ppermute | solution.py:151
  201.9 101.9 %all-gather.11.cloned.1.call-start = ((), (), s32[]{:S(2)}) async-start(), calls=%async_computation.3 | async-start | bytes 2359296 | tf_op jit(solution)/shard_map/all_gather | solution.py:492
  202.0 11.2 %collective-permute-start.20 = (bf16[672,256]{1,0:T(8,128)(2,1)S(1)}, bf16[672,256]{1,0:T(8,128)(2,1)S(1)}, u32[]{:S(2)}, u32[]{:S(2)}) collective-permute-start(bf16[672,256]{1,0:T(8,128)(2,1)S(1)} %get-tuple-element.49), channel_id=1, source_target_pairs={{0,10},{1,11},{2,8},{3,9},{4,14},{5,15},{6,12},{7,13},{8,2},{9,3},... | collective-permute-start | bytes 1032200 | tf_op jit(solution)/shard_map/ppermute | solution.py:151
  213.2 17.6 %collective-permute-start.21 = (bf16[672,256]{1,0:T(8,128)(2,1)S(1)}, bf16[672,256]{1,0:T(8,128)(2,1)S(1)}, u32[]{:S(2)}, u32[]{:S(2)}) collective-permute-start(bf16[672,256]{1,0:T(8,128)(2,1)S(1)} %get-tuple-element.48), channel_id=1, source_target_pairs={{0,12},{1,13},{2,14},{3,15},{4,8},{5,9},{6,10},{7,11},{8,4},{9,5},... | collective-permute-start | bytes 1032200 | tf_op jit(solution)/shard_map/ppermute | solution.py:151
  230.7 15.0 %collective-permute-start.22 = (bf16[672,256]{1,0:T(8,128)(2,1)S(1)}, bf16[672,256]{1,0:T(8,128)(2,1)S(1)}, u32[]{:S(2)}, u32[]{:S(2)}) collective-permute-start(bf16[672,256]{1,0:T(8,128)(2,1)S(1)} %get-tuple-element.47), channel_id=1, source_target_pairs={{0,14},{1,15},{2,12},{3,13},{4,10},{5,11},{6,8},{7,9},{8,6},{9,7},... | collective-permute-start | bytes 1032200 | tf_op jit(solution)/shard_map/ppermute | solution.py:151
  245.7 69.4 %collective-permute-start.39 = (bf16[336,2048]{1,0:T(8,128)(2,1)}, bf16[336,2048]{1,0:T(8,128)(2,1)}, u32[]{:S(2)}, u32[]{:S(2)}) collective-permute-start(bf16[336,2048]{1,0:T(8,128)(2,1)} %bitcast.8.refs_8_), channel_id=1, source_target_pairs={{0,1},{1,0},{2,3},{3,2},{4,5},{5,4},{6,7},{7,6},{8,9},{9,8},{10,11... | collective-permute-start | bytes 4128776 | tf_op jit(solution)/shard_map/ppermute | solution.py:151
  270.0 26.9 %collective-permute-start.30 = (bf16[4,256,256]{2,1,0:T(8,128)(2,1)}, bf16[4,256,256]{2,1,0:T(8,128)(2,1)}, u32[]{:S(2)}, u32[]{:S(2)}) collective-permute-start(bf16[4,256,256]{2,1,0:T(8,128)(2,1)} %get-tuple-element.41), channel_id=1, source_target_pairs={{0,16},{1,17},{2,18},{3,19},{4,20},{5,21},{6,22},{7,23},{8,24},{9,... | collective-permute-start | bytes 1572872 | tf_op jit(solution)/shard_map/ppermute | solution.py:486
  282.5 9.5 %collective-permute-start.42 = (bf16[4,128,256]{2,1,0:T(8,128)(2,1)}, bf16[4,128,256]{2,1,0:T(8,128)(2,1)}, u32[]{:S(2)}, u32[]{:S(2)}) collective-permute-start(bf16[4,128,256]{2,1,0:T(8,128)(2,1)} %get-tuple-element.46), channel_id=1, source_target_pairs={{0,1},{1,0},{2,3},{3,2},{4,5},{5,4},{6,7},{7,6},{8,9},{9,8},{10,11... | collective-permute-start | bytes 786440 | tf_op jit(solution)/shard_map/ppermute | solution.py:151
  285.1 30.0 %collective-permute-start.41 = (bf16[144,2048]{1,0:T(8,128)(2,1)}, bf16[144,2048]{1,0:T(8,128)(2,1)}, u32[]{:S(2)}, u32[]{:S(2)}) collective-permute-start(bf16[144,2048]{1,0:T(8,128)(2,1)} %dynamic-slice_bitcast_fusion.1.refs_12_), channel_id=1, source_target_pairs={{0,1},{1,0},{2,3},{3,2},{4,5},{5,4},{6,7},{7,6},{8,9},{9,8},{10,11... | collective-permute-start | bytes 1769480 | tf_op jit(solution)/shard_map/ppermute | solution.py:151
  293.9 32.5 %collective-permute-start.46 = (bf16[2,4,128,256]{3,2,1,0:T(8,128)(2,1)}, bf16[2,4,128,256]{3,2,1,0:T(8,128)(2,1)}, u32[]{:S(2)}, u32[]{:S(2)}) collective-permute-start(bf16[2,4,128,256]{3,2,1,0:T(8,128)(2,1)} %shard_map.97.refs_0_), channel_id=1, source_target_pairs={{0,8},{1,9},{2,10},{3,11},{4,12},{5,13},{6,14},{7,15},{8,0},{9,1},... | collective-permute-start | bytes 1572872 | tf_op jit(solution)/shard_map/ppermute | solution.py:151
  303.0 9.5 %collective-permute-start.31 = (bf16[4,128,256]{2,1,0:T(8,128)(2,1)}, bf16[4,128,256]{2,1,0:T(8,128)(2,1)}, u32[]{:S(2)}, u32[]{:S(2)}) collective-permute-start(bf16[4,128,256]{2,1,0:T(8,128)(2,1)} %get-tuple-element.43), channel_id=1, source_target_pairs={{0,1},{1,0},{2,3},{3,2},{4,5},{5,4},{6,7},{7,6},{8,9},{9,8},{10,11... | collective-permute-start | bytes 786440 | tf_op jit(solution)/shard_map/ppermute | solution.py:151
  305.9 20.8 %collective-permute-start.40 = (bf16[192,2048]{1,0:T(8,128)(2,1)}, bf16[192,2048]{1,0:T(8,128)(2,1)}, u32[]{:S(2)}, u32[]{:S(2)}) collective-permute-start(bf16[192,2048]{1,0:T(8,128)(2,1)} %dynamic-slice_bitcast_fusion.refs_10_), channel_id=1, source_target_pairs={{0,1},{1,0},{2,3},{3,2},{4,5},{5,4},{6,7},{7,6},{8,9},{9,8},{10,11... | collective-permute-start | bytes 2359304 | tf_op jit(solution)/shard_map/ppermute | solution.py:151
  312.4 14.3 %collective-permute-start.44 = (bf16[2,4,128,256]{3,2,1,0:T(8,128)(2,1)}, bf16[2,4,128,256]{3,2,1,0:T(8,128)(2,1)}, u32[]{:S(2)}, u32[]{:S(2)}) collective-permute-start(bf16[2,4,128,256]{3,2,1,0:T(8,128)(2,1)} %shard_map.97.refs_0_), channel_id=1, source_target_pairs={{0,4},{1,5},{2,6},{3,7},{4,0},{5,1},{6,2},{7,3},{8,12},{9,13},{10,... | collective-permute-start | bytes 1572872 | tf_op jit(solution)/shard_map/ppermute | solution.py:151
  315.1 12.1 %collective-permute-start.43 = (bf16[2,4,128,256]{3,2,1,0:T(8,128)(2,1)}, bf16[2,4,128,256]{3,2,1,0:T(8,128)(2,1)}, u32[]{:S(2)}, u32[]{:S(2)}) collective-permute-start(bf16[2,4,128,256]{3,2,1,0:T(8,128)(2,1)} %shard_map.97.refs_0_), channel_id=1, source_target_pairs={{0,2},{1,3},{2,0},{3,1},{4,6},{5,7},{6,4},{7,5},{8,10},{9,11},{10,... | collective-permute-start | bytes 1572872 | tf_op jit(solution)/shard_map/ppermute | solution.py:151
  315.1 24.1 %collective-permute-start.35 = (bf16[2,4,128,256]{3,2,1,0:T(8,128)(2,1)}, bf16[2,4,128,256]{3,2,1,0:T(8,128)(2,1)}, u32[]{:S(2)}, u32[]{:S(2)}) collective-permute-start(bf16[2,4,128,256]{3,2,1,0:T(8,128)(2,1)} %shard_map.95.refs_0_), channel_id=1, source_target_pairs={{0,8},{1,9},{2,10},{3,11},{4,12},{5,13},{6,14},{7,15},{8,0},{9,1},... | collective-permute-start | bytes 1572872 | tf_op jit(solution)/shard_map/ppermute | solution.py:151
  326.4 15.0 %collective-permute-start.48 = (bf16[2,4,128,256]{3,2,1,0:T(8,128)(2,1)}, bf16[2,4,128,256]{3,2,1,0:T(8,128)(2,1)S(1)}, u32[]{:S(2)}, u32[]{:S(2)}) collective-permute-start(bf16[2,4,128,256]{3,2,1,0:T(8,128)(2,1)} %collective-permute-done.46.refs_4_), channel_id=1, source_target_pairs={{0,4},{1,5},{2,6},{3,7},{4,0},{5,1},{6,2},{7,3},{8,12},{9,13},{10,... | collective-permute-start | bytes 1572872 | tf_op jit(solution)/shard_map/ppermute | solution.py:151
  326.7 15.5 %collective-permute-start.45 = (bf16[2,4,128,256]{3,2,1,0:T(8,128)(2,1)}, bf16[2,4,128,256]{3,2,1,0:T(8,128)(2,1)}, u32[]{:S(2)}, u32[]{:S(2)}) collective-permute-start(bf16[2,4,128,256]{3,2,1,0:T(8,128)(2,1)} %collective-permute-done.44.refs_2_), channel_id=1, source_target_pairs={{0,2},{1,3},{2,0},{3,1},{4,6},{5,7},{6,4},{7,5},{8,10},{9,11},{10,... | collective-permute-start | bytes 1572872 | tf_op jit(solution)/shard_map/ppermute | solution.py:151
  326.7 16.0 %collective-permute-start.47 = (bf16[2,4,128,256]{3,2,1,0:T(8,128)(2,1)}, bf16[2,4,128,256]{3,2,1,0:T(8,128)(2,1)}, u32[]{:S(2)}, u32[]{:S(2)}) collective-permute-start(bf16[2,4,128,256]{3,2,1,0:T(8,128)(2,1)} %collective-permute-done.46.refs_4_), channel_id=1, source_target_pairs={{0,2},{1,3},{2,0},{3,1},{4,6},{5,7},{6,4},{7,5},{8,10},{9,11},{10,... | collective-permute-start | bytes 1572872 | tf_op jit(solution)/shard_map/ppermute | solution.py:151
  327.2 25.5 %collective-permute-start.33 = (bf16[2,4,128,256]{3,2,1,0:T(8,128)(2,1)}, bf16[2,4,128,256]{3,2,1,0:T(8,128)(2,1)}, u32[]{:S(2)}, u32[]{:S(2)}) collective-permute-start(bf16[2,4,128,256]{3,2,1,0:T(8,128)(2,1)} %shard_map.95.refs_0_), channel_id=1, source_target_pairs={{0,4},{1,5},{2,6},{3,7},{4,0},{5,1},{6,2},{7,3},{8,12},{9,13},{10,... | collective-permute-start | bytes 1572872 | tf_op jit(solution)/shard_map/ppermute | solution.py:151
  339.2 23.9 %collective-permute-start.37 = (bf16[2,4,128,256]{3,2,1,0:T(8,128)(2,1)}, bf16[2,4,128,256]{3,2,1,0:T(8,128)(2,1)}, u32[]{:S(2)}, u32[]{:S(2)}) collective-permute-start(bf16[2,4,128,256]{3,2,1,0:T(8,128)(2,1)} %collective-permute-done.35.refs_4_), channel_id=1, source_target_pairs={{0,4},{1,5},{2,6},{3,7},{4,0},{5,1},{6,2},{7,3},{8,12},{9,13},{10,... | collective-permute-start | bytes 1572872 | tf_op jit(solution)/shard_map/ppermute | solution.py:151
  342.2 21.0 %collective-permute-start.49 = (bf16[2,4,128,256]{3,2,1,0:T(8,128)(2,1)S(1)}, bf16[2,4,128,256]{3,2,1,0:T(8,128)(2,1)}, u32[]{:S(2)}, u32[]{:S(2)}) collective-permute-start(bf16[2,4,128,256]{3,2,1,0:T(8,128)(2,1)S(1)} %collective-permute-done.48.refs_6_), channel_id=1, source_target_pairs={{0,2},{1,3},{2,0},{3,1},{4,6},{5,7},{6,4},{7,5},{8,10},{9,11},{10,... | collective-permute-start | bytes 1572872 | tf_op jit(solution)/shard_map/ppermute | solution.py:151
  342.2 29.5 %collective-permute-start.32 = (bf16[2,4,128,256]{3,2,1,0:T(8,128)(2,1)}, bf16[2,4,128,256]{3,2,1,0:T(8,128)(2,1)}, u32[]{:S(2)}, u32[]{:S(2)}) collective-permute-start(bf16[2,4,128,256]{3,2,1,0:T(8,128)(2,1)} %shard_map.95.refs_0_), channel_id=1, source_target_pairs={{0,2},{1,3},{2,0},{3,1},{4,6},{5,7},{6,4},{7,5},{8,10},{9,11},{10,... | collective-permute-start | bytes 1572872 | tf_op jit(solution)/shard_map/ppermute | solution.py:151
  342.7 29.0 %collective-permute-start.36 = (bf16[2,4,128,256]{3,2,1,0:T(8,128)(2,1)}, bf16[2,4,128,256]{3,2,1,0:T(8,128)(2,1)}, u32[]{:S(2)}, u32[]{:S(2)}) collective-permute-start(bf16[2,4,128,256]{3,2,1,0:T(8,128)(2,1)} %collective-permute-done.35.refs_4_), channel_id=1, source_target_pairs={{0,2},{1,3},{2,0},{3,1},{4,6},{5,7},{6,4},{7,5},{8,10},{9,11},{10,... | collective-permute-start | bytes 1572872 | tf_op jit(solution)/shard_map/ppermute | solution.py:151
  352.7 19.0 %collective-permute-start.34 = (bf16[2,4,128,256]{3,2,1,0:T(8,128)(2,1)}, bf16[2,4,128,256]{3,2,1,0:T(8,128)(2,1)}, u32[]{:S(2)}, u32[]{:S(2)}) collective-permute-start(bf16[2,4,128,256]{3,2,1,0:T(8,128)(2,1)} %collective-permute-done.33.refs_2_), channel_id=1, source_target_pairs={{0,2},{1,3},{2,0},{3,1},{4,6},{5,7},{6,4},{7,5},{8,10},{9,11},{10,... | collective-permute-start | bytes 1572872 | tf_op jit(solution)/shard_map/ppermute | solution.py:151
  363.2 8.6 %collective-permute-start.38 = (bf16[2,4,128,256]{3,2,1,0:T(8,128)(2,1)}, bf16[2,4,128,256]{3,2,1,0:T(8,128)(2,1)}, u32[]{:S(2)}, u32[]{:S(2)}) collective-permute-start(bf16[2,4,128,256]{3,2,1,0:T(8,128)(2,1)} %collective-permute-done.37.refs_6_), channel_id=1, source_target_pairs={{0,2},{1,3},{2,0},{3,1},{4,6},{5,7},{6,4},{7,5},{8,10},{9,11},{10,... | collective-permute-start | bytes 1572872 | tf_op jit(solution)/shard_map/ppermute | solution.py:151
  (24 other events, 302.2 us)
Sparse Core Ops, SparseCore 0:
  11.0 72.6 all-gather.6
  103.0 70.0 all-gather.8
  202.0 38.9 all-gather.12
  242.4 43.9 all-gather.10

commit v6 on v5

--- a/solution.py
+++ b/solution.py
@@ -193,26 +193,26 @@
     return scaled * cosine + pltpu.roll(scaled, HD // 2, 1) * sine
 
 
-def project_kernel(n, reach, heads, meta, cosine, sine, key_gain, query_gain, *refs):
-    blocks, kv_parts = refs[: 2 * n], refs[2 * n : 3 * n]
-    q_rows = refs[3 * n]
-    kv_out, tail_out, q_out = refs[3 * n + 1 : 3 * n + 4]
-    block_mem, kv_mem, q_mem, block_sem, weight_sem = refs[3 * n + 4 :]
+def project_kernel(n, reach, heads, meta, cosine, sine, gain, *refs):
+    blocks = refs[: 2 * n]
+    weights = refs[2 * n : -6 if heads == 0 else -5]
+    block_mem, weight_mem, block_sem, weight_sem = refs[-4:]
     place, col = meta[0], meta[2]
-    _, _, tokens, _ = block_mem.shape
-    deep = kv_parts[0].shape[0] // 2
+    tokens = block_mem.shape[2]
+    deep = weight_mem.shape[1] // n
     copies = []
     for m in range(n):
         rows = pl.ds(pl.multiple_of(lax.bitwise_xor(place, m) * deep, 16), deep)
         for half in range(2):
-            for k, (source, target) in enumerate(
-                [
-                    (kv_parts[m].at[pl.ds(half * deep, deep)], kv_mem.at[half, rows, :]),
-                    (q_rows.at[pl.ds((half * n + m) * deep, deep)], q_mem.at[half, rows, :]),
-                ]
-            ):
-                sem = weight_sem.at[4 * m + 2 * half + k]
-                copies.append(pltpu.make_async_copy(source, target, sem))
+            if heads == 0:
+                source = weights[m].at[pl.ds(half * deep, deep)]
+            else:
+                source = weights[0].at[pl.ds((half * n + m) * deep, deep)]
+            copies.append(
+                pltpu.make_async_copy(
+                    source, weight_mem.at[half, rows, :], weight_sem.at[2 * m + half]
+                )
+            )
 
     def loads(m):
         return [
@@ -220,7 +220,7 @@
             for side in range(2)
         ]
 
-    ahead = 1
+    ahead = 2
     for copy in copies:
         copy.start()
     for m in range(ahead):
@@ -240,32 +240,34 @@
 
         for side in range(2):
             pltpu.make_async_copy(blocks[side], block_mem.at[side, t], block_sem.at[t, side]).wait()
-        kv, q = [
-            jnp.dot(block_mem[0, t], mem[col], preferred_element_type=jnp.float32)
-            + jnp.dot(
-                block_mem[1, t],
-                mem[lax.bitwise_xor(col, 1)],
-                preferred_element_type=jnp.float32,
-            )
-            for mem in (kv_mem, q_mem)
-        ]
+        raw = jnp.dot(
+            block_mem[0, t], weight_mem[col], preferred_element_type=jnp.float32
+        ) + jnp.dot(
+            block_mem[1, t],
+            weight_mem[lax.bitwise_xor(col, 1)],
+            preferred_element_type=jnp.float32,
+        )
         at = lax.bitwise_xor(place, t)
         cosine_here, sine_here = cosine[at], sine[at]
-        keys = normed_rotated(kv[:, :HD], key_gain[...], cosine_here, sine_here)
-        keys = keys.astype(jnp.bfloat16)
-        values = kv[:, HD : 2 * HD].astype(jnp.bfloat16)
-        kv_out[at, :, :HD] = keys
-        kv_out[at, :, HD:] = values
+        if heads == 0:
+            kv_out, tail_out = refs[-6:-4]
+            keys = normed_rotated(raw[:, :HD], gain[...], cosine_here, sine_here)
+            keys = keys.astype(jnp.bfloat16)
+            values = raw[:, HD:].astype(jnp.bfloat16)
+            kv_out[at, :, :HD] = keys
+            kv_out[at, :, HD:] = values
+
+            @pl.when(at >= n - reach)
+            def _():
+                tail_out[at - (n - reach), :, :HD] = keys
+                tail_out[at - (n - reach), :, HD:] = values
+
+        q_out = refs[-5]
         for h in range(heads):
             query = normed_rotated(
-                q[:, h * HD : (h + 1) * HD], query_gain[...], cosine_here, sine_here
+                raw[:, h * HD : (h + 1) * HD], gain[...], cosine_here, sine_here
             )
             q_out[at, pl.ds(h * tokens, tokens), :] = query.astype(jnp.bfloat16)
-
-        @pl.when(at >= n - reach)
-        def _():
-            tail_out[at - (n - reach), :, :HD] = keys
-            tail_out[at - (n - reach), :, HD:] = values
 
 
 def attend_kernel(low, count, reach, heads, meta, q_doc, k_doc, queries, kv_own, *refs):
@@ -310,7 +312,7 @@
 
 
 def output_kernel(n, size, meta, *refs):
-    contexts, weights, after = refs[:n], refs[n : n + 6], refs[n + 6 : -5]
+    contexts, weights, after = refs[:n], refs[n : n + 8], refs[n + 8 : -5]
     out, context_mem, weight_mem, context_sem, weight_sem = refs[-5:]
     place, half, col = meta[0], meta[1], meta[2]
     rows_all, deep = weights[0].shape
@@ -319,7 +321,7 @@
     copies = []
     for k, source in enumerate(weights):
         first = (half if k < 2 else lax.bitwise_xor(half, 1)) * rows_all
-        first = first + (0 if k < 4 else weights[2].shape[0])
+        first = first + sum(weights[j].shape[0] for j in range(2 + k % 2, k, 2))
         side = pl.multiple_of(lax.bitwise_xor(col, k % 2) * deep, 128)
         copies.append(
             pltpu.make_async_copy(
@@ -454,43 +456,43 @@
         piece = lax.dynamic_slice_in_dim(kv_rows, first, 2 * HD, 1)
         kv_parts.append(piece if m == 0 else swapped(piece, m, 0))
 
-    flops = 2 * n * tokens * 2 * features * (2 + heads) * HD
-    kv_own, kv_tail, queries = run(
-        functools.partial(project_kernel, n, reach, heads),
-        [
-            shaped((n, tokens, 2 * HD), bf16),
-            shaped((reach, tokens, 2 * HD), bf16),
-            shaped((n, heads * tokens, HD), bf16),
-        ],
-        [SMEM, VMEM, VMEM, VMEM, VMEM] + [ANY] * (3 * n + 1),
-        [VMEM, VMEM, VMEM],
-        [
-            pltpu.VMEM((2, n, tokens, features), bf16),
-            pltpu.VMEM((2, features, 2 * HD), bf16),
-            pltpu.VMEM((2, features, heads * HD), bf16),
-            pltpu.SemaphoreType.DMA((n, 2)),
-            pltpu.SemaphoreType.DMA((4 * n,)),
-        ],
-        flops,
-        2 * n * tokens * features * 2,
-    )(
-        meta,
-        cosine,
-        sine,
-        key_gain.reshape(1, HD),
-        query_gain.reshape(1, HD),
-        *block_list,
-        *kv_parts,
-        q_rows,
+    def project(kept, gain, weights, outs):
+        return run(
+            functools.partial(project_kernel, n, reach, kept),
+            outs,
+            [SMEM, VMEM, VMEM, VMEM] + [ANY] * (2 * n + len(weights)),
+            [VMEM] * len(outs),
+            [
+                pltpu.VMEM((2, n, tokens, features), bf16),
+                pltpu.VMEM((2, features, (kept or 2) * HD), bf16),
+                pltpu.SemaphoreType.DMA((n, 2)),
+                pltpu.SemaphoreType.DMA((2 * n,)),
+            ],
+            2 * n * tokens * 2 * features * (kept or 2) * HD,
+            2 * n * tokens * features * 2,
+        )(meta, cosine, sine, gain.reshape(1, HD), *block_list, *weights)
+
+    kv_own, kv_tail = project(
+        0,
+        key_gain,
+        kv_parts,
+        [shaped((n, tokens, 2 * HD), bf16), shaped((reach, tokens, 2 * HD), bf16)],
     )
     kv_back = lax.ppermute(kv_tail, "half", [(0, 1)])
+    queries = project(heads, query_gain, [q_rows], [shaped((n, heads * tokens, HD), bf16)])[0]
 
     own_weight, _ = lax.optimization_barrier((output_weight.T, q_own))
-    ahead = own_weight.shape[0] * 4 // 7 // 16 * 16
+    rows_all = own_weight.shape[0]
+    step = rows_all * 8 // 21 // 16 * 16
+    cuts = [0, rows_all - 2 * step, rows_all - step, rows_all]
     out_weights = [own_weight, swapped(own_weight, 0, 1)]
-    for rows in [own_weight[:ahead], own_weight[ahead:]]:
-        both = lax.all_gather(rows, "half", axis=0)
-        piece = lax.dynamic_index_in_dim(both, 1 - half, 0, keepdims=False)
+    for k in range(3):
+        piece = own_weight[cuts[k] : cuts[k + 1]]
+        if k == 0:
+            piece = lax.ppermute(piece, "half", [(0, 1), (1, 0)])
+        else:
+            both = lax.all_gather(piece, "half", axis=0)
+            piece = lax.dynamic_index_in_dim(both, 1 - half, 0, keepdims=False)
         out_weights += [piece, swapped(piece, 0, 1)]
 
     contexts = []
@@ -534,13 +536,13 @@
             run(
                 functools.partial(output_kernel, n, count),
                 shaped((blocks_out, out_cols, part), bf16),
-                [SMEM] + [ANY] * (n + 6) + [VMEM] * len(result),
+                [SMEM] + [ANY] * (n + 8) + [VMEM] * len(result),
                 VMEM,
                 [
                     pltpu.VMEM((count, part, 2 * deep_out), bf16),
                     pltpu.VMEM((2 * out_cols, 2 * deep_out), bf16),
                     pltpu.SemaphoreType.DMA((2 * n,)),
-                    pltpu.SemaphoreType.DMA((6,)),
+                    pltpu.SemaphoreType.DMA((8,)),
                 ],
                 8 * count * part * deep_out * out_cols,
                 8 * deep_out * out_cols,

time: 420 us -> 420 us (level)
  starting transfers between devices: 60.1 us -> 48 us
  waiting for transfers between devices: 228 us -> 236 us
  Pallas kernels: 65.8 us -> 72.6 us
    ppermute x49 -> x50, starting transfers between devices: 55.4 us -> 41.7 us  [swapped(): return lax.ppermute(value, ('place', 'cols'), pairs)]
    ppermute x49 -> x50, waiting for transfers between devices: 228 us -> 236 us  [swapped(): return lax.ppermute(value, ('place', 'cols'), pairs)]
    pallas_call x1 -> x2, Pallas kernels: 22.6 us -> 29.5 us  [project(): run(functools.partial(project_kernel, n, reach, kept), outs, [SMEM, VMEM,...]
  transfers between devices with their start and end apart: 54 -> 56, of which waited for: 23 -> 23; matrix products, arithmetic and copies ran while one was open for 5% -> 5% of each run, Pallas kernels for 12% -> 14%
where the time goes in v6:
time: 420 us; the launch traced here: 419 us
  waiting for transfers between devices  236 us (56%)
  Pallas kernels  72.6 us (17%)
  starting transfers between devices  48 us (11%)
  blocking collectives  24.7 us (6%)
  local copies, waits for them, and re-layouts  15.4 us (4%)
  between operations  13.4 us (3%)
  other arithmetic  9.6 us (2%)
    ppermute x50, waiting for transfers between devices, swapped(): return lax.ppermute(value, ('place', 'cols'), pairs)  236 us
    ppermute x50, starting transfers between devices, swapped(): return lax.ppermute(value, ('place', 'cols'), pairs)  41.7 us
    pallas_call x2, Pallas kernels, project(): run(functools.partial(project_kernel, n, reach, kept), outs, [SMEM, VMEM,...  29.5 us
    all_to_all x1, blocking collectives, split_body(): arrived = lax.all_to_all(result[0], ('place', 'cols'), 0, 0, tiled=True)  24.7 us
    pallas_call x2, Pallas kernels, split_body(): run(functools.partial(output_kernel, n, count), shaped((blocks_out, out_c...  17.8 us
    pallas_call x2, Pallas kernels, split_body(): run(functools.partial(attend_kernel, low, count, reach, heads), [shape, s...  12 us
  transfers between devices with their start and end apart: 56, of which 23 were waited for; matrix products, arithmetic and copies ran while one was open for 5% of the time, Pallas kernels for 14%

profile of v6, /device:TPU:0, one launch (start us, length us, event | category | flops | bytes accessed | tf_op | source)
XLA Modules:
  0.0 419.3 jit_solution(2154107342294653649)
XLA Ops:
  8.2 3.0 collective-permute-start
  11.9 3.7 shard_map.91
  23.6 3.8 collective-permute-done.17.refs_2_
  31.6 52.4 %collective-permute-done.19.refs_4_ = bf16[336,256]{1,0:T(8,128)(2,1)} collective-permute-done((bf16[336,256]{1,0:T(8,128)(2,1)S(1)}, bf16[336,256]{1,0:T(8,128)(2,1)}, u32[]{:S(2)}, u32[]{:S(2)}) %collective-permute-start.19) | collective-permute-done | bytes 172064 | tf_op jit(solution)/shard_map/ppermute | solution.py:151
  84.1 3.6 collective-permute-done.20.refs_5_
  88.8 3.1 collective-permute-done.21.refs_6_
  93.3 5.6 %collective-permute-done.22.refs_7_ = bf16[336,256]{1,0:T(8,128)(2,1)} collective-permute-done((bf16[336,256]{1,0:T(8,128)(2,1)S(1)}, bf16[336,256]{1,0:T(8,128)(2,1)}, u32[]{:S(2)}, u32[]{:S(2)}) %collective-permute-start.22) | collective-permute-done | bytes 172064 | tf_op jit(solution)/shard_map/ppermute | solution.py:151
  99.4 2.6 shard_map.92
  103.7 13.8 %collective-permute-done.1.refs_1_ = bf16[256,2688]{1,0:T(8,128)(2,1)} collective-permute-done((bf16[256,2688]{1,0:T(8,128)(2,1)}, bf16[256,2688]{1,0:T(8,128)(2,1)}, u32[]{:S(2)}, u32[]{:S(2)}) %collective-permute-start.1) | collective-permute-done | bytes 1376288 | tf_op jit(solution)/shard_map/ppermute | solution.py:151
  118.0 10.2 %collective-permute-done.12.refs_12_ = bf16[256,2688]{1,0:T(8,128)(2,1)} collective-permute-done((bf16[256,2688]{1,0:T(8,128)(2,1)}, bf16[256,2688]{1,0:T(8,128)(2,1)}, u32[]{:S(2)}, u32[]{:S(2)}) %collective-permute-start.12) | collective-permute-done | bytes 1376288 | tf_op jit(solution)/shard_map/ppermute | solution.py:151
  128.4 18.5 %collective-permute-done.9.refs_9_ = bf16[256,2688]{1,0:T(8,128)(2,1)} collective-permute-done((bf16[256,2688]{1,0:T(8,128)(2,1)}, bf16[256,2688]{1,0:T(8,128)(2,1)}, u32[]{:S(2)}, u32[]{:S(2)}) %collective-permute-start.9) | collective-permute-done | bytes 1376288 | tf_op jit(solution)/shard_map/ppermute | solution.py:151
  147.0 3.7 fusion.3
  150.8 2.1 pad_maximum_fusion
  152.8 2.8 constant_dynamic-slice_fusion
  155.6 20.7 %collective-permute-done.5.refs_5_ = bf16[256,2688]{1,0:T(8,128)(2,1)S(1)} collective-permute-done((bf16[256,2688]{1,0:T(8,128)(2,1)}, bf16[256,2688]{1,0:T(8,128)(2,1)S(1)}, u32[]{:S(2)}, u32[]{:S(2)}) %collective-permute-start.5) | collective-permute-done | bytes 1376288 | tf_op jit(solution)/shard_map/ppermute | solution.py:151
  178.2 2.5 collective-permute-start.26
  180.8 6.5 %collective-permute-done.24.refs_18_ = bf16[672,256]{1,0:T(8,128)(2,1)S(1)} collective-permute-done((bf16[672,256]{1,0:T(8,128)(2,1)S(1)}, bf16[672,256]{1,0:T(8,128)(2,1)S(1)}, u32[]{:S(2)}, u32[]{:S(2)}) %collective-permute-start.24) | collective-permute-done | bytes 344096 | tf_op jit(solution)/shard_map/ppermute | solution.py:151
  187.4 6.3 %collective-permute-done.25.refs_19_ = bf16[672,256]{1,0:T(8,128)(2,1)S(1)} collective-permute-done((bf16[672,256]{1,0:T(8,128)(2,1)S(1)}, bf16[672,256]{1,0:T(8,128)(2,1)S(1)}, u32[]{:S(2)}, u32[]{:S(2)}) %collective-permute-start.25) | collective-permute-done | bytes 344096 | tf_op jit(solution)/shard_map/ppermute | solution.py:151
  194.4 5.2 %collective-permute-done.13.refs_13_ = bf16[256,2688]{1,0:T(8,128)(2,1)} collective-permute-done((bf16[256,2688]{1,0:T(8,128)(2,1)}, bf16[256,2688]{1,0:T(8,128)(2,1)}, u32[]{:S(2)}, u32[]{:S(2)}) %collective-permute-start.13) | collective-permute-done | bytes 1376288 | tf_op jit(solution)/shard_map/ppermute | solution.py:151
  199.6 2.3 fusion.4
  202.0 2.8 collective-permute-start.27
  204.8 10.2 %collective-permute-done.27.refs_21_ = bf16[672,256]{1,0:T(8,128)(2,1)S(1)} collective-permute-done((bf16[672,256]{1,0:T(8,128)(2,1)}, bf16[672,256]{1,0:T(8,128)(2,1)S(1)}, u32[]{:S(2)}, u32[]{:S(2)}) %collective-permute-start.27) | collective-permute-done | bytes 344096 | tf_op jit(solution)/shard_map/ppermute | solution.py:151
  215.6 16.3 %collective-permute-done.28.refs_22_ = bf16[672,256]{1,0:T(8,128)(2,1)S(1)} collective-permute-done((bf16[672,256]{1,0:T(8,128)(2,1)S(1)}, bf16[672,256]{1,0:T(8,128)(2,1)S(1)}, u32[]{:S(2)}, u32[]{:S(2)}) %collective-permute-start.28) | collective-permute-done | bytes 344096 | tf_op jit(solution)/shard_map/ppermute | solution.py:151
  232.6 2.7 collective-permute-start.29
  235.9 1.7 slice.24
  239.0 6.1 %collective-permute-done.29.refs_23_ = bf16[672,256]{1,0:T(8,128)(2,1)S(1)} collective-permute-done((bf16[672,256]{1,0:T(8,128)(2,1)S(1)}, bf16[672,256]{1,0:T(8,128)(2,1)S(1)}, u32[]{:S(2)}, u32[]{:S(2)}) %collective-permute-start.29) | collective-permute-done | bytes 344096 | tf_op jit(solution)/shard_map/ppermute | solution.py:151
  246.1 2.8 collective-permute-start.40
  248.8 14.7 %shard_map.94 = (bf16[8,256,256]{2,1,0:T(8,128)(2,1)}, bf16[4,256,256]{2,1,0:T(8,128)(2,1)}) custom-call(s32[3]{0:T(128)} %pad_add_fusion.meta, f32[8,256,128]{2,1,0:T(8,128)} %get-tuple-element.27.cosine, f32[8,256,128]{2,1,0:T(8,128)} %get-tuple-element.28.sine, f32[1,128]{1,0:T(1,128)} %bitcast.22, bf16[256,2688]{1,0:T(8,128)(2,1)} %fusion.2.refs_0_, ...), custom_call_target="tpu_custom_call" | custom-call | flops 5637144576 | bytes 22020096 | tf_op jit(solution)/shard_map/pallas_call | solution.py:460
  263.5 3.4 collective-permute-start.30
  266.9 14.8 %shard_map.93.queries = bf16[8,512,128]{2,1,0:T(8,128)(2,1)} custom-call(s32[3]{0:T(128)} %pad_add_fusion.meta, f32[8,256,128]{2,1,0:T(8,128)} %get-tuple-element.27.cosine, f32[8,256,128]{2,1,0:T(8,128)} %get-tuple-element.28.sine, f32[1,128]{1,0:T(1,128)} %bitcast.23, bf16[256,2688]{1,0:T(8,128)(2,1)} %fusion.2.refs_0_, ...), custom_call_target="tpu_custom_call" | custom-call | flops 5637144576 | bytes 22020096 | tf_op jit(solution)/shard_map/pallas_call | solution.py:460
  281.7 6.0 %shard_map.97 = (bf16[4,128,256]{2,1,0:T(8,128)(2,1)}, bf16[4,128,256]{2,1,0:T(8,128)(2,1)}) custom-call(s32[3]{0:T(128)} %pad_add_fusion.meta, s32[8,256,1]{2,1,0:T(8,128)} %copy.10.q_doc, s32[12,1,256]{2,1,0:T(1,128)} %bitcast.19, bf16[8,512,128]{2,1,0:T(8,128)(2,1)} %shard_map.93.queries, bf16[8,256,256]{2,1,0:T(8,128)(2,1)} %get-tuple-element.38.kv_own), custom_call_target="tpu_custom_call" | custom-call | flops 2684354560 | bytes 2097152 | tf_op jit(solution)/shard_map/pallas_call | solution.py:503
  289.0 1.9 dynamic-slice_bitcast_fusion.1.refs_12_
  292.9 4.2 collective-permute-done.44.second
  297.1 1.9 shard_map.98.refs_0_
  299.0 6.1 %shard_map.95 = (bf16[4,128,256]{2,1,0:T(8,128)(2,1)}, bf16[4,128,256]{2,1,0:T(8,128)(2,1)}) custom-call(s32[3]{0:T(128)} %pad_add_fusion.meta, s32[8,256,1]{2,1,0:T(8,128)} %copy.10.q_doc, s32[12,1,256]{2,1,0:T(1,128)} %bitcast.20, bf16[8,512,128]{2,1,0:T(8,128)(2,1)} %shard_map.93.queries, bf16[8,256,256]{2,1,0:T(8,128)(2,1)} %get-tuple-element.38.kv_own, ...), custom_call_target="tpu_custom_call" | custom-call | flops 2684354560 | bytes 2097152 | tf_op jit(solution)/shard_map/pallas_call | solution.py:503
  306.5 1.9 dynamic-slice_bitcast_fusion.refs_14_
  308.4 11.6 %collective-permute-done.31.second = bf16[4,128,256]{2,1,0:T(8,128)(2,1)} collective-permute-done((bf16[4,128,256]{2,1,0:T(8,128)(2,1)}, bf16[4,128,256]{2,1,0:T(8,128)(2,1)}, u32[]{:S(2)}, u32[]{:S(2)}) %collective-permute-start.31) | collective-permute-done | bytes 262176 | tf_op jit(solution)/shard_map/ppermute | solution.py:151
  320.0 1.9 shard_map.96.refs_0_
  323.1 3.9 collective-permute-start.35
  327.5 7.6 %collective-permute-done.46.refs_2_ = bf16[2,4,128,256]{3,2,1,0:T(8,128)(2,1)} collective-permute-done((bf16[2,4,128,256]{3,2,1,0:T(8,128)(2,1)}, bf16[2,4,128,256]{3,2,1,0:T(8,128)(2,1)}, u32[]{:S(2)}, u32[]{:S(2)}) %collective-permute-start.46) | collective-permute-done | bytes 524320 | tf_op jit(solution)/shard_map/ppermute | solution.py:151
  336.9 3.0 collective-permute-done.35.refs_4_
  340.3 5.9 %collective-permute-done.50.refs_6_ = bf16[2,4,128,256]{3,2,1,0:T(8,128)(2,1)S(1)} collective-permute-done((bf16[2,4,128,256]{3,2,1,0:T(8,128)(2,1)}, bf16[2,4,128,256]{3,2,1,0:T(8,128)(2,1)S(1)}, u32[]{:S(2)}, u32[]{:S(2)}) %collective-permute-start.50) | collective-permute-done | bytes 524320 | tf_op jit(solution)/shard_map/ppermute | solution.py:151
  347.6 10.0 %collective-permute-done.33.refs_2_ = bf16[2,4,128,256]{3,2,1,0:T(8,128)(2,1)} collective-permute-done((bf16[2,4,128,256]{3,2,1,0:T(8,128)(2,1)}, bf16[2,4,128,256]{3,2,1,0:T(8,128)(2,1)}, u32[]{:S(2)}, u32[]{:S(2)}) %collective-permute-start.33) | collective-permute-done | bytes 524320 | tf_op jit(solution)/shard_map/ppermute | solution.py:151
  357.6 9.4 %collective-permute-done.37.refs_6_ = bf16[2,4,128,256]{3,2,1,0:T(8,128)(2,1)} collective-permute-done((bf16[2,4,128,256]{3,2,1,0:T(8,128)(2,1)}, bf16[2,4,128,256]{3,2,1,0:T(8,128)(2,1)}, u32[]{:S(2)}, u32[]{:S(2)}) %collective-permute-start.37) | collective-permute-done | bytes 524320 | tf_op jit(solution)/shard_map/ppermute | solution.py:151
  367.0 8.6 %shard_map.99.refs_16_ = bf16[8,336,128]{2,1,0:T(8,128)(2,1)} custom-call(s32[3]{0:T(128)} %pad_add_fusion.meta, bf16[2,4,128,256]{3,2,1,0:T(8,128)(2,1)} %shard_map.98.refs_0_, bf16[2,4,128,256]{3,2,1,0:T(8,128)(2,1)} %collective-permute-done.45.refs_1_, bf16[2,4,128,256]{3,2,1,0:T(8,128)(2,1)} %collective-permute-done.46.refs_2_, ...), custom_call_target="tpu_custom_call" | custom-call | flops 2818572288 | bytes 5505024 | tf_op jit(solution)/shard_map/pallas_call | solution.py:536
  375.6 9.3 %shard_map.100 = bf16[16,336,128]{2,1,0:T(8,128)(2,1)} custom-call(s32[3]{0:T(128)} %pad_add_fusion.meta, bf16[2,4,128,256]{3,2,1,0:T(8,128)(2,1)} %shard_map.96.refs_0_, bf16[2,4,128,256]{3,2,1,0:T(8,128)(2,1)} %collective-permute-done.32.refs_1_, bf16[2,4,128,256]{3,2,1,0:T(8,128)(2,1)} %collective-permute-done.33.refs_2_, ...), custom_call_target="tpu_custom_call" | custom-call | flops 2818572288 | bytes 5505024 | tf_op jit(solution)/shard_map/pallas_call | solution.py:536
  384.8 24.7 %all_to_all.5.arrived = bf16[16,336,128]{2,1,0:T(8,128)(2,1)} all-to-all(bf16[16,336,128]{2,1,0:T(8,128)(2,1)} %shard_map.100), channel_id=1, replica_groups=mesh['groups'=1,'half'=2,'place'=8,'cols'=2,'sub'=1] {'place','cols'}, dimensions={0} | all-to-all | bytes 2752512 | tf_op jit(solution)/shard_map/all_to_all | solution.py:552
  409.5 3.3 shard_map.101
  (138 shorter events, 36.9 us)
Async XLA Ops:
  6.5 146.3 %all-gather.7.cloned.1.call-start = ((), (), s32[]{:S(2)}) async-start(), calls=%async_computation.1 | async-start | bytes 4128768 | tf_op jit(solution)/shard_map/all_gather | solution.py:405
  15.7 251.2 %all-gather.9.cloned.1.call-start = ((), (), s32[]{:S(2)}) async-start(), calls=%async_computation.2 | async-start | bytes 4128768 | tf_op jit(solution)/shard_map/all_gather | solution.py:451
  18.5 73.5 %collective-permute-start.8 = (bf16[256,2688]{1,0:T(8,128)(2,1)}, bf16[256,2688]{1,0:T(8,128)(2,1)}, u32[]{:S(2)}, u32[]{:S(2)}) collective-permute-start(bf16[256,2688]{1,0:T(8,128)(2,1)} %fusion.2.refs_0_), channel_id=1, source_target_pairs={{0,8},{1,9},{2,10},{3,11},{4,12},{5,13},{6,14},{7,15},{8,0},{9,1},... | collective-permute-start | bytes 4128776 | tf_op jit(solution)/shard_map/ppermute | solution.py:151
  21.9 62.2 %collective-permute-start.19 = (bf16[336,256]{1,0:T(8,128)(2,1)S(1)}, bf16[336,256]{1,0:T(8,128)(2,1)}, u32[]{:S(2)}, u32[]{:S(2)}) collective-permute-start(bf16[336,256]{1,0:T(8,128)(2,1)S(1)} %copy-done.15), channel_id=1, source_target_pairs={{0,8},{1,9},{2,10},{3,11},{4,12},{5,13},{6,14},{7,15},{8,0},{9,1},... | collective-permute-start | bytes 516104 | tf_op jit(solution)/shard_map/ppermute | solution.py:151
  22.4 65.3 %collective-permute-start.20 = (bf16[336,256]{1,0:T(8,128)(2,1)S(1)}, bf16[336,256]{1,0:T(8,128)(2,1)}, u32[]{:S(2)}, u32[]{:S(2)}) collective-permute-start(bf16[336,256]{1,0:T(8,128)(2,1)S(1)} %copy-done.14), channel_id=1, source_target_pairs={{0,10},{1,11},{2,8},{3,9},{4,14},{5,15},{6,12},{7,13},{8,2},{9,3},... | collective-permute-start | bytes 516104 | tf_op jit(solution)/shard_map/ppermute | solution.py:151
  27.5 64.4 %collective-permute-start.21 = (bf16[336,256]{1,0:T(8,128)(2,1)S(1)}, bf16[336,256]{1,0:T(8,128)(2,1)}, u32[]{:S(2)}, u32[]{:S(2)}) collective-permute-start(bf16[336,256]{1,0:T(8,128)(2,1)S(1)} %copy-done.13), channel_id=1, source_target_pairs={{0,12},{1,13},{2,14},{3,15},{4,8},{5,9},{6,10},{7,11},{8,4},{9,5},... | collective-permute-start | bytes 516104 | tf_op jit(solution)/shard_map/ppermute | solution.py:151
  30.1 72.0 %collective-permute-start.4 = (bf16[256,2688]{1,0:T(8,128)(2,1)}, bf16[256,2688]{1,0:T(8,128)(2,1)}, u32[]{:S(2)}, u32[]{:S(2)}) collective-permute-start(bf16[256,2688]{1,0:T(8,128)(2,1)} %fusion.2.refs_0_), channel_id=1, source_target_pairs={{0,4},{1,5},{2,6},{3,7},{4,0},{5,1},{6,2},{7,3},{8,12},{9,13},{10,... | collective-permute-start | bytes 4128776 | tf_op jit(solution)/shard_map/ppermute | solution.py:151
  84.1 33.4 %collective-permute-start.1 = (bf16[256,2688]{1,0:T(8,128)(2,1)}, bf16[256,2688]{1,0:T(8,128)(2,1)}, u32[]{:S(2)}, u32[]{:S(2)}) collective-permute-start(bf16[256,2688]{1,0:T(8,128)(2,1)} %fusion.2.refs_0_), channel_id=1, source_target_pairs={{0,1},{1,0},{2,3},{3,2},{4,5},{5,4},{6,7},{7,6},{8,9},{9,8},{10,11... | collective-permute-start | bytes 4128776 | tf_op jit(solution)/shard_map/ppermute | solution.py:151
  87.7 29.8 %collective-permute-start.2 = (bf16[256,2688]{1,0:T(8,128)(2,1)}, bf16[256,2688]{1,0:T(8,128)(2,1)}, u32[]{:S(2)}, u32[]{:S(2)}) collective-permute-start(bf16[256,2688]{1,0:T(8,128)(2,1)} %fusion.2.refs_0_), channel_id=1, source_target_pairs={{0,2},{1,3},{2,0},{3,1},{4,6},{5,7},{6,4},{7,5},{8,10},{9,11},{10,... | collective-permute-start | bytes 4128776 | tf_op jit(solution)/shard_map/ppermute | solution.py:151
  91.9 36.3 %collective-permute-start.12 = (bf16[256,2688]{1,0:T(8,128)(2,1)}, bf16[256,2688]{1,0:T(8,128)(2,1)}, u32[]{:S(2)}, u32[]{:S(2)}) collective-permute-start(bf16[256,2688]{1,0:T(8,128)(2,1)} %collective-permute-done.8.refs_8_), channel_id=1, source_target_pairs={{0,4},{1,5},{2,6},{3,7},{4,0},{5,1},{6,2},{7,3},{8,12},{9,13},{10,... | collective-permute-start | bytes 4128776 | tf_op jit(solution)/shard_map/ppermute | solution.py:151
  98.9 48.1 %collective-permute-start.9 = (bf16[256,2688]{1,0:T(8,128)(2,1)}, bf16[256,2688]{1,0:T(8,128)(2,1)}, u32[]{:S(2)}, u32[]{:S(2)}) collective-permute-start(bf16[256,2688]{1,0:T(8,128)(2,1)} %collective-permute-done.8.refs_8_), channel_id=1, source_target_pairs={{0,1},{1,0},{2,3},{3,2},{4,5},{5,4},{6,7},{7,6},{8,9},{9,8},{10,11... | collective-permute-start | bytes 4128776 | tf_op jit(solution)/shard_map/ppermute | solution.py:151
  102.1 187.0 %all-gather.11.cloned.1.call-start = ((), (), s32[]{:S(2)}) async-start(), calls=%async_computation.3 | async-start | bytes 1572864 | tf_op jit(solution)/shard_map/all_gather | solution.py:494
  102.1 74.2 %collective-permute-start.5 = (bf16[256,2688]{1,0:T(8,128)(2,1)}, bf16[256,2688]{1,0:T(8,128)(2,1)S(1)}, u32[]{:S(2)}, u32[]{:S(2)}) collective-permute-start(bf16[256,2688]{1,0:T(8,128)(2,1)} %collective-permute-done.4.refs_4_), channel_id=1, source_target_pairs={{0,1},{1,0},{2,3},{3,2},{4,5},{5,4},{6,7},{7,6},{8,9},{9,8},{10,11... | collective-permute-start | bytes 4128776 | tf_op jit(solution)/shard_map/ppermute | solution.py:151
  117.5 58.9 %collective-permute-start.10 = (bf16[256,2688]{1,0:T(8,128)(2,1)}, bf16[256,2688]{1,0:T(8,128)(2,1)S(1)}, u32[]{:S(2)}, u32[]{:S(2)}) collective-permute-start(bf16[256,2688]{1,0:T(8,128)(2,1)} %collective-permute-done.8.refs_8_), channel_id=1, source_target_pairs={{0,2},{1,3},{2,0},{3,1},{4,6},{5,7},{6,4},{7,5},{8,10},{9,11},{10,... | collective-permute-start | bytes 4128776 | tf_op jit(solution)/shard_map/ppermute | solution.py:151
  117.5 60.5 %collective-permute-start.6 = (bf16[256,2688]{1,0:T(8,128)(2,1)}, bf16[256,2688]{1,0:T(8,128)(2,1)}, u32[]{:S(2)}, u32[]{:S(2)}) collective-permute-start(bf16[256,2688]{1,0:T(8,128)(2,1)} %collective-permute-done.4.refs_4_), channel_id=1, source_target_pairs={{0,2},{1,3},{2,0},{3,1},{4,6},{5,7},{6,4},{7,5},{8,10},{9,11},{10,... | collective-permute-start | bytes 4128776 | tf_op jit(solution)/shard_map/ppermute | solution.py:151
  128.2 50.0 %collective-permute-start.3 = (bf16[256,2688]{1,0:T(8,128)(2,1)}, bf16[256,2688]{1,0:T(8,128)(2,1)}, u32[]{:S(2)}, u32[]{:S(2)}) collective-permute-start(bf16[256,2688]{1,0:T(8,128)(2,1)} %collective-permute-done.1.refs_1_), channel_id=1, source_target_pairs={{0,2},{1,3},{2,0},{3,1},{4,6},{5,7},{6,4},{7,5},{8,10},{9,11},{10,... | collective-permute-start | bytes 4128776 | tf_op jit(solution)/shard_map/ppermute | solution.py:151
  146.9 52.7 %collective-permute-start.13 = (bf16[256,2688]{1,0:T(8,128)(2,1)}, bf16[256,2688]{1,0:T(8,128)(2,1)}, u32[]{:S(2)}, u32[]{:S(2)}) collective-permute-start(bf16[256,2688]{1,0:T(8,128)(2,1)} %collective-permute-done.12.refs_12_), channel_id=1, source_target_pairs={{0,1},{1,0},{2,3},{3,2},{4,5},{5,4},{6,7},{7,6},{8,9},{9,8},{10,11... | collective-permute-start | bytes 4128776 | tf_op jit(solution)/shard_map/ppermute | solution.py:151
  176.4 11.0 %collective-permute-start.24 = (bf16[672,256]{1,0:T(8,128)(2,1)S(1)}, bf16[672,256]{1,0:T(8,128)(2,1)S(1)}, u32[]{:S(2)}, u32[]{:S(2)}) collective-permute-start(bf16[672,256]{1,0:T(8,128)(2,1)S(1)} %get-tuple-element.50), channel_id=1, source_target_pairs={{0,4},{1,5},{2,6},{3,7},{4,0},{5,1},{6,2},{7,3},{8,12},{9,13},{10,... | collective-permute-start | bytes 1032200 | tf_op jit(solution)/shard_map/ppermute | solution.py:151
  178.0 15.7 %collective-permute-start.25 = (bf16[672,256]{1,0:T(8,128)(2,1)S(1)}, bf16[672,256]{1,0:T(8,128)(2,1)S(1)}, u32[]{:S(2)}, u32[]{:S(2)}) collective-permute-start(bf16[672,256]{1,0:T(8,128)(2,1)S(1)} %get-tuple-element.49), channel_id=1, source_target_pairs={{0,6},{1,7},{2,4},{3,5},{4,2},{5,3},{6,0},{7,1},{8,14},{9,15},{10,... | collective-permute-start | bytes 1032200 | tf_op jit(solution)/shard_map/ppermute | solution.py:151
  178.2 23.8 %collective-permute-start.26 = (bf16[672,256]{1,0:T(8,128)(2,1)}, bf16[672,256]{1,0:T(8,128)(2,1)}, u32[]{:S(2)}, u32[]{:S(2)}) collective-permute-start(bf16[672,256]{1,0:T(8,128)(2,1)} %get-tuple-element.48), channel_id=1, source_target_pairs={{0,8},{1,9},{2,10},{3,11},{4,12},{5,13},{6,14},{7,15},{8,0},{9,1},... | collective-permute-start | bytes 1032200 | tf_op jit(solution)/shard_map/ppermute | solution.py:151
  180.7 65.3 %collective-permute-start.14 = (bf16[256,2688]{1,0:T(8,128)(2,1)}, bf16[256,2688]{1,0:T(8,128)(2,1)}, u32[]{:S(2)}, u32[]{:S(2)}) collective-permute-start(bf16[256,2688]{1,0:T(8,128)(2,1)} %collective-permute-done.12.refs_12_), channel_id=1, source_target_pairs={{0,2},{1,3},{2,0},{3,1},{4,6},{5,7},{6,4},{7,5},{8,10},{9,11},{10,... | collective-permute-start | bytes 4128776 | tf_op jit(solution)/shard_map/ppermute | solution.py:151
  187.4 61.5 %collective-permute-start.11 = (bf16[256,2688]{1,0:T(8,128)(2,1)}, bf16[256,2688]{1,0:T(8,128)(2,1)}, u32[]{:S(2)}, u32[]{:S(2)}) collective-permute-start(bf16[256,2688]{1,0:T(8,128)(2,1)} %collective-permute-done.9.refs_9_), channel_id=1, source_target_pairs={{0,2},{1,3},{2,0},{3,1},{4,6},{5,7},{6,4},{7,5},{8,10},{9,11},{10,... | collective-permute-start | bytes 4128776 | tf_op jit(solution)/shard_map/ppermute | solution.py:151
  193.7 55.2 %collective-permute-start.7 = (bf16[256,2688]{1,0:T(8,128)(2,1)S(1)}, bf16[256,2688]{1,0:T(8,128)(2,1)}, u32[]{:S(2)}, u32[]{:S(2)}) collective-permute-start(bf16[256,2688]{1,0:T(8,128)(2,1)S(1)} %collective-permute-done.5.refs_5_), channel_id=1, source_target_pairs={{0,2},{1,3},{2,0},{3,1},{4,6},{5,7},{6,4},{7,5},{8,10},{9,11},{10,... | collective-permute-start | bytes 4128776 | tf_op jit(solution)/shard_map/ppermute | solution.py:151
  199.6 49.2 %collective-permute-start.15 = (bf16[256,2688]{1,0:T(8,128)(2,1)}, bf16[256,2688]{1,0:T(8,128)(2,1)}, u32[]{:S(2)}, u32[]{:S(2)}) collective-permute-start(bf16[256,2688]{1,0:T(8,128)(2,1)} %collective-permute-done.13.refs_13_), channel_id=1, source_target_pairs={{0,2},{1,3},{2,0},{3,1},{4,6},{5,7},{6,4},{7,5},{8,10},{9,11},{10,... | collective-permute-start | bytes 4128776 | tf_op jit(solution)/shard_map/ppermute | solution.py:151
  202.0 104.5 %all-gather.13.cloned.1.call-start = ((), (), s32[]{:S(2)}) async-start(), calls=%async_computation.4 | async-start | bytes 1572864 | tf_op jit(solution)/shard_map/all_gather | solution.py:494
  202.0 13.0 %collective-permute-start.27 = (bf16[672,256]{1,0:T(8,128)(2,1)}, bf16[672,256]{1,0:T(8,128)(2,1)S(1)}, u32[]{:S(2)}, u32[]{:S(2)}) collective-permute-start(bf16[672,256]{1,0:T(8,128)(2,1)} %get-tuple-element.47), channel_id=1, source_target_pairs={{0,10},{1,11},{2,8},{3,9},{4,14},{5,15},{6,12},{7,13},{8,2},{9,3},... | collective-permute-start | bytes 1032200 | tf_op jit(solution)/shard_map/ppermute | solution.py:151
  215.0 16.9 %collective-permute-start.28 = (bf16[672,256]{1,0:T(8,128)(2,1)S(1)}, bf16[672,256]{1,0:T(8,128)(2,1)S(1)}, u32[]{:S(2)}, u32[]{:S(2)}) collective-permute-start(bf16[672,256]{1,0:T(8,128)(2,1)S(1)} %get-tuple-element.46), channel_id=1, source_target_pairs={{0,12},{1,13},{2,14},{3,15},{4,8},{5,9},{6,10},{7,11},{8,4},{9,5},... | collective-permute-start | bytes 1032200 | tf_op jit(solution)/shard_map/ppermute | solution.py:151
  232.6 12.6 %collective-permute-start.29 = (bf16[672,256]{1,0:T(8,128)(2,1)S(1)}, bf16[672,256]{1,0:T(8,128)(2,1)S(1)}, u32[]{:S(2)}, u32[]{:S(2)}) collective-permute-start(bf16[672,256]{1,0:T(8,128)(2,1)S(1)} %get-tuple-element.45), channel_id=1, source_target_pairs={{0,14},{1,15},{2,12},{3,13},{4,10},{5,11},{6,8},{7,9},{8,6},{9,7},... | collective-permute-start | bytes 1032200 | tf_op jit(solution)/shard_map/ppermute | solution.py:151
  245.1 77.9 %collective-permute-start.39 = (bf16[336,2048]{1,0:T(8,128)(2,1)}, bf16[336,2048]{1,0:T(8,128)(2,1)}, u32[]{:S(2)}, u32[]{:S(2)}) collective-permute-start(bf16[336,2048]{1,0:T(8,128)(2,1)} %bitcast.8.refs_8_), channel_id=1, source_target_pairs={{0,1},{1,0},{2,3},{3,2},{4,5},{5,4},{6,7},{7,6},{8,9},{9,8},{10,11... | collective-permute-start | bytes 4128776 | tf_op jit(solution)/shard_map/ppermute | solution.py:151
  246.1 45.5 %collective-permute-start.40 = (bf16[80,2048]{1,0:T(8,128)(2,1)}, bf16[80,2048]{1,0:T(8,128)(2,1)}, u32[]{:S(2)}, u32[]{:S(2)}) collective-permute-start(bf16[80,2048]{1,0:T(8,128)(2,1)} %slice.24), channel_id=1, source_target_pairs={{0,16},{16,0},{1,17},{17,1},{2,18},{18,2},{3,19},{19,3},{4,20},{20... | collective-permute-start | bytes 983048 | tf_op jit(solution)/shard_map/ppermute | solution.py:492
  263.5 35.5 %collective-permute-start.30 = (bf16[4,256,256]{2,1,0:T(8,128)(2,1)}, bf16[4,256,256]{2,1,0:T(8,128)(2,1)}, u32[]{:S(2)}, u32[]{:S(2)}) collective-permute-start(bf16[4,256,256]{2,1,0:T(8,128)(2,1)} %get-tuple-element.39), channel_id=1, source_target_pairs={{0,16},{1,17},{2,18},{3,19},{4,20},{5,21},{6,22},{7,23},{8,24},{9,... | collective-permute-start | bytes 1572872 | tf_op jit(solution)/shard_map/ppermute | solution.py:481
  290.9 32.2 %collective-permute-start.42 = (bf16[128,2048]{1,0:T(8,128)(2,1)}, bf16[128,2048]{1,0:T(8,128)(2,1)}, u32[]{:S(2)}, u32[]{:S(2)}) collective-permute-start(bf16[128,2048]{1,0:T(8,128)(2,1)} %dynamic-slice_bitcast_fusion.1.refs_12_), channel_id=1, source_target_pairs={{0,1},{1,0},{2,3},{3,2},{4,5},{5,4},{6,7},{7,6},{8,9},{9,8},{10,11... | collective-permute-start | bytes 1572872 | tf_op jit(solution)/shard_map/ppermute | solution.py:151
  291.5 30.3 %collective-permute-start.41 = (bf16[80,2048]{1,0:T(8,128)(2,1)}, bf16[80,2048]{1,0:T(8,128)(2,1)}, u32[]{:S(2)}, u32[]{:S(2)}) collective-permute-start(bf16[80,2048]{1,0:T(8,128)(2,1)} %collective-permute-done.40.refs_10_), channel_id=1, source_target_pairs={{0,1},{1,0},{2,3},{3,2},{4,5},{5,4},{6,7},{7,6},{8,9},{9,8},{10,11... | collective-permute-start | bytes 983048 | tf_op jit(solution)/shard_map/ppermute | solution.py:151
  299.0 28.0 %collective-permute-start.48 = (bf16[2,4,128,256]{3,2,1,0:T(8,128)(2,1)}, bf16[2,4,128,256]{3,2,1,0:T(8,128)(2,1)}, u32[]{:S(2)}, u32[]{:S(2)}) collective-permute-start(bf16[2,4,128,256]{3,2,1,0:T(8,128)(2,1)} %shard_map.98.refs_0_), channel_id=1, source_target_pairs={{0,8},{1,9},{2,10},{3,11},{4,12},{5,13},{6,14},{7,15},{8,0},{9,1},... | collective-permute-start | bytes 1572872 | tf_op jit(solution)/shard_map/ppermute | solution.py:151
  305.1 14.9 %collective-permute-start.31 = (bf16[4,128,256]{2,1,0:T(8,128)(2,1)}, bf16[4,128,256]{2,1,0:T(8,128)(2,1)}, u32[]{:S(2)}, u32[]{:S(2)}) collective-permute-start(bf16[4,128,256]{2,1,0:T(8,128)(2,1)} %get-tuple-element.41), channel_id=1, source_target_pairs={{0,1},{1,0},{2,3},{3,2},{4,5},{5,4},{6,7},{7,6},{8,9},{9,8},{10,11... | collective-permute-start | bytes 786440 | tf_op jit(solution)/shard_map/ppermute | solution.py:151
  320.0 15.1 %collective-permute-start.46 = (bf16[2,4,128,256]{3,2,1,0:T(8,128)(2,1)}, bf16[2,4,128,256]{3,2,1,0:T(8,128)(2,1)}, u32[]{:S(2)}, u32[]{:S(2)}) collective-permute-start(bf16[2,4,128,256]{3,2,1,0:T(8,128)(2,1)} %shard_map.98.refs_0_), channel_id=1, source_target_pairs={{0,4},{1,5},{2,6},{3,7},{4,0},{5,1},{6,2},{7,3},{8,12},{9,13},{10,... | collective-permute-start | bytes 1572872 | tf_op jit(solution)/shard_map/ppermute | solution.py:151
  321.9 13.3 %collective-permute-start.43 = (bf16[128,2048]{1,0:T(8,128)(2,1)}, bf16[128,2048]{1,0:T(8,128)(2,1)}, u32[]{:S(2)}, u32[]{:S(2)}) collective-permute-start(bf16[128,2048]{1,0:T(8,128)(2,1)} %dynamic-slice_bitcast_fusion.refs_14_), channel_id=1, source_target_pairs={{0,1},{1,0},{2,3},{3,2},{4,5},{5,4},{6,7},{7,6},{8,9},{9,8},{10,11... | collective-permute-start | bytes 1572872 | tf_op jit(solution)/shard_map/ppermute | solution.py:151
  323.0 12.6 %collective-permute-start.45 = (bf16[2,4,128,256]{3,2,1,0:T(8,128)(2,1)}, bf16[2,4,128,256]{3,2,1,0:T(8,128)(2,1)}, u32[]{:S(2)}, u32[]{:S(2)}) collective-permute-start(bf16[2,4,128,256]{3,2,1,0:T(8,128)(2,1)} %shard_map.98.refs_0_), channel_id=1, source_target_pairs={{0,2},{1,3},{2,0},{3,1},{4,6},{5,7},{6,4},{7,5},{8,10},{9,11},{10,... | collective-permute-start | bytes 1572872 | tf_op jit(solution)/shard_map/ppermute | solution.py:151
  323.1 16.8 %collective-permute-start.35 = (bf16[2,4,128,256]{3,2,1,0:T(8,128)(2,1)}, bf16[2,4,128,256]{3,2,1,0:T(8,128)(2,1)}, u32[]{:S(2)}, u32[]{:S(2)}) collective-permute-start(bf16[2,4,128,256]{3,2,1,0:T(8,128)(2,1)} %shard_map.96.refs_0_), channel_id=1, source_target_pairs={{0,8},{1,9},{2,10},{3,11},{4,12},{5,13},{6,14},{7,15},{8,0},{9,1},... | collective-permute-start | bytes 1572872 | tf_op jit(solution)/shard_map/ppermute | solution.py:151
  327.0 19.2 %collective-permute-start.50 = (bf16[2,4,128,256]{3,2,1,0:T(8,128)(2,1)}, bf16[2,4,128,256]{3,2,1,0:T(8,128)(2,1)S(1)}, u32[]{:S(2)}, u32[]{:S(2)}) collective-permute-start(bf16[2,4,128,256]{3,2,1,0:T(8,128)(2,1)} %collective-permute-done.48.refs_4_), channel_id=1, source_target_pairs={{0,4},{1,5},{2,6},{3,7},{4,0},{5,1},{6,2},{7,3},{8,12},{9,13},{10,... | collective-permute-start | bytes 1572872 | tf_op jit(solution)/shard_map/ppermute | solution.py:151
  335.1 11.9 %collective-permute-start.47 = (bf16[2,4,128,256]{3,2,1,0:T(8,128)(2,1)}, bf16[2,4,128,256]{3,2,1,0:T(8,128)(2,1)}, u32[]{:S(2)}, u32[]{:S(2)}) collective-permute-start(bf16[2,4,128,256]{3,2,1,0:T(8,128)(2,1)} %collective-permute-done.46.refs_2_), channel_id=1, source_target_pairs={{0,2},{1,3},{2,0},{3,1},{4,6},{5,7},{6,4},{7,5},{8,10},{9,11},{10,... | collective-permute-start | bytes 1572872 | tf_op jit(solution)/shard_map/ppermute | solution.py:151
  335.1 12.4 %collective-permute-start.49 = (bf16[2,4,128,256]{3,2,1,0:T(8,128)(2,1)}, bf16[2,4,128,256]{3,2,1,0:T(8,128)(2,1)}, u32[]{:S(2)}, u32[]{:S(2)}) collective-permute-start(bf16[2,4,128,256]{3,2,1,0:T(8,128)(2,1)} %collective-permute-done.48.refs_4_), channel_id=1, source_target_pairs={{0,2},{1,3},{2,0},{3,1},{4,6},{5,7},{6,4},{7,5},{8,10},{9,11},{10,... | collective-permute-start | bytes 1572872 | tf_op jit(solution)/shard_map/ppermute | solution.py:151
  335.6 22.0 %collective-permute-start.33 = (bf16[2,4,128,256]{3,2,1,0:T(8,128)(2,1)}, bf16[2,4,128,256]{3,2,1,0:T(8,128)(2,1)}, u32[]{:S(2)}, u32[]{:S(2)}) collective-permute-start(bf16[2,4,128,256]{3,2,1,0:T(8,128)(2,1)} %shard_map.96.refs_0_), channel_id=1, source_target_pairs={{0,4},{1,5},{2,6},{3,7},{4,0},{5,1},{6,2},{7,3},{8,12},{9,13},{10,... | collective-permute-start | bytes 1572872 | tf_op jit(solution)/shard_map/ppermute | solution.py:151
  339.8 27.1 %collective-permute-start.37 = (bf16[2,4,128,256]{3,2,1,0:T(8,128)(2,1)}, bf16[2,4,128,256]{3,2,1,0:T(8,128)(2,1)}, u32[]{:S(2)}, u32[]{:S(2)}) collective-permute-start(bf16[2,4,128,256]{3,2,1,0:T(8,128)(2,1)} %collective-permute-done.35.refs_4_), channel_id=1, source_target_pairs={{0,4},{1,5},{2,6},{3,7},{4,0},{5,1},{6,2},{7,3},{8,12},{9,13},{10,... | collective-permute-start | bytes 1572872 | tf_op jit(solution)/shard_map/ppermute | solution.py:151
  347.0 19.9 %collective-permute-start.51 = (bf16[2,4,128,256]{3,2,1,0:T(8,128)(2,1)S(1)}, bf16[2,4,128,256]{3,2,1,0:T(8,128)(2,1)}, u32[]{:S(2)}, u32[]{:S(2)}) collective-permute-start(bf16[2,4,128,256]{3,2,1,0:T(8,128)(2,1)S(1)} %collective-permute-done.50.refs_6_), channel_id=1, source_target_pairs={{0,2},{1,3},{2,0},{3,1},{4,6},{5,7},{6,4},{7,5},{8,10},{9,11},{10,... | collective-permute-start | bytes 1572872 | tf_op jit(solution)/shard_map/ppermute | solution.py:151
  347.0 28.5 %collective-permute-start.32 = (bf16[2,4,128,256]{3,2,1,0:T(8,128)(2,1)}, bf16[2,4,128,256]{3,2,1,0:T(8,128)(2,1)}, u32[]{:S(2)}, u32[]{:S(2)}) collective-permute-start(bf16[2,4,128,256]{3,2,1,0:T(8,128)(2,1)} %shard_map.96.refs_0_), channel_id=1, source_target_pairs={{0,2},{1,3},{2,0},{3,1},{4,6},{5,7},{6,4},{7,5},{8,10},{9,11},{10,... | collective-permute-start | bytes 1572872 | tf_op jit(solution)/shard_map/ppermute | solution.py:151
  347.5 28.0 %collective-permute-start.36 = (bf16[2,4,128,256]{3,2,1,0:T(8,128)(2,1)}, bf16[2,4,128,256]{3,2,1,0:T(8,128)(2,1)}, u32[]{:S(2)}, u32[]{:S(2)}) collective-permute-start(bf16[2,4,128,256]{3,2,1,0:T(8,128)(2,1)} %collective-permute-done.35.refs_4_), channel_id=1, source_target_pairs={{0,2},{1,3},{2,0},{3,1},{4,6},{5,7},{6,4},{7,5},{8,10},{9,11},{10,... | collective-permute-start | bytes 1572872 | tf_op jit(solution)/shard_map/ppermute | solution.py:151
  357.6 18.0 %collective-permute-start.34 = (bf16[2,4,128,256]{3,2,1,0:T(8,128)(2,1)}, bf16[2,4,128,256]{3,2,1,0:T(8,128)(2,1)}, u32[]{:S(2)}, u32[]{:S(2)}) collective-permute-start(bf16[2,4,128,256]{3,2,1,0:T(8,128)(2,1)} %collective-permute-done.33.refs_2_), channel_id=1, source_target_pairs={{0,2},{1,3},{2,0},{3,1},{4,6},{5,7},{6,4},{7,5},{8,10},{9,11},{10,... | collective-permute-start | bytes 1572872 | tf_op jit(solution)/shard_map/ppermute | solution.py:151
  (27 other events, 353.6 us)
Sparse Core Ops, SparseCore 0:
  15.8 70.2 all-gather.6
  102.2 71.0 all-gather.8
  202.1 34.9 all-gather.10
  238.5 47.4 all-gather.12
